TPU v7x, 32 devices: a whole 2x2x4 slice. The times are simulated.
32 devices in a mesh: group: 2 (over y), wide: 4 (over z), narrow: 2 (over x), deep: 2 (over core).
Axes of the slice: x: 2, y: 2, z: 4, core: 2. Of those that a mesh axis runs over, the one named last changes fastest.
Arguments:
- queries: bfloat16 [384, 4096], P(('group', 'wide', 'deep'), 'narrow'), parts along dimension 0, may hold values from -110 to 110
- cache_keys: bfloat16 [384, 4, 32, 128], P(('group', 'wide', 'deep'), 'narrow'), parts along dimension 0, may hold values from -4.1 to 4.1
- cache_values: bfloat16 [384, 4, 32, 128], P(('group', 'wide', 'deep'), 'narrow'), parts along dimension 0, may hold values from -6 to 6
- fresh_pairs: bfloat16 [384, 2, 512], P(('group', 'wide', 'deep'), None, 'narrow'), parts along dimension 0, may hold values from -6 to 6
- lengths: int32 [384], P(('group', 'wide', 'deep')), parts along dimension 0, may hold values from 2 to 32, as said below
- residual: bfloat16 [384, 2048], P(('group', 'wide', 'deep')), parts along dimension 0, may hold values from -6 to 6
- norm_gain: float32 [2048], replicated, may hold values from 0.1 to 1.9
- output_weight: bfloat16 [4096, 2048], P('narrow', 'deep'), may hold values from -0.09375 to 0.09375
- expert_gate_up: bfloat16 [8, 2, 768, 2048], P(('wide', 'deep'), None, 'narrow'), may hold values from -0.125 to 0.125
- expert_down: bfloat16 [8, 768, 2048], P(('wide', 'deep'), None, 'narrow'), may hold values from -0.21875 to 0.21875
- routed_experts: int32 [384, 1], P(('group', 'wide', 'deep')), parts along dimension 0, may hold values from 0 to 7, as said below
- router_weights: float32 [384, 1], P(('group', 'wide', 'deep')), parts along dimension 0, may hold values from 0.1 to 1
Outputs:
- layer_out: bfloat16 [384, 2048], P(('group', 'wide', 'deep'), 'narrow'), parts along dimension 0
There are 2 independent parts, one for each index of `group`. A program takes and returns all parts, laid end to end along the dimension named above; an argument that names none is the same for every part. Nothing has to cross between parts.
Inputs may be any that keep to these rules, and one draw needn't show every extreme that they name: `routed_experts`: each row names 1 different experts. Among the rows of one device no expert is named more than 6 times, and one and the same expert is named exactly 6 times by the rows of every device. `lengths`: each device's block of 24 requests holds one of length 32.
All inputs are finite; a program needn't handle non-finite values.
Results may differ from a plain program's by a relative error of at most 0.0095.
Values may be sent and summed in bfloat16 or wider, within the bound.
No kernel may reach another device: no remote copies, remote signals or barrier semaphores. Data moves between devices by JAX's collectives and lax.ppermute only.
A program may use at most 64 MiB of HBM per device.

v0:
```python
import math

import jax
import jax.numpy as jnp
from jax import lax
from jax.sharding import PartitionSpec as P


def shards(
    queries,
    cache_keys,
    cache_values,
    fresh_pairs,
    lengths,
    residual,
    norm_gain,
    output_weight,
    expert_gate_up,
    expert_down,
    routed_experts,
    router_weights,
):
    row_count = queries.shape[0]
    local_heads = cache_keys.shape[1]
    length = cache_keys.shape[2]
    head_size = cache_keys.shape[3]
    group_size = queries.shape[1] // (local_heads * head_size)
    score_scale = 1.0 / math.sqrt(head_size)
    query_heads = queries.reshape(row_count, local_heads, group_size, head_size)
    fresh_heads = fresh_pairs.reshape(row_count, 2, local_heads, head_size)
    scores = (
        jnp.einsum("rkgd,rkld->rkgl", query_heads, cache_keys, preferred_element_type=jnp.float32)
        * score_scale
    )
    in_cache = jnp.arange(length, dtype=jnp.int32)[None, :] < lengths[:, None]
    scores = jnp.where(in_cache[:, None, None, :], scores, -1e30)
    own_score = (
        jnp.einsum(
            "rkgd,rkd->rkg", query_heads, fresh_heads[:, 0], preferred_element_type=jnp.float32
        )
        * score_scale
    )
    row_max = jnp.maximum(jnp.max(scores, -1), own_score)
    weights_raw = jnp.exp(scores - row_max[..., None])
    own_raw = jnp.exp(own_score - row_max)
    denominator = jnp.sum(weights_raw, -1) + own_raw
    attention_weights = (weights_raw / denominator[..., None]).astype(jnp.bfloat16)
    own_weight = (own_raw / denominator).astype(jnp.bfloat16)
    attended = jnp.einsum(
        "rkgl,rkld->rkgd", attention_weights, cache_values, preferred_element_type=jnp.float32
    )
    attended = (
        attended
        + own_weight.astype(jnp.float32)[..., None]
        * fresh_heads[:, 1].astype(jnp.float32)[:, :, None, :]
    )
    attended = attended.astype(jnp.bfloat16).reshape(row_count, -1)
    paired = jnp.dot(
        lax.all_gather(attended, "deep", axis=0, tiled=True),
        output_weight,
        preferred_element_type=jnp.float32,
    )
    partial_value = lax.all_to_all(
        paired.astype(jnp.bfloat16), "deep", split_axis=0, concat_axis=1, tiled=True
    ).astype(paired.dtype)
    full_width = residual.shape[1]
    narrow_count = lax.axis_size("narrow")
    narrow_index = lax.axis_index("narrow")
    share_width = full_width // narrow_count
    experts = lax.axis_size(("wide", "deep"))
    picks_per_row = routed_experts.shape[1]
    capacity = row_count // 4
    pick_count = row_count * picks_per_row
    weights = router_weights / jnp.sum(router_weights, -1, keepdims=True)
    flat_experts = routed_experts.reshape(-1)
    expert_hits = (flat_experts[:, None] == jnp.arange(experts, dtype=jnp.int32)[None, :]).astype(
        jnp.int32
    )
    slot_index = jnp.sum((jnp.cumsum(expert_hits, 0) - expert_hits) * expert_hits, 1)
    target = flat_experts * capacity + slot_index
    placing = (jnp.arange(experts * capacity, dtype=jnp.int32)[:, None] == target[None, :]).astype(
        jnp.bfloat16
    )
    owner_map = (
        jnp.arange(pick_count, dtype=jnp.int32)[:, None] // picks_per_row
        == jnp.arange(row_count, dtype=jnp.int32)[None, :]
    ).astype(jnp.bfloat16)
    spread = jnp.dot(placing, owner_map, preferred_element_type=jnp.float32).astype(jnp.bfloat16)
    gate_up = expert_gate_up[0]
    down_local = expert_down[0]
    share = lax.psum_scatter(
        partial_value.astype(jnp.bfloat16), "narrow", scatter_dimension=1, tiled=True
    ).astype(jnp.float32)
    mixed_mine = (
        lax.dynamic_slice_in_dim(residual, narrow_index * share_width, share_width, 1).astype(
            jnp.float32
        )
        + share
    )
    squares = lax.psum(jnp.sum(mixed_mine * mixed_mine, -1, keepdims=True), "narrow")
    gain_mine = lax.dynamic_slice_in_dim(norm_gain, narrow_index * share_width, share_width, 0)
    normed = (mixed_mine * lax.rsqrt(squares / full_width + 1e-06) * gain_mine).astype(jnp.bfloat16)
    outgoing = (
        jnp.dot(spread, normed, preferred_element_type=jnp.float32)
        .astype(jnp.bfloat16)
        .reshape(experts, capacity, share_width)
    )
    incoming = lax.all_to_all(
        outgoing, ("wide", "deep"), split_axis=0, concat_axis=0, tiled=True
    ).reshape(experts * capacity, share_width)
    both_parts = jnp.einsum(
        "nd,gfd->gnf",
        lax.all_gather(incoming, "narrow", axis=1, tiled=True),
        gate_up,
        preferred_element_type=jnp.float32,
    )
    hidden_act = (jax.nn.silu(both_parts[0]) * both_parts[1]).astype(jnp.bfloat16)
    expert_share = jnp.dot(
        lax.all_gather(hidden_act, "narrow", axis=1, tiled=True),
        down_local,
        preferred_element_type=jnp.float32,
    ).astype(jnp.bfloat16)
    returned = lax.all_to_all(
        expert_share.reshape(experts, capacity, share_width),
        ("wide", "deep"),
        split_axis=0,
        concat_axis=0,
        tiled=True,
    )
    chosen = jnp.take(returned.reshape(experts * capacity, share_width), target, axis=0)
    chosen = chosen.reshape(row_count, picks_per_row, share_width).astype(jnp.float32)
    combined = jnp.sum(chosen * weights[:, :, None], 1)
    return (mixed_mine + combined).astype(jnp.bfloat16)


def solution(mesh):
    in_specs = (
        P(("group", "wide", "deep"), "narrow"),
        P(("group", "wide", "deep"), "narrow", None, None),
        P(("group", "wide", "deep"), "narrow", None, None),
        P(("group", "wide", "deep"), None, "narrow"),
        P(("group", "wide", "deep")),
        P(("group", "wide", "deep"), None),
        P(),
        P("narrow", "deep"),
        P(("wide", "deep"), None, "narrow", None),
        P(("wide", "deep"), None, "narrow"),
        P(("group", "wide", "deep"), None),
        P(("group", "wide", "deep"), None),
    )
    out_specs = P(("group", "wide", "deep"), "narrow")
    return jax.shard_map(shards, mesh=mesh, in_specs=in_specs, out_specs=out_specs, check_vma=False)
```

profile of v0, /device:TPU:0, one launch (start us, length us, event | category | flops | bytes accessed | tf_op | source)
XLA Modules:
  0.0 82.4 jit_solution(6561578115436360470)
XLA Ops:
  6.5 1.1 %copy.21 = bf16[3,8,16,128]{3,2,1,0:T(8,128)(2,1)S(1)} copy(bf16[3,8,16,128]{3,1,2,0:T(8,128)(2,1)} %bitcast.77) | data formatting | bytes 196608
  7.6 0.7 iota_compare_fusion.5
  8.3 0.8 reshape.108
  9.1 0.0 copy-start.1
  9.1 0.2 fusion.21
  9.3 1.6 %fusion.30 = (f32[24,2,8]{2,1,0:T(2,128)S(1)}, f32[24,2,8,32]{3,2,1,0:T(8,128)S(1)}) fusion(bf16[24,2,8,128]{3,2,1,0:T(8,128)(2,1)S(1)} %bitcast.75, bf16[24,2,32,128]{3,2,1,0:T(8,128)(2,1)} %param.13, pred[24,32]{1,0:T(8,128)(4,1)S(1)} %iota_compare_fusion.5), kind=kOutput, calls=%fused_computation.57 | convolution fusion | flops 3182208 | bytes 542976 | tf_op jit(solution)/shard_map/rkgd,rkld->rkgl/dot_general | solution.py:32
  10.9 0.2 fusion.13
  11.2 1.3 %fusion.5 = bf16[24,2,8,128]{3,2,1,0:T(8,128)(2,1)S(1)} fusion(bf16[24,2,32,128]{3,2,1,0:T(8,128)(2,1)} %param.14, f32[24,2,8,32]{3,2,1,0:T(8,128)S(1)} %get-tuple-element.12, f32[24,2,128]{2,1,0:T(2,128)S(1)} %get-tuple-element.10, f32[24,2,8]{2,1,0:T(2,128)S(1)} %get-tuple-element.8, f32[24,2,8]{2,1,0:T(2,128)S(1)} %get-tuple-element.7, ...), kind=kOutput, calls=%fused_computation.8 | convolution fusion | flops 3330048 | bytes 569856 | tf_op jit(solution)/shard_map/rkgl,rkld->rkgd/dot_general | solution.py:49
  12.5 0.0 copy-start.5
  12.6 2.1 %all_gather.9 = bf16[48,2048]{1,0:T(8,128)(2,1)S(1)} all-gather(bf16[24,2048]{1,0:T(8,128)(2,1)S(1)} %bitcast.73), channel_id=1, replica_groups=mesh['group'=2,'wide'=4,'narrow'=2,'deep'=2] {'deep'}, dimensions={0}, use_global_device_ids=true | all-gather | bytes 294912 | tf_op jit(solution)/shard_map/all_gather | solution.py:59
  14.7 0.8 %convolution_convert_fusion.1 = bf16[48,1024]{1,0:T(8,128)(2,1)S(1)} fusion(bf16[48,2048]{1,0:T(8,128)(2,1)S(1)} %all_gather.9, bf16[2048,1024]{1,0:T(8,128)(2,1)S(1)} %copy-done.1), kind=kOutput, calls=%fused_computation.12 | convolution fusion | flops 201375744 | bytes 4489216 | tf_op jit(solution)/shard_map/dot_general | solution.py:58
  15.5 3.8 %all_to_all.29 = bf16[2,24,1024]{2,1,0:T(8,128)(2,1)S(1)} all-to-all(bf16[2,24,1024]{2,1,0:T(8,128)(2,1)S(1)} %bitcast.76), channel_id=1, replica_groups=mesh['group'=2,'wide'=4,'narrow'=2,'deep'=2] {'deep'}, dimensions={0} | all-to-all | bytes 196608 | tf_op jit(solution)/shard_map/all_to_all | solution.py:63
  19.3 0.6 copy.20
  19.9 0.0 reduce-scatter.2.cloned.1.call-update
  20.0 0.1 fusion.26
  20.1 0.2 select_reduce_fusion
  20.3 12.5 %reduce-scatter.2.cloned.1.call-done = bf16[24,1024]{1,0:T(8,128)(2,1)} async-done(((bf16[24,2048]{1,0:T(8,128)(2,1)}), bf16[24,1024]{1,0:T(8,128)(2,1)}) %reduce-scatter.2.cloned.1.call-update) | async-done | bytes 49168 | tf_op jit(solution)/shard_map/reduce_scatter | solution.py:91
  32.8 0.9 %multiply_reduce_fusion = f32[24]{0:T(128)S(1)} fusion(bf16[24,1024]{1,0:T(8,128)(2,1)} %reduce-scatter.2.cloned.1.call-done, bf16[24,2048]{1,0:T(8,128)(2,1)S(1)} %copy-done.4, s32[]{:T(128)S(6)} %select_n.26), kind=kLoop, calls=%fused_computation.21 | loop fusion | flops 122856 | bytes 98404 | tf_op jit(solution)/shard_map/reduce_sum | solution.py:100
  33.8 4.9 %psum.7 = f32[24,1]{0,1:T(1,128)S(1)} all-reduce(f32[24,1]{0,1:T(1,128)S(1)} %bitcast.84), channel_id=1, replica_groups=mesh['group'=2,'wide'=4,'narrow'=2,'deep'=2] {'narrow'}, use_global_device_ids=true, to_apply=%region_6.7 | all-reduce | flops 24 | bytes 192 | tf_op jit(solution)/shard_map/psum | solution.py:100
  38.7 1.1 %convolution_convert_fusion = bf16[48,1024]{1,0:T(8,128)(2,1)S(1)} fusion(bf16[24,1024]{1,0:T(8,128)(2,1)} %reduce-scatter.2.cloned.1.call-done, f32[1024]{0:T(1024)S(1)} %dynamic_slice.7, f32[24]{0:T(128)S(1)} %rsqrt_bitcast_fusion, bf16[24,2048]{1,0:T(8,128)(2,1)S(1)} %copy-done.4, s32[]{:T(128)S(6)} %select_n.26, s32[24]{0:T(128)S(1)} %multiply_add_fusion), kind=kOutput, calls=%fused_computation.11 | convolution fusion | flops 2614080 | bytes 201732 | tf_op jit(solution)/shard_map/dot_general | solution.py:104
  39.8 0.7 reshape.110
  40.4 4.6 %all-to-all-start.1 = ((bf16[8,6,1024]{2,1,0:T(8,128)(2,1)}), bf16[8,6,1024]{2,1,0:T(8,128)(2,1)S(1)}, u32[]{:S(2)}, u32[]{:S(2)}) async-start(bf16[8,6,1024]{2,1,0:T(8,128)(2,1)} %reshape.110), calls=%async_computation.2 | async-start | bytes 262144 | tf_op jit(solution)/shard_map/all_to_all | solution.py:108
  45.1 6.7 %all-to-all-done.1 = bf16[8,6,1024]{2,1,0:T(8,128)(2,1)S(1)} async-done(((bf16[8,6,1024]{2,1,0:T(8,128)(2,1)}), bf16[8,6,1024]{2,1,0:T(8,128)(2,1)S(1)}, u32[]{:S(2)}, u32[]{:S(2)}) %all-to-all-start.1) | async-done | bytes 98336 | tf_op jit(solution)/shard_map/all_to_all | solution.py:108
  51.9 5.4 %all_gather.10 = bf16[48,2048]{1,0:T(8,128)(2,1)S(1)} all-gather(bf16[48,1024]{1,0:T(8,128)(2,1)S(1)} %reshape.111), channel_id=1, replica_groups=mesh['group'=2,'wide'=4,'narrow'=2,'deep'=2] {'narrow'}, dimensions={1}, use_global_device_ids=true | all-gather | bytes 294912 | tf_op jit(solution)/shard_map/all_gather | solution.py:113
  57.3 1.1 %fusion.9 = f32[2,48,384]{2,1,0:T(8,128)S(1)} fusion(bf16[1,2,384,2048]{3,2,1,0:T(8,128)(2,1)S(1)} %copy-done, bf16[48,2048]{1,0:T(8,128)(2,1)S(1)} %all_gather.10), kind=kOutput, calls=%fused_computation.10 | convolution fusion | flops 150994944 | bytes 3489792 | tf_op jit(solution)/shard_map/nd,gfd->gnf/dot_general | solution.py:111
  58.4 4.6 %all_gather.11 = bf16[48,768]{1,0:T(8,128)(2,1)S(1)} all-gather(bf16[48,384]{1,0:T(8,128)(2,1)S(1)} %fusion.17), channel_id=1, replica_groups=mesh['group'=2,'wide'=4,'narrow'=2,'deep'=2] {'narrow'}, dimensions={1}, use_global_device_ids=true | all-gather | bytes 110592 | tf_op jit(solution)/shard_map/all_gather | solution.py:119
  63.0 0.4 fusion.6
  63.4 0.7 reshape.112
  64.1 3.4 %all-to-all-start.2 = ((bf16[8,6,1024]{2,1,0:T(8,128)(2,1)}), bf16[8,6,1024]{2,1,0:T(8,128)(2,1)S(1)}, u32[]{:S(2)}, u32[]{:S(2)}) async-start(bf16[8,6,1024]{2,1,0:T(8,128)(2,1)} %reshape.112), calls=%async_computation.3 | async-start | bytes 262144 | tf_op jit(solution)/shard_map/all_to_all | solution.py:123
  67.5 6.7 %all-to-all-done.2 = bf16[8,6,1024]{2,1,0:T(8,128)(2,1)S(1)} async-done(((bf16[8,6,1024]{2,1,0:T(8,128)(2,1)}), bf16[8,6,1024]{2,1,0:T(8,128)(2,1)S(1)}, u32[]{:S(2)}, u32[]{:S(2)}) %all-to-all-start.2) | async-done | bytes 98336 | tf_op jit(solution)/shard_map/all_to_all | solution.py:123
  74.2 0.6 gather_fusion
  74.8 0.7 add_convert_fusion
  (29 shorter events, 0.4 us)
Async XLA Ops:
  6.5 50.7 %copy-start = (bf16[1,2,384,2048]{3,2,1,0:T(8,128)(2,1)S(1)}, bf16[1,2,384,2048]{3,2,1,0:T(8,128)(2,1)}, u32[]{:S(2)}) copy-start(bf16[1,2,384,2048]{3,2,1,0:T(8,128)(2,1)} %param.20) | copy-start | bytes 9437188
  6.5 26.3 %reduce-scatter.2.cloned.1.call-start = ((), (), s32[]{:S(2)}) async-start(), calls=%async_computation.4 | async-start | bytes 147456 | tf_op jit(solution)/shard_map/reduce_scatter | solution.py:91
  9.1 5.5 %copy-start.1 = (bf16[2048,1024]{1,0:T(8,128)(2,1)S(1)}, bf16[2048,1024]{1,0:T(8,128)(2,1)}, u32[]{:S(2)}) copy-start(bf16[2048,1024]{1,0:T(8,128)(2,1)} %param.19) | copy-start | bytes 12582916
  12.5 7.5 %copy-start.5 = (s32[24,1]{0,1:T(1,128)S(1)}, s32[24,1]{0,1:T(1,128)}, u32[]{:S(2)}) copy-start(s32[24,1]{0,1:T(1,128)} %param.22) | copy-start | bytes 292
  12.5 7.8 %copy-start.6 = (f32[2048]{0:T(1024)S(1)}, f32[2048]{0:T(1024)}, u32[]{:S(2)}) copy-start(f32[2048]{0:T(1024)} %param.18) | copy-start | bytes 24580
  12.5 20.3 %copy-start.4 = (bf16[24,2048]{1,0:T(8,128)(2,1)S(1)}, bf16[24,2048]{1,0:T(8,128)(2,1)}, u32[]{:S(2)}) copy-start(bf16[24,2048]{1,0:T(8,128)(2,1)} %param.17) | copy-start | bytes 294916
  40.4 11.3 %all-to-all-start.1 = ((bf16[8,6,1024]{2,1,0:T(8,128)(2,1)}), bf16[8,6,1024]{2,1,0:T(8,128)(2,1)S(1)}, u32[]{:S(2)}, u32[]{:S(2)}) async-start(bf16[8,6,1024]{2,1,0:T(8,128)(2,1)} %reshape.110), calls=%async_computation.2 | async-start | bytes 262144 | tf_op jit(solution)/shard_map/all_to_all | solution.py:108
  51.8 11.2 %copy-start.2 = (bf16[1,768,1024]{2,1,0:T(8,128)(2,1)S(1)}, bf16[1,768,1024]{2,1,0:T(8,128)(2,1)}, u32[]{:S(2)}) copy-start(bf16[1,768,1024]{2,1,0:T(8,128)(2,1)} %param.21) | copy-start | bytes 4718596
  51.8 15.6 %copy-start.7 = (f32[24,1]{0,1:T(1,128)S(1)}, f32[24,1]{0,1:T(1,128)}, u32[]{:S(2)}) copy-start(f32[24,1]{0,1:T(1,128)} %param.23) | copy-start | bytes 292
  57.3 17.5 %copy-start.3 = (bf16[24,1024]{1,0:T(8,128)(2,1)S(1)}, bf16[24,1024]{1,0:T(8,128)(2,1)}, u32[]{:S(2)}) copy-start(bf16[24,1024]{1,0:T(8,128)(2,1)} %reduce-scatter.2.cloned.1.call-done) | copy-start | bytes 147460
  64.1 10.1 %all-to-all-start.2 = ((bf16[8,6,1024]{2,1,0:T(8,128)(2,1)}), bf16[8,6,1024]{2,1,0:T(8,128)(2,1)S(1)}, u32[]{:S(2)}, u32[]{:S(2)}) async-start(bf16[8,6,1024]{2,1,0:T(8,128)(2,1)} %reshape.112), calls=%async_computation.3 | async-start | bytes 262144 | tf_op jit(solution)/shard_map/all_to_all | solution.py:123
Sparse Core Ops, SparseCore 0:
  20.1 12.7 reduce-scatter.1
where the time goes:
time: 82.9 us; the launch traced here: 82.4 us
  waiting for transfers between devices  25.9 us (31%)
  blocking collectives  20.8 us (25%)
  between operations  13.6 us (16%)
  starting transfers between devices  7.97 us (10%)
  matrix products  6.37 us (8%)
  local copies, waits for them, and re-layouts  4.57 us (6%)
  other arithmetic  3.07 us (4%)
    reduce_scatter x1, waiting for transfers between devices, shards(): lax.psum_scatter(partial_value.astype(jnp.bfloat16), 'narrow', scatter_di...  12.5 us
    all_to_all x1, waiting for transfers between devices, shards(): lax.all_to_all(outgoing, ('wide', 'deep'), split_axis=0, concat_axis=0, t...  6.72 us
    all_to_all x1, waiting for transfers between devices, shards(): lax.all_to_all(expert_share.reshape(experts, capacity, share_width), ('wi...  6.66 us
    all_gather x1, blocking collectives, shards(): lax.all_gather(incoming, 'narrow', axis=1, tiled=True)  5.42 us
    psum x1, blocking collectives, shards(): lax.psum(jnp.sum(mixed_mine * mixed_mine, -1, keepdims=True), 'narrow')  4.93 us
    all_gather x1, blocking collectives, shards(): lax.all_gather(hidden_act, 'narrow', axis=1, tiled=True)  4.63 us
    all_to_all x1, starting transfers between devices, shards(): lax.all_to_all(outgoing, ('wide', 'deep'), split_axis=0, concat_axis=0, t...  4.6 us
    all_to_all x1, blocking collectives, shards(): lax.all_to_all(paired.astype(jnp.bfloat16), 'deep', split_axis=0, concat_...  3.79 us
  transfers between devices with their start and end apart: 3, of which 3 were waited for; matrix products, arithmetic and copies ran while one was open for 0% of the time, Pallas kernels for 0%

commit v1 on v0

v1 whole, which is shorter than its diff:
```python
import math

import jax
import jax.numpy as jnp
from jax import lax
from jax.sharding import PartitionSpec as P


def swap(value, axis):
    return lax.ppermute(value, axis, [(0, 1), (1, 0)])


def from_others(value, axis):
    size = lax.axis_size(axis)
    return [
        lax.ppermute(value, axis, [(i, (i + step) % size) for i in range(size)])
        for step in range(1, size)
    ]


def direct(size):
    return size <= 4 and size & (size - 1) == 0


def exchange(blocks, axis):
    size = lax.axis_size(axis)
    if not direct(size):
        return lax.all_to_all(blocks, axis, split_axis=0, concat_axis=0, tiled=True)
    parts = [blocks[0]]
    for k in range(1, size):
        parts.append(lax.ppermute(blocks[k], axis, [(i, i ^ k) for i in range(size)]))
    return jnp.stack(parts)


def attention(queries, cache_keys, cache_values, fresh_pairs, lengths):
    row_count = queries.shape[0]
    local_heads = cache_keys.shape[1]
    length = cache_keys.shape[2]
    head_size = cache_keys.shape[3]
    group_size = queries.shape[1] // (local_heads * head_size)
    score_scale = 1.0 / math.sqrt(head_size)
    query_heads = queries.reshape(row_count, local_heads, group_size, head_size)
    fresh_heads = fresh_pairs.reshape(row_count, 2, local_heads, head_size)
    scores = (
        jnp.einsum("rkgd,rkld->rkgl", query_heads, cache_keys, preferred_element_type=jnp.float32)
        * score_scale
    )
    in_cache = jnp.arange(length, dtype=jnp.int32)[None, :] < lengths[:, None]
    scores = jnp.where(in_cache[:, None, None, :], scores, -1e30)
    own_score = (
        jnp.einsum(
            "rkgd,rkd->rkg", query_heads, fresh_heads[:, 0], preferred_element_type=jnp.float32
        )
        * score_scale
    )
    row_max = jnp.maximum(jnp.max(scores, -1), own_score)
    weights_raw = jnp.exp(scores - row_max[..., None])
    own_raw = jnp.exp(own_score - row_max)
    denominator = jnp.sum(weights_raw, -1) + own_raw
    attention_weights = (weights_raw / denominator[..., None]).astype(jnp.bfloat16)
    own_weight = (own_raw / denominator).astype(jnp.bfloat16)
    attended = jnp.einsum(
        "rkgl,rkld->rkgd", attention_weights, cache_values, preferred_element_type=jnp.float32
    )
    attended = (
        attended
        + own_weight.astype(jnp.float32)[..., None]
        * fresh_heads[:, 1].astype(jnp.float32)[:, :, None, :]
    )
    return attended.astype(jnp.bfloat16).reshape(row_count, -1)


def shards(
    queries,
    cache_keys,
    cache_values,
    fresh_pairs,
    lengths,
    residual,
    norm_gain,
    output_weight,
    expert_gate_up,
    expert_down,
    routed_experts,
    router_weights,
):
    row_count, full_width = residual.shape
    half_width = output_weight.shape[1]
    narrow_count = lax.axis_size("narrow")
    wide_count = lax.axis_size("wide")
    deep_count = lax.axis_size("deep")
    assert deep_count == 2 and narrow_count % deep_count == 0
    narrow_index = lax.axis_index("narrow")
    wide_index = lax.axis_index("wide")
    deep_index = lax.axis_index("deep")
    share_width = full_width // narrow_count
    picks = routed_experts.shape[1]
    capacity = row_count // 4
    pair_rows = 2 * capacity
    block_rows = 2 * pair_rows
    slots = wide_count * block_rows

    flat_experts = routed_experts.reshape(-1)
    expert_count = wide_count * deep_count
    hits = (flat_experts[:, None] == jnp.arange(expert_count, dtype=jnp.int32)[None, :]).astype(
        jnp.int32
    )
    place = jnp.sum((jnp.cumsum(hits, 0) - hits) * hits, 1)
    expert_wide = flat_experts // 2
    wide_step = expert_wide ^ wide_index if direct(wide_count) else expert_wide
    crosses = (flat_experts % 2) ^ deep_index
    own_target = (wide_step * 2 + crosses) * pair_rows + crosses * capacity + place
    lent_target = (wide_step * 2 + 1 - crosses) * pair_rows + crosses * capacity + place
    other_target = swap(lent_target, "deep")
    targets = jnp.concatenate([own_target, other_target]).reshape(2 * row_count, picks)
    selector = jnp.sum(
        (jnp.arange(slots, dtype=jnp.int32)[:, None, None] == targets[None]).astype(jnp.bfloat16),
        -1,
    )
    other_residual = swap(
        lax.dynamic_slice_in_dim(residual, (1 - deep_index) * half_width, half_width, 1), "deep"
    )
    residual_half = jnp.concatenate(
        [
            lax.dynamic_slice_in_dim(residual, deep_index * half_width, half_width, 1),
            other_residual,
        ]
    ).astype(jnp.float32)

    attended = attention(queries, cache_keys, cache_values, fresh_pairs, lengths)
    both = jnp.concatenate([attended, swap(attended, "deep")])
    partial_sum = jnp.dot(both, output_weight, preferred_element_type=jnp.float32)
    mixed = residual_half + partial_sum
    for other in from_others(partial_sum.astype(jnp.bfloat16), "narrow"):
        mixed = mixed + other.astype(jnp.float32)

    other_half = swap(mixed[row_count:], "deep")
    shares_per_half = half_width // share_width
    mixed_mine = jnp.where(
        narrow_index // shares_per_half == deep_index, mixed[:row_count], other_half
    )
    mixed_mine = lax.dynamic_slice_in_dim(
        mixed_mine, (narrow_index % shares_per_half) * share_width, share_width, 1
    )

    outgoing = jnp.dot(
        selector, mixed.astype(jnp.bfloat16), preferred_element_type=jnp.float32
    ).astype(jnp.bfloat16)
    arrived = exchange(outgoing.reshape(wide_count, block_rows, half_width), "wide")
    kept = arrived[:, :pair_rows].reshape(wide_count * pair_rows, half_width)
    passed = arrived[:, pair_rows:].reshape(wide_count * pair_rows, half_width)
    crossed = swap(passed, "deep")
    rows = jnp.where(
        deep_index == 0,
        jnp.concatenate([kept, crossed], 1),
        jnp.concatenate([crossed, kept], 1),
    ).astype(jnp.float32)
    mean_square = jnp.mean(rows * rows, -1, keepdims=True)
    normed = (rows * lax.rsqrt(mean_square + 1e-06) * norm_gain).astype(jnp.bfloat16)
    both_parts = jnp.einsum(
        "nd,gfd->gnf", normed, expert_gate_up[0], preferred_element_type=jnp.float32
    )
    hidden_act = (jax.nn.silu(both_parts[0]) * both_parts[1]).astype(jnp.bfloat16)
    if narrow_count == 2:
        other_hidden = swap(hidden_act, "narrow")
        hidden_full = jnp.where(
            narrow_index == 0,
            jnp.concatenate([hidden_act, other_hidden], 1),
            jnp.concatenate([other_hidden, hidden_act], 1),
        )
    else:
        hidden_full = lax.all_gather(hidden_act, "narrow", axis=1, tiled=True)
    expert_share = jnp.dot(
        hidden_full, expert_down[0], preferred_element_type=jnp.float32
    ).astype(jnp.bfloat16)
    returned = exchange(expert_share.reshape(wide_count, pair_rows, share_width), "wide")
    returned = returned.reshape(wide_count * pair_rows, share_width)
    candidates = jnp.concatenate([returned, swap(returned, "deep")])
    back = (crosses * wide_count + wide_step) * pair_rows + crosses * capacity + place
    gatherer = (
        back[:, None] == jnp.arange(candidates.shape[0], dtype=jnp.int32)[None, :]
    ).astype(jnp.bfloat16)
    chosen = jnp.dot(gatherer, candidates, preferred_element_type=jnp.float32)
    weights = router_weights / jnp.sum(router_weights, -1, keepdims=True)
    combined = jnp.sum(
        chosen.reshape(row_count, picks, share_width) * weights[:, :, None], 1
    )
    return (mixed_mine + combined).astype(jnp.bfloat16)


def solution(mesh):
    in_specs = (
        P(("group", "wide", "deep"), "narrow"),
        P(("group", "wide", "deep"), "narrow", None, None),
        P(("group", "wide", "deep"), "narrow", None, None),
        P(("group", "wide", "deep"), None, "narrow"),
        P(("group", "wide", "deep")),
        P(("group", "wide", "deep"), None),
        P(),
        P("narrow", "deep"),
        P(("wide", "deep"), None, "narrow", None),
        P(("wide", "deep"), None, "narrow"),
        P(("group", "wide", "deep"), None),
        P(("group", "wide", "deep"), None),
    )
    out_specs = P(("group", "wide", "deep"), "narrow")
    return jax.shard_map(shards, mesh=mesh, in_specs=in_specs, out_specs=out_specs, check_vma=False)
```

time: 82.9 us -> 49 us (0.59)
  blocking collectives: 20.8 us -> 0 us
  between operations: 13.6 us -> 0.2 us
  waiting for transfers between devices: 25.9 us -> 15 us
  starting transfers between devices: 7.97 us -> 14.2 us
  matrix products: 6.37 us -> 10.7 us
  local copies, waits for them, and re-layouts: 4.57 us -> 6.11 us
    ppermute x0 -> x14, waiting for transfers between devices: none -> 15 us  [the longest x6 7.78 us: exchange(): lax.ppermute(blocks[k], axis, [(i, i ^ k) for i in range(size)])]
    ppermute x0 -> x14, starting transfers between devices: none -> 14.2 us  [the longest x6 8.93 us: exchange(): lax.ppermute(blocks[k], axis, [(i, i ^ k) for i in range(size)])]
    all_to_all x2 -> x0, waiting for transfers between devices: 13.4 us -> none  [the longest x1 6.72 us: shards(): lax.all_to_all(outgoing, ('wide', 'deep'), split_axis=0, concat_axis=0, t...]
    reduce_scatter x1 -> x0, waiting for transfers between devices: 12.5 us -> none  [shards(): lax.psum_scatter(partial_value.astype(jnp.bfloat16), 'narrow', scatter_di...]
    all_gather x3 -> x0, blocking collectives: 12.1 us -> none  [the longest x1 5.42 us: shards(): lax.all_gather(incoming, 'narrow', axis=1, tiled=True)]
    all_to_all x2 -> x0, starting transfers between devices: 7.97 us -> none  [the longest x1 4.6 us: shards(): lax.all_to_all(outgoing, ('wide', 'deep'), split_axis=0, concat_axis=0, t...]
    psum x1 -> x0, blocking collectives: 4.93 us -> none  [shards(): lax.psum(jnp.sum(mixed_mine * mixed_mine, -1, keepdims=True), 'narrow')]
    dot_general x7 -> x8, matrix products: 6.37 us -> 10.7 us  [the longest x1 3.03 us: shards(): jnp.dot(both, output_weight, preferred_element_type=jnp.float32)]
  transfers between devices with their start and end apart: 3 -> 14, of which waited for: 3 -> 7; matrix products, arithmetic and copies ran while one was open for 0% -> 14% of each run, Pallas kernels for 0% -> 0%
where the time goes in v1:
time: 49 us; the launch traced here: 48.6 us
  waiting for transfers between devices  15 us (31%)
  starting transfers between devices  14.2 us (29%)
  matrix products  10.7 us (22%)
  local copies, waits for them, and re-layouts  6.11 us (12%)
  other arithmetic  2.43 us (5%)
    ppermute x6, starting transfers between devices, exchange(): lax.ppermute(blocks[k], axis, [(i, i ^ k) for i in range(size)])  8.93 us
    ppermute x6, waiting for transfers between devices, exchange(): lax.ppermute(blocks[k], axis, [(i, i ^ k) for i in range(size)])  7.78 us
    ppermute x7, waiting for transfers between devices, swap(): return lax.ppermute(value, axis, [(0, 1), (1, 0)])  3.9 us
    ppermute x1, waiting for transfers between devices, from_others(): lax.ppermute(value, axis, [(i, (i + step) % size) for i in range(size)])  3.35 us
    dot_general x1, matrix products, shards(): jnp.dot(both, output_weight, preferred_element_type=jnp.float32)  3.03 us
    ppermute x7, starting transfers between devices, swap(): return lax.ppermute(value, axis, [(0, 1), (1, 0)])  2.7 us
    ppermute x1, starting transfers between devices, from_others(): lax.ppermute(value, axis, [(i, (i + step) % size) for i in range(size)])  2.57 us
    dot_general x1, matrix products, shards(): jnp.dot(hidden_full, expert_down[0], preferred_element_type=jnp.float32)  1.79 us
  transfers between devices with their start and end apart: 14, of which 7 were waited for; matrix products, arithmetic and copies ran while one was open for 14% of the time, Pallas kernels for 0%

profile of v1, /device:TPU:0, one launch (start us, length us, event | category | flops | bytes accessed | tf_op | source)
XLA Modules:
  0.0 48.6 jit_solution(4502841683105896199)
XLA Ops:
  0.0 1.1 %copy.18 = bf16[3,8,16,128]{3,2,1,0:T(8,128)(2,1)S(1)} copy(bf16[3,8,16,128]{3,1,2,0:T(8,128)(2,1)} %bitcast.81) | data formatting | bytes 196608
  1.1 0.7 %iota_compare_fusion.4 = pred[24,32]{1,0:T(8,128)(4,1)S(1)} fusion(s32[24]{0:T(128)} %param.16), kind=kLoop, calls=%fused_computation.68 | loop fusion | flops 768 | bytes 864 | tf_op jit(solution)/shard_map/lt | solution.py:48
  1.8 0.8 %reshape.102 = bf16[24,2,2,128]{3,2,1,0:T(2,128)(2,1)S(1)} reshape(bf16[24,2,256]{2,1,0:T(2,128)(2,1)} %param.15) | data formatting | bytes 49152 | tf_op jit(solution)/shard_map/reshape | solution.py:43
  2.8 1.4 %fusion.59 = (f32[24,2,8]{2,1,0:T(2,128)S(1)}, f32[24,2,8,32]{3,2,1,0:T(8,128)S(1)}) fusion(bf16[24,2,8,128]{3,2,1,0:T(8,128)(2,1)S(1)} %bitcast.78, bf16[24,2,32,128]{3,2,1,0:T(8,128)(2,1)} %param.13, pred[24,32]{1,0:T(8,128)(4,1)S(1)} %iota_compare_fusion.4), kind=kOutput, calls=%fused_computation.99 | convolution fusion | flops 3182208 | bytes 542976 | tf_op jit(solution)/shard_map/rkgd,rkld->rkgl/dot_general | solution.py:45
  4.2 0.2 fusion.26
  4.5 1.3 %fusion.5 = bf16[24,2,8,128]{3,2,1,0:T(8,128)(2,1)S(1)} fusion(bf16[24,2,32,128]{3,2,1,0:T(8,128)(2,1)} %param.14, f32[24,2,8,32]{3,2,1,0:T(8,128)S(1)} %get-tuple-element.25, f32[24,2,128]{2,1,0:T(2,128)S(1)} %get-tuple-element.23, f32[24,2,8]{2,1,0:T(2,128)S(1)} %get-tuple-element.21, f32[24,2,8]{2,1,0:T(2,128)S(1)} %get-tuple-element.20, ...), kind=kOutput, calls=%fused_computation.8 | convolution fusion | flops 3330048 | bytes 569856 | tf_op jit(solution)/shard_map/rkgl,rkld->rkgd/dot_general | solution.py:62
  5.9 0.6 %collective-permute-start.1 = (bf16[24,2048]{1,0:T(8,128)(2,1)S(1)}, bf16[24,2048]{1,0:T(8,128)(2,1)S(1)}, u32[]{:S(2)}, u32[]{:S(2)}) collective-permute-start(bf16[24,2048]{1,0:T(8,128)(2,1)S(1)} %bitcast.79), channel_id=1, source_target_pairs={{0,1},{1,0},{2,3},{3,2},{4,5},{5,4},{6,7},{7,6},{8,9},{9,8},{10,11... | collective-permute-start | bytes 294920 | tf_op jit(solution)/shard_map/ppermute | solution.py:10
  6.4 0.6 %constant_dynamic-slice_fusion.1 = (bf16[24,1024]{1,0:T(8,128)(2,1)S(1)}, bf16[24,1024]{1,0:T(8,128)(2,1)}) fusion(bf16[24,2048]{1,0:T(8,128)(2,1)S(1)} %copy-done.1, s32[]{:T(128)S(6)} %select_n.64, s32[]{:T(128)S(6)} %select_n.65), kind=kLoop, calls=%fused_computation.91 | loop fusion | bytes 196616 | tf_op jit(solution)/shard_map/dynamic_slice | solution.py:125
  7.4 0.5 %collective-permute-start.4 = (s32[24]{0:T(128)S(1)}, s32[24]{0:T(128)S(1)}, u32[]{:S(2)}, u32[]{:S(2)}) collective-permute-start(s32[24]{0:T(128)S(1)} %add_add_fusion), channel_id=1, source_target_pairs={{0,1},{1,0},{2,3},{3,2},{4,5},{5,4},{6,7},{7,6},{8,9},{9,8},{10,11... | collective-permute-start | bytes 296 | tf_op jit(solution)/shard_map/ppermute | solution.py:10
  8.0 3.0 %fusion.60 = (bf16[48,1024]{1,0:T(8,128)(2,1)S(1)}, f32[48,1024]{1,0:T(8,128)S(1)}) fusion(bf16[2048,1024]{1,0:T(8,128)(2,1)} %param.19, bf16[24,2048]{1,0:T(8,128)(2,1)S(1)} %collective-permute-done.1, bf16[24,2048]{1,0:T(8,128)(2,1)S(1)} %bitcast.80), kind=kOutput, calls=%fused_computation.100 | convolution fusion | flops 201768960 | bytes 4685824 | tf_op jit(solution)/shard_map/dot_general | solution.py:132
  11.0 2.6 %collective-permute-start.2 = (bf16[48,1024]{1,0:T(8,128)(2,1)S(1)}, bf16[48,1024]{1,0:T(8,128)(2,1)S(1)}, u32[]{:S(2)}, u32[]{:S(2)}) collective-permute-start(bf16[48,1024]{1,0:T(8,128)(2,1)S(1)} %get-tuple-element.26), channel_id=1, source_target_pairs={{0,2},{2,0},{1,3},{3,1},{4,6},{6,4},{5,7},{7,5},{8,10},{10,8},{9,1... | collective-permute-start | bytes 294920 | tf_op jit(solution)/shard_map/ppermute | solution.py:16
  13.7 3.4 %collective-permute-done.2 = bf16[48,1024]{1,0:T(8,128)(2,1)S(1)} collective-permute-done((bf16[48,1024]{1,0:T(8,128)(2,1)S(1)}, bf16[48,1024]{1,0:T(8,128)(2,1)S(1)}, u32[]{:S(2)}, u32[]{:S(2)}) %collective-permute-start.2) | collective-permute-done | bytes 98336 | tf_op jit(solution)/shard_map/ppermute | solution.py:16
  17.3 2.9 %collective-permute-start.6 = (bf16[24,1024]{1,0:T(8,128)(2,1)S(1)}, bf16[24,1024]{1,0:T(8,128)(2,1)S(1)}, u32[]{:S(2)}, u32[]{:S(2)}) collective-permute-start(bf16[24,1024]{1,0:T(8,128)(2,1)S(1)} %get-tuple-element.12), channel_id=1, source_target_pairs={{0,8},{4,12},{8,0},{12,4},{1,9},{5,13},{9,1},{13,5},{2,10},{6,14},... | collective-permute-start | bytes 147464 | tf_op jit(solution)/shard_map/ppermute | solution.py:31
  20.2 1.3 %collective-permute-start.7 = (bf16[24,1024]{1,0:T(8,128)(2,1)S(1)}, bf16[24,1024]{1,0:T(8,128)(2,1)S(1)}, u32[]{:S(2)}, u32[]{:S(2)}) collective-permute-start(bf16[24,1024]{1,0:T(8,128)(2,1)S(1)} %get-tuple-element.11), channel_id=1, source_target_pairs={{0,12},{4,8},{8,4},{12,0},{1,13},{5,9},{9,5},{13,1},{2,14},{6,10},... | collective-permute-start | bytes 147464 | tf_op jit(solution)/shard_map/ppermute | solution.py:31
  21.8 1.0 %collective-permute-done.6 = bf16[24,1024]{1,0:T(8,128)(2,1)S(1)} collective-permute-done((bf16[24,1024]{1,0:T(8,128)(2,1)S(1)}, bf16[24,1024]{1,0:T(8,128)(2,1)S(1)}, u32[]{:S(2)}, u32[]{:S(2)}) %collective-permute-start.6) | collective-permute-done | bytes 49184 | tf_op jit(solution)/shard_map/ppermute | solution.py:31
  22.8 3.4 %collective-permute-done.7 = bf16[24,1024]{1,0:T(8,128)(2,1)S(1)} collective-permute-done((bf16[24,1024]{1,0:T(8,128)(2,1)S(1)}, bf16[24,1024]{1,0:T(8,128)(2,1)S(1)}, u32[]{:S(2)}, u32[]{:S(2)}) %collective-permute-start.7) | collective-permute-done | bytes 49184 | tf_op jit(solution)/shard_map/ppermute | solution.py:31
  26.2 0.7 %fusion.58 = (bf16[4,12,1024]{2,1,0:T(8,128)(2,1)S(1)}, bf16[4,12,1024]{2,1,0:T(8,128)(2,1)}) fusion(bf16[4,24,1024]{2,1,0:T(8,128)(2,1)S(1)} %pad_maximum_fusion), kind=kLoop, calls=%fused_computation.98 | loop fusion | bytes 393216 | tf_op jit(solution)/shard_map/slice | solution.py:151
  26.9 0.7 %reshape.105 = bf16[48,1024]{1,0:T(8,128)(2,1)} reshape(bf16[4,12,1024]{2,1,0:T(8,128)(2,1)S(1)} %get-tuple-element.8) | data formatting | bytes 196608 | tf_op jit(solution)/shard_map/reshape | solution.py:151
  27.5 0.9 %reshape.104 = bf16[48,1024]{1,0:T(8,128)(2,1)S(1)} reshape(bf16[4,12,1024]{2,1,0:T(8,128)(2,1)} %get-tuple-element.9) | data formatting | bytes 196608 | tf_op jit(solution)/shard_map/reshape | solution.py:150
  28.5 0.6 %collective-permute-done.8 = bf16[48,1024]{1,0:T(8,128)(2,1)S(1)} collective-permute-done((bf16[48,1024]{1,0:T(8,128)(2,1)}, bf16[48,1024]{1,0:T(8,128)(2,1)S(1)}, u32[]{:S(2)}, u32[]{:S(2)}) %collective-permute-start.8) | collective-permute-done | bytes 98336 | tf_op jit(solution)/shard_map/ppermute | solution.py:10
  29.2 1.1 %fusion.9 = f32[2,48,384]{2,1,0:T(8,128)S(1)} fusion(bf16[1,2,384,2048]{3,2,1,0:T(8,128)(2,1)S(1)} %copy-done, f32[2048]{0:T(1024)S(1)} %copy-done.2, f32[48]{0:T(128)S(1)} %add_rsqrt_fusion, bf16[48,1024]{1,0:T(8,128)(2,1)S(1)} %collective-permute-done.8, bf16[48,1024]{1,0:T(8,128)(2,1)S(1)} %reshape.104, pred[]{:T(512)S(6)} %eq.69), kind=kOutput, calls=%fused_computation.10 | convolution fusion | flops 152272896 | bytes 3498177 | tf_op jit(solution)/shard_map/nd,gfd->gnf/dot_general | solution.py:160
  30.3 1.6 %collective-permute-start.9 = (bf16[48,384]{1,0:T(8,128)(2,1)S(1)}, bf16[48,384]{1,0:T(8,128)(2,1)S(1)}, u32[]{:S(2)}, u32[]{:S(2)}) collective-permute-start(bf16[48,384]{1,0:T(8,128)(2,1)S(1)} %fusion.33), channel_id=1, source_target_pairs={{0,2},{2,0},{1,3},{3,1},{4,6},{6,4},{5,7},{7,5},{8,10},{10,8},{9,1... | collective-permute-start | bytes 110600 | tf_op jit(solution)/shard_map/ppermute | solution.py:10
  31.9 2.5 %collective-permute-done.9 = bf16[48,384]{1,0:T(8,128)(2,1)S(1)} collective-permute-done((bf16[48,384]{1,0:T(8,128)(2,1)S(1)}, bf16[48,384]{1,0:T(8,128)(2,1)S(1)}, u32[]{:S(2)}, u32[]{:S(2)}) %collective-permute-start.9) | collective-permute-done | bytes 36896 | tf_op jit(solution)/shard_map/ppermute | solution.py:10
  34.4 1.8 %fusion.6 = bf16[48,1024]{1,0:T(8,128)(2,1)S(1)} fusion(bf16[1,768,1024]{2,1,0:T(8,128)(2,1)} %param.21, bf16[48,384]{1,0:T(8,128)(2,1)S(1)} %collective-permute-done.9, bf16[48,384]{1,0:T(8,128)(2,1)S(1)} %fusion.33, pred[]{:T(512)S(6)} %eq.68), kind=kOutput, calls=%fused_computation.9 | convolution fusion | flops 75878400 | bytes 1744897 | tf_op jit(solution)/shard_map/dot_general | solution.py:173
  36.3 2.7 %collective-permute-start.11 = (bf16[12,1024]{1,0:T(8,128)(2,1)S(1)}, bf16[12,1024]{1,0:T(8,128)(2,1)S(1)}, u32[]{:S(2)}, u32[]{:S(2)}) collective-permute-start(bf16[12,1024]{1,0:T(8,128)(2,1)S(1)} %get-tuple-element.16), channel_id=1, source_target_pairs={{0,8},{4,12},{8,0},{12,4},{1,9},{5,13},{9,1},{13,5},{2,10},{6,14},... | collective-permute-start | bytes 73736 | tf_op jit(solution)/shard_map/ppermute | solution.py:31
  39.0 1.7 %collective-permute-start.12 = (bf16[12,1024]{1,0:T(8,128)(2,1)S(1)}, bf16[12,1024]{1,0:T(8,128)(2,1)S(1)}, u32[]{:S(2)}, u32[]{:S(2)}) collective-permute-start(bf16[12,1024]{1,0:T(8,128)(2,1)S(1)} %get-tuple-element.15), channel_id=1, source_target_pairs={{0,12},{4,8},{8,4},{12,0},{1,13},{5,9},{9,5},{13,1},{2,14},{6,10},... | collective-permute-start | bytes 73736 | tf_op jit(solution)/shard_map/ppermute | solution.py:31
  40.7 0.6 %slice.81 = f32[24,1024]{1,0:T(8,128)} slice(f32[48,1024]{1,0:T(8,128)S(1)} %convert_add_fusion), slice={[24:48], [0:1024]} | slice | bytes 196608 | tf_op jit(solution)/shard_map/slice | solution.py:137
  41.3 3.4 %collective-permute-done.12 = bf16[12,1024]{1,0:T(8,128)(2,1)S(1)} collective-permute-done((bf16[12,1024]{1,0:T(8,128)(2,1)S(1)}, bf16[12,1024]{1,0:T(8,128)(2,1)S(1)}, u32[]{:S(2)}, u32[]{:S(2)}) %collective-permute-start.12) | collective-permute-done | bytes 24608 | tf_op jit(solution)/shard_map/ppermute | solution.py:31
  44.7 0.7 %reshape.106 = bf16[48,1024]{1,0:T(8,128)(2,1)} reshape(bf16[4,12,1024]{2,1,0:T(8,128)(2,1)S(1)} %pad_maximum_fusion.1) | data formatting | bytes 196608 | tf_op jit(solution)/shard_map/reshape | solution.py:177
  45.4 0.7 %divide_bitcast_fusion = f32[24]{0:T(128)S(1)} fusion(f32[24,1]{0,1:T(1,128)} %param.23), kind=kLoop, calls=%fused_computation.92 | loop fusion | flops 24 | bytes 192 | tf_op jit(solution)/shard_map/mul | solution.py:186
  46.1 0.8 %collective-permute-done.13 = bf16[48,1024]{1,0:T(8,128)(2,1)S(1)} collective-permute-done((bf16[48,1024]{1,0:T(8,128)(2,1)}, bf16[48,1024]{1,0:T(8,128)(2,1)S(1)}, u32[]{:S(2)}, u32[]{:S(2)}) %collective-permute-start.13) | collective-permute-done | bytes 98336 | tf_op jit(solution)/shard_map/ppermute | solution.py:10
  46.9 1.7 %fusion.28 = bf16[24,1024]{1,0:T(8,128)(2,1)} fusion(f32[24,1024]{1,0:T(8,128)} %collective-permute-done.3, f32[48,1024]{1,0:T(8,128)S(1)} %convert_add_fusion, f32[24]{0:T(128)S(1)} %divide_bitcast_fusion, bf16[48,1024]{1,0:T(8,128)(2,1)S(1)} %collective-permute-done.13, bf16[48,1024]{1,0:T(8,128)(2,1)} %reshape.106, pred[]{:T(512)S(6)} %eq.59, ...), kind=kOutput, calls=%fused_computation.37 | convolution fusion | flops 5212416 | bytes 442561 | tf_op jit(solution)/shard_map/dot_general | solution.py:183
  (42 shorter events, 1.6 us)
Async XLA Ops:
  0.0 29.2 %copy-start = (bf16[1,2,384,2048]{3,2,1,0:T(8,128)(2,1)S(1)}, bf16[1,2,384,2048]{3,2,1,0:T(8,128)(2,1)}, u32[]{:S(2)}) copy-start(bf16[1,2,384,2048]{3,2,1,0:T(8,128)(2,1)} %param.20) | copy-start | bytes 9437188
  0.0 6.4 %copy-start.1 = (bf16[24,2048]{1,0:T(8,128)(2,1)S(1)}, bf16[24,2048]{1,0:T(8,128)(2,1)}, u32[]{:S(2)}) copy-start(bf16[24,2048]{1,0:T(8,128)(2,1)} %param.17) | copy-start | bytes 294916
  2.6 4.5 %copy-start.3 = (s32[24,1]{0,1:T(1,128)S(1)}, s32[24,1]{0,1:T(1,128)}, u32[]{:S(2)}) copy-start(s32[24,1]{0,1:T(1,128)} %param.22) | copy-start | bytes 292
  5.9 2.1 %collective-permute-start.1 = (bf16[24,2048]{1,0:T(8,128)(2,1)S(1)}, bf16[24,2048]{1,0:T(8,128)(2,1)S(1)}, u32[]{:S(2)}, u32[]{:S(2)}) collective-permute-start(bf16[24,2048]{1,0:T(8,128)(2,1)S(1)} %bitcast.79), channel_id=1, source_target_pairs={{0,1},{1,0},{2,3},{3,2},{4,5},{5,4},{6,7},{7,6},{8,9},{9,8},{10,11... | collective-permute-start | bytes 294920 | tf_op jit(solution)/shard_map/ppermute | solution.py:10
  7.0 6.6 %collective-permute-start = (bf16[24,1024]{1,0:T(8,128)(2,1)}, bf16[24,1024]{1,0:T(8,128)(2,1)S(1)}, u32[]{:S(2)}, u32[]{:S(2)}) collective-permute-start(bf16[24,1024]{1,0:T(8,128)(2,1)} %get-tuple-element.19), channel_id=1, source_target_pairs={{0,1},{1,0},{2,3},{3,2},{4,5},{5,4},{6,7},{7,6},{8,9},{9,8},{10,11... | collective-permute-start | bytes 147464 | tf_op jit(solution)/shard_map/ppermute | solution.py:10
  7.4 21.8 %copy-start.2 = (f32[2048]{0:T(1024)S(1)}, f32[2048]{0:T(1024)}, u32[]{:S(2)}) copy-start(f32[2048]{0:T(1024)} %param.18) | copy-start | bytes 24580
  7.4 6.2 %collective-permute-start.4 = (s32[24]{0:T(128)S(1)}, s32[24]{0:T(128)S(1)}, u32[]{:S(2)}, u32[]{:S(2)}) collective-permute-start(s32[24]{0:T(128)S(1)} %add_add_fusion), channel_id=1, source_target_pairs={{0,1},{1,0},{2,3},{3,2},{4,5},{5,4},{6,7},{7,6},{8,9},{9,8},{10,11... | collective-permute-start | bytes 296 | tf_op jit(solution)/shard_map/ppermute | solution.py:10
  11.0 6.0 %collective-permute-start.2 = (bf16[48,1024]{1,0:T(8,128)(2,1)S(1)}, bf16[48,1024]{1,0:T(8,128)(2,1)S(1)}, u32[]{:S(2)}, u32[]{:S(2)}) collective-permute-start(bf16[48,1024]{1,0:T(8,128)(2,1)S(1)} %get-tuple-element.26), channel_id=1, source_target_pairs={{0,2},{2,0},{1,3},{3,1},{4,6},{6,4},{5,7},{7,5},{8,10},{10,8},{9,1... | collective-permute-start | bytes 294920 | tf_op jit(solution)/shard_map/ppermute | solution.py:16
  17.3 5.5 %collective-permute-start.6 = (bf16[24,1024]{1,0:T(8,128)(2,1)S(1)}, bf16[24,1024]{1,0:T(8,128)(2,1)S(1)}, u32[]{:S(2)}, u32[]{:S(2)}) collective-permute-start(bf16[24,1024]{1,0:T(8,128)(2,1)S(1)} %get-tuple-element.12), channel_id=1, source_target_pairs={{0,8},{4,12},{8,0},{12,4},{1,9},{5,13},{9,1},{13,5},{2,10},{6,14},... | collective-permute-start | bytes 147464 | tf_op jit(solution)/shard_map/ppermute | solution.py:31
  20.2 6.0 %collective-permute-start.7 = (bf16[24,1024]{1,0:T(8,128)(2,1)S(1)}, bf16[24,1024]{1,0:T(8,128)(2,1)S(1)}, u32[]{:S(2)}, u32[]{:S(2)}) collective-permute-start(bf16[24,1024]{1,0:T(8,128)(2,1)S(1)} %get-tuple-element.11), channel_id=1, source_target_pairs={{0,12},{4,8},{8,4},{12,0},{1,13},{5,9},{9,5},{13,1},{2,14},{6,10},... | collective-permute-start | bytes 147464 | tf_op jit(solution)/shard_map/ppermute | solution.py:31
  21.5 4.6 %collective-permute-start.5 = (bf16[24,1024]{1,0:T(8,128)(2,1)S(1)}, bf16[24,1024]{1,0:T(8,128)(2,1)S(1)}, u32[]{:S(2)}, u32[]{:S(2)}) collective-permute-start(bf16[24,1024]{1,0:T(8,128)(2,1)S(1)} %get-tuple-element.13), channel_id=1, source_target_pairs={{0,4},{4,0},{8,12},{12,8},{1,5},{5,1},{9,13},{13,9},{2,6},{6,2},{1... | collective-permute-start | bytes 147464 | tf_op jit(solution)/shard_map/ppermute | solution.py:31
  27.5 1.5 %collective-permute-start.8 = (bf16[48,1024]{1,0:T(8,128)(2,1)}, bf16[48,1024]{1,0:T(8,128)(2,1)S(1)}, u32[]{:S(2)}, u32[]{:S(2)}) collective-permute-start(bf16[48,1024]{1,0:T(8,128)(2,1)} %reshape.105), channel_id=1, source_target_pairs={{0,1},{1,0},{2,3},{3,2},{4,5},{5,4},{6,7},{7,6},{8,9},{9,8},{10,11... | collective-permute-start | bytes 294920 | tf_op jit(solution)/shard_map/ppermute | solution.py:10
  30.3 4.0 %collective-permute-start.9 = (bf16[48,384]{1,0:T(8,128)(2,1)S(1)}, bf16[48,384]{1,0:T(8,128)(2,1)S(1)}, u32[]{:S(2)}, u32[]{:S(2)}) collective-permute-start(bf16[48,384]{1,0:T(8,128)(2,1)S(1)} %fusion.33), channel_id=1, source_target_pairs={{0,2},{2,0},{1,3},{3,1},{4,6},{6,4},{5,7},{7,5},{8,10},{10,8},{9,1... | collective-permute-start | bytes 110600 | tf_op jit(solution)/shard_map/ppermute | solution.py:10
  36.2 5.1 %collective-permute-start.10 = (bf16[12,1024]{1,0:T(8,128)(2,1)S(1)}, bf16[12,1024]{1,0:T(8,128)(2,1)S(1)}, u32[]{:S(2)}, u32[]{:S(2)}) collective-permute-start(bf16[12,1024]{1,0:T(8,128)(2,1)S(1)} %get-tuple-element.17), channel_id=1, source_target_pairs={{0,4},{4,0},{8,12},{12,8},{1,5},{5,1},{9,13},{13,9},{2,6},{6,2},{1... | collective-permute-start | bytes 73736 | tf_op jit(solution)/shard_map/ppermute | solution.py:31
  36.3 5.0 %collective-permute-start.11 = (bf16[12,1024]{1,0:T(8,128)(2,1)S(1)}, bf16[12,1024]{1,0:T(8,128)(2,1)S(1)}, u32[]{:S(2)}, u32[]{:S(2)}) collective-permute-start(bf16[12,1024]{1,0:T(8,128)(2,1)S(1)} %get-tuple-element.16), channel_id=1, source_target_pairs={{0,8},{4,12},{8,0},{12,4},{1,9},{5,13},{9,1},{13,5},{2,10},{6,14},... | collective-permute-start | bytes 73736 | tf_op jit(solution)/shard_map/ppermute | solution.py:31
  39.0 5.7 %collective-permute-start.12 = (bf16[12,1024]{1,0:T(8,128)(2,1)S(1)}, bf16[12,1024]{1,0:T(8,128)(2,1)S(1)}, u32[]{:S(2)}, u32[]{:S(2)}) collective-permute-start(bf16[12,1024]{1,0:T(8,128)(2,1)S(1)} %get-tuple-element.15), channel_id=1, source_target_pairs={{0,12},{4,8},{8,4},{12,0},{1,13},{5,9},{9,5},{13,1},{2,14},{6,10},... | collective-permute-start | bytes 73736 | tf_op jit(solution)/shard_map/ppermute | solution.py:31
  41.3 4.8 %collective-permute-start.3 = (f32[24,1024]{1,0:T(8,128)}, f32[24,1024]{1,0:T(8,128)}, u32[]{:S(2)}, u32[]{:S(2)}) collective-permute-start(f32[24,1024]{1,0:T(8,128)} %slice.81), channel_id=1, source_target_pairs={{0,1},{1,0},{2,3},{3,2},{4,5},{5,4},{6,7},{7,6},{8,9},{9,8},{10,11... | collective-permute-start | bytes 294920 | tf_op jit(solution)/shard_map/ppermute | solution.py:10
  45.4 1.5 %collective-permute-start.13 = (bf16[48,1024]{1,0:T(8,128)(2,1)}, bf16[48,1024]{1,0:T(8,128)(2,1)S(1)}, u32[]{:S(2)}, u32[]{:S(2)}) collective-permute-start(bf16[48,1024]{1,0:T(8,128)(2,1)} %reshape.106), channel_id=1, source_target_pairs={{0,1},{1,0},{2,3},{3,2},{4,5},{5,4},{6,7},{7,6},{8,9},{9,8},{10,11... | collective-permute-start | bytes 294920 | tf_op jit(solution)/shard_map/ppermute | solution.py:10

commit v2 on v0

v2 whole, which is shorter than its diff:
```python
import functools
import math

import jax
import jax.numpy as jnp
from jax import lax
from jax.experimental import pallas as pl
from jax.experimental.pallas import tpu as pltpu
from jax.sharding import PartitionSpec as P

SUBLANES = 8
LANES = 128
F32 = jnp.float32
BF16 = jnp.bfloat16
VMEM = pl.BlockSpec(memory_space=pltpu.VMEM)
SMEM = pl.BlockSpec(memory_space=pltpu.SMEM)


def iota(shape, axis):
    return lax.broadcasted_iota(jnp.int32, shape, axis)


def dot(a, b):
    return jnp.dot(a, b, preferred_element_type=F32)


def dot_t(a, b):
    return lax.dot_general(a, b, (((1,), (1,)), ((), ())), preferred_element_type=F32)


def call(body, outs, operands, in_specs=None, flops=0):
    size = sum(math.prod(o.shape) * o.dtype.itemsize for o in [*operands, *outs])
    return pl.pallas_call(
        body,
        out_shape=outs,
        in_specs=in_specs or [VMEM] * len(operands),
        out_specs=[VMEM] * len(outs),
        compiler_params=pltpu.CompilerParams(vmem_limit_bytes=min(size * 2 + (8 << 20), 48 << 20)),
        cost_estimate=pl.CostEstimate(flops=flops, bytes_accessed=size, transcendentals=0),
    )(*operands)


def from_others(value, axis):
    size = lax.axis_size(axis)
    return [
        lax.ppermute(value, axis, [(i, (i + step) % size) for i in range(size)])
        for step in range(1, size)
    ]


def swap(value, axis):
    return lax.ppermute(value, axis, [(0, 1), (1, 0)])


def attention_body(capacity, experts, place, q, k, v, fresh, lengths, residual, routed, ext, kept):
    rows, heads, length, size = k.shape
    width = q.shape[1]
    group = width // (heads * size)
    scale = 1.0 / math.sqrt(size)
    many = SUBLANES * group
    q_all = q[...].astype(F32)
    shape = (many, SUBLANES * length)
    row_request = lax.rem(iota(shape, 0), SUBLANES)
    column = iota(shape, 1)
    same = row_request == lax.div(column, length)
    position = lax.rem(column, length)
    for first in range(0, rows, SUBLANES):
        batch = slice(first, first + SUBLANES)
        limit = jnp.concatenate([lengths[batch, :]] * group, 0)
        valid = same & (position < limit)
        for head in range(heads):
            at = head * group * size
            query = jnp.concatenate(
                [q_all[batch, at + g * size : at + (g + 1) * size] for g in range(group)], 0
            )
            own_key = fresh[batch, 0, head * size : (head + 1) * size].astype(F32)
            own_value = fresh[batch, 1, head * size : (head + 1) * size].astype(F32)
            keys = k[batch, head].reshape(SUBLANES * length, size)
            values = v[batch, head].reshape(SUBLANES * length, size)
            scores = jnp.where(valid, dot_t(query.astype(BF16), keys) * scale, -1e30)
            own = (
                jnp.sum(query * jnp.concatenate([own_key] * group, 0), -1, keepdims=True) * scale
            )
            top = jnp.maximum(jnp.max(scores, -1, keepdims=True), own)
            raw = jnp.exp(scores - top)
            own_raw = jnp.exp(own - top)
            inverse = 1.0 / (jnp.sum(raw, -1, keepdims=True) + own_raw)
            probs = (raw * inverse).astype(BF16)
            own_prob = (own_raw * inverse).astype(BF16).astype(F32)
            out = dot(probs, values) + own_prob * jnp.concatenate([own_value] * group, 0)
            for g in range(group):
                ext[batch, at + g * size : at + (g + 1) * size] = out[
                    g * SUBLANES : (g + 1) * SUBLANES
                ].astype(BF16)
    deep = place[0]
    half = kept.shape[1]
    kept[...] = residual[:, pl.ds(pl.multiple_of(deep * half, LANES), half)]
    ext[:, width : width + half] = residual[
        :, pl.ds(pl.multiple_of((1 - deep) * half, LANES), half)
    ]
    picks = routed.shape[1]
    lane = iota((rows, LANES), 1)
    hits = jnp.zeros((rows, LANES), F32)
    for j in range(picks):
        hits = hits + (routed[:, j : j + 1] == lane).astype(F32)
    earlier = (iota((rows, rows), 1) < iota((rows, rows), 0)).astype(F32)
    before = dot(earlier.astype(BF16), hits.astype(BF16))
    notes = jnp.zeros((rows, LANES), F32)
    for j in range(picks):
        expert = routed[:, j : j + 1]
        slot = jnp.sum(jnp.where(expert == lane, before, 0.0), -1, keepdims=True)
        slot = slot + (deep * capacity).astype(F32)
        notes = jnp.where(lane == j, expert.astype(F32), notes)
        notes = jnp.where(lane == picks + j, slot, notes)
    ext[:, width + half :] = notes.astype(BF16)


def project_body(own, other, weight, total, short):
    depth = weight.shape[0]
    both = jnp.concatenate([own[:, :depth], other[:, :depth]], 0)
    out = dot(both, weight[...])
    total[...] = out
    short[...] = out.astype(BF16)


def pack_body(picks, experts, own, other, kept, total, *rest):
    *parts, packed, mine, lent = rest
    rows = own.shape[0]
    half = total.shape[1]
    mixed = total[...]
    for part in parts:
        mixed = mixed + part[...].astype(F32)
    width = own.shape[1] - half - LANES
    mixed_own = mixed[:rows] + kept[...].astype(F32)
    mixed_other = mixed[rows:] + other[:, width : width + half].astype(F32)
    mine[...] = mixed_own
    lent[...] = mixed_other
    mixed = jnp.concatenate([mixed_own, mixed_other], 0).astype(BF16)
    notes = jnp.concatenate([own[:, width + half :], other[:, width + half :]], 0).astype(F32)
    notes = notes.astype(jnp.int32)
    tail_width = packed.shape[1] - half
    tail_parts = half // tail_width
    tail_rows = SUBLANES // tail_parts
    column = iota((2 * rows, experts * SUBLANES), 1)
    picked = [jnp.zeros(column.shape, F32) for _ in range(1 + tail_parts)]
    for j in range(picks):
        expert = notes[:, j : j + 1]
        slot = notes[:, picks + j : picks + j + 1]
        start = expert * SUBLANES
        picked[0] = picked[0] + ((column == start + slot) & (slot < SUBLANES)).astype(F32)
        for p in range(tail_parts):
            picked[1 + p] = picked[1 + p] + (
                (column == start + slot - SUBLANES + p * tail_rows) & (slot >= SUBLANES)
            ).astype(F32)
    picked = [jnp.transpose(p).astype(BF16) for p in picked]
    packed[:, :half] = dot(picked[0], mixed).astype(BF16)
    tail = dot(picked[1], mixed[:, :tail_width])
    for p in range(1, tail_parts):
        tail = tail + dot(picked[1 + p], mixed[:, p * tail_width : (p + 1) * tail_width])
    packed[:, half:] = tail.astype(BF16)


def hidden_body(half, arrived, gain, gate_up, hidden, rows_ref):
    sources = arrived.shape[0] // SUBLANES
    chips = sources // 2
    tail_width = arrived.shape[1] - half
    tail_parts = half // tail_width
    tail_rows = SUBLANES // tail_parts
    value = arrived[...].astype(F32)
    for chip in range(chips):
        for deep in range(2):
            at = (chip * 2 + deep) * SUBLANES
            rows_ref[chip * SUBLANES : (chip + 1) * SUBLANES, deep * half : (deep + 1) * half] = (
                value[at : at + SUBLANES, :half]
            )
    row_part = lax.div(iota((SUBLANES, tail_width), 0), tail_rows)
    for first in range(0, chips, tail_parts):
        to = chips * SUBLANES + first * tail_rows
        for deep in range(2):
            for p in range(tail_parts):
                joined = None
                for c in range(tail_parts):
                    at = ((first + c) * 2 + deep) * SUBLANES
                    piece = value[at : at + SUBLANES, half:]
                    shift = (c - p) * tail_rows % SUBLANES
                    if shift:
                        piece = pltpu.roll(piece, shift, 0)
                    joined = piece if joined is None else jnp.where(row_part == c, piece, joined)
                left = deep * half + p * tail_width
                rows_ref[to : to + SUBLANES, left : left + tail_width] = joined
    rows = rows_ref[...]
    scale = lax.rsqrt(jnp.mean(rows * rows, -1, keepdims=True) + 1e-06)
    normed = (rows * scale * gain[...]).astype(BF16)
    gate = dot_t(normed, gate_up[0])
    up = dot_t(normed, gate_up[1])
    hidden[...] = (gate / (1.0 + jnp.exp(-gate)) * up).astype(BF16)


def down_body(capacity, place, *rest):
    *pieces, weight, out = rest
    count = len(pieces)
    narrow = place[1]
    depth = pieces[0].shape[1]
    rows = pieces[0].shape[0]
    chips = out.shape[0] // (2 * SUBLANES)
    shape = (out.shape[0], rows)
    row = iota(shape, 0)
    chip = lax.div(row, 2 * SUBLANES)
    source = lax.rem(lax.div(row, SUBLANES), 2)
    slot = lax.rem(row, SUBLANES)
    full = source * capacity + slot
    tail_rows = 2 * capacity - SUBLANES
    column = jnp.where(
        full < SUBLANES, chip * SUBLANES + full, (chips + 0) * SUBLANES + chip * tail_rows + full - SUBLANES
    )
    order = ((column == iota(shape, 1)) & (slot < capacity)).astype(BF16)
    total = None
    for step in range(count):
        owner = lax.rem(narrow + count - step, count)
        piece = dot(order, pieces[step][...]).astype(BF16)
        term = dot(piece, weight[pl.ds(pl.multiple_of(owner * depth, LANES), depth), :])
        total = term if total is None else total + term
    out[...] = total.astype(BF16)


def combine_body(capacity, per_half, place, returned, own, mine, borrowed, router, out):
    rows, share = out.shape
    picks = router.shape[1]
    deep, narrow = place[0], place[1]
    notes = own[:, own.shape[1] - LANES :].astype(F32).astype(jnp.int32)
    weights = router[...]
    weights = weights / jnp.sum(weights, -1, keepdims=True)
    column = iota((rows, returned.shape[0]), 1)
    left = pl.multiple_of(lax.rem(narrow, per_half) * share, LANES)
    here = lax.div(narrow, per_half) == deep
    total = jnp.where(here, mine[:, pl.ds(left, share)], borrowed[:, pl.ds(left, share)])
    value = returned[...]
    for j in range(picks):
        target = notes[:, j : j + 1] * SUBLANES + notes[:, picks + j : picks + j + 1] - deep * capacity
        chosen = dot((column == target).astype(BF16), value)
        total = total + chosen * weights[:, j : j + 1]
    out[...] = total.astype(BF16)


def shards(
    queries,
    cache_keys,
    cache_values,
    fresh_pairs,
    lengths,
    residual,
    norm_gain,
    output_weight,
    expert_gate_up,
    expert_down,
    routed_experts,
    router_weights,
):
    rows, full_width = residual.shape
    head_width, half = output_weight.shape
    narrow_count = lax.axis_size("narrow")
    wide_count = lax.axis_size("wide")
    share = full_width // narrow_count
    picks = routed_experts.shape[1]
    capacity = rows // 4
    experts = wide_count * 2
    tail_rows = 2 * capacity - SUBLANES
    assert lax.axis_size("deep") == 2 and half % share == 0 and half * 2 == full_width
    assert rows % SUBLANES == 0 and SUBLANES % tail_rows == 0 and capacity <= SUBLANES
    assert wide_count % (SUBLANES // tail_rows) == 0 and 2 * picks <= LANES and experts <= LANES
    packed_width = half + half * tail_rows // SUBLANES
    row_slots = wide_count * 2 * capacity
    place = jnp.stack([lax.axis_index("deep"), lax.axis_index("narrow")]).astype(jnp.int32)
    sds = jax.ShapeDtypeStruct

    ext, kept = call(
        functools.partial(attention_body, capacity, experts),
        [sds((rows, head_width + half + LANES), BF16), sds((rows, half), BF16)],
        [
            place,
            queries,
            cache_keys,
            cache_values,
            fresh_pairs,
            lengths[:, None],
            residual,
            routed_experts,
        ],
        [SMEM] + [VMEM] * 7,
    )
    other = swap(ext, "deep")
    total, short = call(
        project_body,
        [sds((2 * rows, half), F32), sds((2 * rows, half), BF16)],
        [ext, other, pltpu.with_memory_space_constraint(output_weight, pltpu.VMEM)],
        flops=4 * rows * head_width * half,
    )
    parts = from_others(short, "narrow")
    packed, mine, lent = call(
        functools.partial(pack_body, picks, experts),
        [
            sds((experts * SUBLANES, packed_width), BF16),
            sds((rows, half), F32),
            sds((rows, half), F32),
        ],
        [ext, other, kept, total, *parts],
    )
    borrowed = swap(lent, "deep")
    arrived = lax.all_to_all(
        packed.reshape(experts, SUBLANES, packed_width),
        ("wide", "deep"),
        split_axis=0,
        concat_axis=0,
        tiled=True,
    ).reshape(experts * SUBLANES, packed_width)
    gate_up = pltpu.with_memory_space_constraint(expert_gate_up[0], pltpu.VMEM)
    hidden_width = gate_up.shape[1]
    outs = [sds((row_slots, hidden_width), BF16)]
    operands = [arrived, norm_gain[None, :], gate_up]
    hidden = pl.pallas_call(
        functools.partial(hidden_body, half),
        out_shape=outs,
        in_specs=[VMEM] * 3,
        out_specs=[VMEM],
        scratch_shapes=[pltpu.VMEM((row_slots, full_width), F32)],
        compiler_params=pltpu.CompilerParams(vmem_limit_bytes=40 << 20),
        cost_estimate=pl.CostEstimate(
            flops=4 * row_slots * hidden_width * full_width,
            bytes_accessed=4 * hidden_width * full_width,
            transcendentals=0,
        ),
    )(*operands)[0]
    pieces = [hidden, *from_others(hidden, "narrow")]
    (expert_rows,) = call(
        functools.partial(down_body, capacity),
        [sds((experts * SUBLANES, share), BF16)],
        [place, *pieces, pltpu.with_memory_space_constraint(expert_down[0], pltpu.VMEM)],
        [SMEM] + [VMEM] * (len(pieces) + 1),
        flops=2 * row_slots * share * hidden_width * narrow_count,
    )
    returned = lax.all_to_all(
        expert_rows.reshape(experts, SUBLANES, share),
        ("wide", "deep"),
        split_axis=0,
        concat_axis=0,
        tiled=True,
    ).reshape(experts * SUBLANES, share)
    (out,) = call(
        functools.partial(combine_body, capacity, half // share),
        [sds((rows, share), BF16)],
        [place, returned, ext, mine, borrowed, router_weights],
        [SMEM] + [VMEM] * 5,
    )
    return out


def solution(mesh):
    in_specs = (
        P(("group", "wide", "deep"), "narrow"),
        P(("group", "wide", "deep"), "narrow", None, None),
        P(("group", "wide", "deep"), "narrow", None, None),
        P(("group", "wide", "deep"), None, "narrow"),
        P(("group", "wide", "deep")),
        P(("group", "wide", "deep"), None),
        P(),
        P("narrow", "deep"),
        P(("wide", "deep"), None, "narrow", None),
        P(("wide", "deep"), None, "narrow"),
        P(("group", "wide", "deep"), None),
        P(("group", "wide", "deep"), None),
    )
    out_specs = P(("group", "wide", "deep"), "narrow")
    return jax.shard_map(shards, mesh=mesh, in_specs=in_specs, out_specs=out_specs, check_vma=False)
```

time: 82.9 us -> 51.9 us (0.63)
  between operations: 13.6 us -> 0.05 us
  waiting for transfers between devices: 25.9 us -> 12.8 us
  Pallas kernels: 0 us -> 8.2 us
  blocking collectives: 20.8 us -> 13.2 us
  matrix products: 6.37 us -> 0 us
  local copies, waits for them, and re-layouts: 4.57 us -> 8.27 us
  other arithmetic: 3.07 us -> 0.07 us
    reduce_scatter x1 -> x0, waiting for transfers between devices: 12.5 us -> none  [shards(): lax.psum_scatter(partial_value.astype(jnp.bfloat16), 'narrow', scatter_di...]
    all_gather x3 -> x0, blocking collectives: 12.1 us -> none  [the longest x1 5.42 us: shards(): lax.all_gather(incoming, 'narrow', axis=1, tiled=True)]
    all_to_all x1, blocking collectives: 3.79 us -> 13.2 us  [shards(): lax.all_to_all(packed.reshape(experts, SUBLANES, packed_width), ('wide',...]
    pallas_call x0 -> x6, Pallas kernels: none -> 8.2 us  [the longest x5 7.11 us: call(): pl.pallas_call(body, out_shape=outs, in_specs=in_specs or [VMEM] * len(op...]
    all_to_all x2 -> x1, waiting for transfers between devices: 13.4 us -> 5.26 us  [shards(): lax.all_to_all(expert_rows.reshape(experts, SUBLANES, share), ('wide', 'd...]
    ppermute x0 -> x4, waiting for transfers between devices: none -> 7.52 us  [the longest x2 5.57 us: from_others(): lax.ppermute(value, axis, [(i, (i + step) % size) for i in range(size)])]
    unnamed x18 -> x22, local copies, waits for them, and re-layouts: 1.13 us -> 7.53 us
    dot_general x7 -> x0, matrix products: 6.37 us -> none  [the longest x1 1.57 us: shards(): jnp.einsum('rkgd,rkld->rkgl', query_heads, cache_keys, preferred_element_...]
  transfers between devices with their start and end apart: 3 -> 5, of which waited for: 3 -> 5; matrix products, arithmetic and copies ran while one was open for 0% -> 0% of each run, Pallas kernels for 0% -> 0%
where the time goes in v2:
time: 51.9 us; the launch traced here: 51.4 us
  blocking collectives  13.2 us (25%)
  waiting for transfers between devices  12.8 us (25%)
  starting transfers between devices  8.76 us (17%)
  local copies, waits for them, and re-layouts  8.27 us (16%)
  Pallas kernels  8.2 us (16%)
    all_to_all x1, blocking collectives, shards(): lax.all_to_all(packed.reshape(experts, SUBLANES, packed_width), ('wide',...  13.2 us
    unnamed x22, local copies, waits for them, and re-layouts  7.53 us
    pallas_call x5, Pallas kernels, call(): pl.pallas_call(body, out_shape=outs, in_specs=in_specs or [VMEM] * len(op...  7.11 us
    ppermute x2, waiting for transfers between devices, from_others(): lax.ppermute(value, axis, [(i, (i + step) % size) for i in range(size)])  5.57 us
    all_to_all x1, waiting for transfers between devices, shards(): lax.all_to_all(expert_rows.reshape(experts, SUBLANES, share), ('wide', 'd...  5.26 us
    ppermute x2, starting transfers between devices, from_others(): lax.ppermute(value, axis, [(i, (i + step) % size) for i in range(size)])  4.47 us
    all_to_all x1, starting transfers between devices, shards(): lax.all_to_all(expert_rows.reshape(experts, SUBLANES, share), ('wide', 'd...  3.37 us
    ppermute x2, waiting for transfers between devices, swap(): return lax.ppermute(value, axis, [(0, 1), (1, 0)])  1.95 us
  transfers between devices with their start and end apart: 5, of which 5 were waited for; matrix products, arithmetic and copies ran while one was open for 0% of the time, Pallas kernels for 0%

profile of v2, /device:TPU:0, one launch (start us, length us, event | category | flops | bytes accessed | tf_op | source)
XLA Modules:
  0.0 51.4 jit_solution(13141103821845119140)
XLA Ops:
  0.0 0.7 %copy.13.lengths = s32[24,1]{1,0:T(8,128)S(1)} copy(s32[24,1]{0,1:T(1,128)} %bitcast.16) | data formatting | bytes 192 | tf_op jit(solution)/shard_map/broadcast_in_dim | solution.py:285
  0.7 0.7 %copy.14.routed = s32[24,1]{1,0:T(8,128)S(1)} copy(s32[24,1]{0,1:T(1,128)} %param.22) | data formatting | bytes 192 | tf_op args[10]
  1.5 0.1 pad_add_fusion.place
  1.5 1.0 %copy-done.3 = bf16[24,2,32,128]{3,2,1,0:T(8,128)(2,1)S(1)} copy-done((bf16[24,2,32,128]{3,2,1,0:T(8,128)(2,1)S(1)}, bf16[24,2,32,128]{3,2,1,0:T(8,128)(2,1)}, u32[]{:S(2)}) %copy-start.3) | copy-done | bytes 393240
  2.5 1.0 %copy-done.4 = bf16[24,2,32,128]{3,2,1,0:T(8,128)(2,1)S(1)} copy-done((bf16[24,2,32,128]{3,2,1,0:T(8,128)(2,1)S(1)}, bf16[24,2,32,128]{3,2,1,0:T(8,128)(2,1)}, u32[]{:S(2)}) %copy-start.4) | copy-done | bytes 393240
  3.5 0.9 %copy-done.5 = bf16[24,2048]{1,0:T(8,128)(2,1)S(1)} copy-done((bf16[24,2048]{1,0:T(8,128)(2,1)S(1)}, bf16[24,2048]{1,0:T(8,128)(2,1)}, u32[]{:S(2)}) %copy-start.5) | copy-done | bytes 98328
  4.4 0.9 %copy-done.6 = bf16[24,2048]{1,0:T(8,128)(2,1)S(1)} copy-done((bf16[24,2048]{1,0:T(8,128)(2,1)S(1)}, bf16[24,2048]{1,0:T(8,128)(2,1)}, u32[]{:S(2)}) %copy-start.6) | copy-done | bytes 98328
  5.3 0.7 %copy-done.7 = bf16[24,2,256]{2,1,0:T(2,128)(2,1)S(1)} copy-done((bf16[24,2,256]{2,1,0:T(2,128)(2,1)S(1)}, bf16[24,2,256]{2,1,0:T(2,128)(2,1)}, u32[]{:S(2)}) %copy-start.7) | copy-done | bytes 24600
  6.1 2.7 %shard_map.118 = (bf16[24,3200]{1,0:T(8,128)(2,1)S(1)}, bf16[24,1024]{1,0:T(8,128)(2,1)S(1)}) custom-call(s32[2]{0:T(128)S(1)} %pad_add_fusion.place, bf16[24,2048]{1,0:T(8,128)(2,1)S(1)} %copy-done.5, bf16[24,2,32,128]{3,2,1,0:T(8,128)(2,1)S(1)} %copy-done.3, bf16[24,2,32,128]{3,2,1,0:T(8,128)(2,1)S(1)} %copy-done.4, bf16[24,2,256]{2,1,0:T(2,128)(2,1)S(1)} %copy-done.7, ...), custom_call_target="tpu_custom_call" | custom-call | bytes 1210568 | tf_op jit(solution)/shard_map/pallas_call | solution.py:33
  8.8 0.5 %collective-permute-start = (bf16[24,3200]{1,0:T(8,128)(2,1)S(1)}, bf16[24,3200]{1,0:T(8,128)(2,1)S(1)}, u32[]{:S(2)}, u32[]{:S(2)}) collective-permute-start(bf16[24,3200]{1,0:T(8,128)(2,1)S(1)} %get-tuple-element.12.own), channel_id=1, source_target_pairs={{0,1},{1,0},{2,3},{3,2},{4,5},{5,4},{6,7},{7,6},{8,9},{9,8},{10,11... | collective-permute-start | bytes 460808 | tf_op jit(solution)/shard_map/ppermute | solution.py:52
  9.3 1.0 %collective-permute-done.other = bf16[24,3200]{1,0:T(8,128)(2,1)S(1)} collective-permute-done((bf16[24,3200]{1,0:T(8,128)(2,1)S(1)}, bf16[24,3200]{1,0:T(8,128)(2,1)S(1)}, u32[]{:S(2)}, u32[]{:S(2)}) %collective-permute-start) | collective-permute-done | bytes 153632 | tf_op jit(solution)/shard_map/ppermute | solution.py:52
  10.3 2.2 %copy-done = bf16[2048,1024]{1,0:T(8,128)(2,1)S(1)} copy-done((bf16[2048,1024]{1,0:T(8,128)(2,1)S(1)}, bf16[2048,1024]{1,0:T(8,128)(2,1)}, u32[]{:S(2)}) %copy-start) | copy-done | bytes 4194328
  12.5 0.8 %shard_map.119 = (f32[48,1024]{1,0:T(8,128)S(1)}, bf16[48,1024]{1,0:T(8,128)(2,1)S(1)}) custom-call(bf16[24,3200]{1,0:T(8,128)(2,1)S(1)} %get-tuple-element.12.own, bf16[24,3200]{1,0:T(8,128)(2,1)S(1)} %collective-permute-done.other, bf16[2048,1024]{1,0:T(8,128)(2,1)S(1)} %copy-done), custom_call_target="tpu_custom_call" | custom-call | flops 201326592 | bytes 4796416 | tf_op jit(solution)/shard_map/pallas_call | solution.py:33
  13.3 0.0 copy-start.2
  13.3 2.9 %collective-permute-start.1 = (bf16[48,1024]{1,0:T(8,128)(2,1)S(1)}, bf16[48,1024]{1,0:T(8,128)(2,1)S(1)}, u32[]{:S(2)}, u32[]{:S(2)}) collective-permute-start(bf16[48,1024]{1,0:T(8,128)(2,1)S(1)} %get-tuple-element.15), channel_id=1, source_target_pairs={{0,2},{2,0},{1,3},{3,1},{4,6},{6,4},{5,7},{7,5},{8,10},{10,8},{9,1... | collective-permute-start | bytes 294920 | tf_op jit(solution)/shard_map/ppermute | solution.py:46
  16.3 3.1 %collective-permute-done.1.rest_0_ = bf16[48,1024]{1,0:T(8,128)(2,1)S(1)} collective-permute-done((bf16[48,1024]{1,0:T(8,128)(2,1)S(1)}, bf16[48,1024]{1,0:T(8,128)(2,1)S(1)}, u32[]{:S(2)}, u32[]{:S(2)}) %collective-permute-start.1) | collective-permute-done | bytes 98336 | tf_op jit(solution)/shard_map/ppermute | solution.py:46
  19.4 0.4 shard_map.120
  19.8 13.2 %all_to_all.10 = bf16[8,8,1536]{2,1,0:T(8,128)(2,1)S(1)} all-to-all(bf16[8,8,1536]{2,1,0:T(8,128)(2,1)S(1)} %bitcast.14), channel_id=1, replica_groups=mesh['group'=2,'wide'=4,'narrow'=2,'deep'=2] {'wide','deep'}, dimensions={0} | all-to-all | bytes 393216 | tf_op jit(solution)/shard_map/all_to_all | solution.py:309
  33.0 0.0 copy-done.8
  33.0 0.0 copy-done.1
  33.0 1.1 %shard_map.121.rest_0_ = bf16[48,384]{1,0:T(8,128)(2,1)S(1)} custom-call(bf16[64,1536]{1,0:T(8,128)(2,1)S(1)} %bitcast.12, f32[1,2048]{1,0:T(1,128)S(1)} %bitcast.15, bf16[2,384,2048]{2,1,0:T(8,128)(2,1)S(1)} %bitcast.10), custom_call_target="tpu_custom_call" | custom-call | flops 150994944 | bytes 3145728 | tf_op jit(solution)/shard_map/pallas_call | solution.py:320
  34.1 1.6 %collective-permute-start.2 = (bf16[48,384]{1,0:T(8,128)(2,1)S(1)}, bf16[48,384]{1,0:T(8,128)(2,1)S(1)}, u32[]{:S(2)}, u32[]{:S(2)}) collective-permute-start(bf16[48,384]{1,0:T(8,128)(2,1)S(1)} %shard_map.121.rest_0_), channel_id=1, source_target_pairs={{0,2},{2,0},{1,3},{3,1},{4,6},{6,4},{5,7},{7,5},{8,10},{10,8},{9,1... | collective-permute-start | bytes 110600 | tf_op jit(solution)/shard_map/ppermute | solution.py:46
  35.7 2.5 %collective-permute-done.2.rest_1_ = bf16[48,384]{1,0:T(8,128)(2,1)S(1)} collective-permute-done((bf16[48,384]{1,0:T(8,128)(2,1)S(1)}, bf16[48,384]{1,0:T(8,128)(2,1)S(1)}, u32[]{:S(2)}, u32[]{:S(2)}) %collective-permute-start.2) | collective-permute-done | bytes 36896 | tf_op jit(solution)/shard_map/ppermute | solution.py:46
  38.1 0.0 copy-done.2
  38.1 1.7 %shard_map.122 = bf16[64,1024]{1,0:T(8,128)(2,1)} custom-call(s32[2]{0:T(128)S(1)} %pad_add_fusion.place, bf16[48,384]{1,0:T(8,128)(2,1)S(1)} %shard_map.121.rest_0_, bf16[48,384]{1,0:T(8,128)(2,1)S(1)} %collective-permute-done.2.rest_1_, bf16[768,1024]{1,0:T(8,128)(2,1)S(1)} %bitcast.11), custom_call_target="tpu_custom_call" | custom-call | flops 75497472 | bytes 1777672 | tf_op jit(solution)/shard_map/pallas_call | solution.py:33
  39.9 3.4 %all-to-all-start.1 = ((bf16[8,8,1024]{2,1,0:T(8,128)(2,1)}), bf16[8,8,1024]{2,1,0:T(8,128)(2,1)S(1)}, u32[]{:S(2)}, u32[]{:S(2)}) async-start(bf16[8,8,1024]{2,1,0:T(8,128)(2,1)} %bitcast.8), calls=%async_computation.1 | async-start | bytes 262144 | tf_op jit(solution)/shard_map/all_to_all | solution.py:341
  43.2 0.4 collective-permute-start.3
  43.6 0.0 copy-done.9
  43.6 0.1 copy.15.router
  43.7 0.9 %collective-permute-done.3.borrowed = f32[24,1024]{1,0:T(8,128)S(1)} collective-permute-done((f32[24,1024]{1,0:T(8,128)S(1)}, f32[24,1024]{1,0:T(8,128)S(1)}, u32[]{:S(2)}, u32[]{:S(2)}) %collective-permute-start.3) | collective-permute-done | bytes 98336 | tf_op jit(solution)/shard_map/ppermute | solution.py:52
  44.7 5.3 %all-to-all-done.1 = bf16[8,8,1024]{2,1,0:T(8,128)(2,1)S(1)} async-done(((bf16[8,8,1024]{2,1,0:T(8,128)(2,1)}), bf16[8,8,1024]{2,1,0:T(8,128)(2,1)S(1)}, u32[]{:S(2)}, u32[]{:S(2)}) %all-to-all-start.1) | async-done | bytes 131104 | tf_op jit(solution)/shard_map/all_to_all | solution.py:341
  49.9 1.4 %shard_map.123 = bf16[24,1024]{1,0:T(8,128)(2,1)} custom-call(s32[2]{0:T(128)S(1)} %pad_add_fusion.place, bf16[64,1024]{1,0:T(8,128)(2,1)S(1)} %bitcast.13, bf16[24,3200]{1,0:T(8,128)(2,1)S(1)} %get-tuple-element.12.own, f32[24,1024]{1,0:T(8,128)S(1)} %get-tuple-element.17.mine, f32[24,1024]{1,0:T(8,128)S(1)} %collective-permute-done.3.borrowed, ...), custom_call_target="tpu_custom_call" | custom-call | bytes 530536 | tf_op jit(solution)/shard_map/pallas_call | solution.py:33
  (9 shorter events, 0.0 us)
Async XLA Ops:
  1.5 1.0 %copy-start.3 = (bf16[24,2,32,128]{3,2,1,0:T(8,128)(2,1)S(1)}, bf16[24,2,32,128]{3,2,1,0:T(8,128)(2,1)}, u32[]{:S(2)}) copy-start(bf16[24,2,32,128]{3,2,1,0:T(8,128)(2,1)} %k.1) | copy-start | bytes 1179652
  2.5 1.0 %copy-start.4 = (bf16[24,2,32,128]{3,2,1,0:T(8,128)(2,1)S(1)}, bf16[24,2,32,128]{3,2,1,0:T(8,128)(2,1)}, u32[]{:S(2)}) copy-start(bf16[24,2,32,128]{3,2,1,0:T(8,128)(2,1)} %v.1) | copy-start | bytes 1179652
  3.5 0.9 %copy-start.5 = (bf16[24,2048]{1,0:T(8,128)(2,1)S(1)}, bf16[24,2048]{1,0:T(8,128)(2,1)}, u32[]{:S(2)}) copy-start(bf16[24,2048]{1,0:T(8,128)(2,1)} %q.1) | copy-start | bytes 294916
  4.4 0.9 %copy-start.6 = (bf16[24,2048]{1,0:T(8,128)(2,1)S(1)}, bf16[24,2048]{1,0:T(8,128)(2,1)}, u32[]{:S(2)}) copy-start(bf16[24,2048]{1,0:T(8,128)(2,1)} %residual.1) | copy-start | bytes 294916
  5.3 0.7 %copy-start.7 = (bf16[24,2,256]{2,1,0:T(2,128)(2,1)S(1)}, bf16[24,2,256]{2,1,0:T(2,128)(2,1)}, u32[]{:S(2)}) copy-start(bf16[24,2,256]{2,1,0:T(2,128)(2,1)} %fresh.1) | copy-start | bytes 73732
  6.1 26.9 %copy-start.8 = (f32[2048]{0:T(1024)S(1)}, f32[2048]{0:T(1024)}, u32[]{:S(2)}) copy-start(f32[2048]{0:T(1024)} %param.18) | copy-start | bytes 24580
  8.8 1.5 %collective-permute-start = (bf16[24,3200]{1,0:T(8,128)(2,1)S(1)}, bf16[24,3200]{1,0:T(8,128)(2,1)S(1)}, u32[]{:S(2)}, u32[]{:S(2)}) collective-permute-start(bf16[24,3200]{1,0:T(8,128)(2,1)S(1)} %get-tuple-element.12.own), channel_id=1, source_target_pairs={{0,1},{1,0},{2,3},{3,2},{4,5},{5,4},{6,7},{7,6},{8,9},{9,8},{10,11... | collective-permute-start | bytes 460808 | tf_op jit(solution)/shard_map/ppermute | solution.py:52
  10.3 2.2 %copy-start = (bf16[2048,1024]{1,0:T(8,128)(2,1)S(1)}, bf16[2048,1024]{1,0:T(8,128)(2,1)}, u32[]{:S(2)}) copy-start(bf16[2048,1024]{1,0:T(8,128)(2,1)} %weight.1) | copy-start | bytes 12582916
  12.5 20.5 %copy-start.1 = (bf16[1,2,384,2048]{3,2,1,0:T(8,128)(2,1)S(1)}, bf16[1,2,384,2048]{3,2,1,0:T(8,128)(2,1)}, u32[]{:S(2)}) copy-start(bf16[1,2,384,2048]{3,2,1,0:T(8,128)(2,1)} %param.20) | copy-start | bytes 9437188
  13.3 24.8 %copy-start.2 = (bf16[1,768,1024]{2,1,0:T(8,128)(2,1)S(1)}, bf16[1,768,1024]{2,1,0:T(8,128)(2,1)}, u32[]{:S(2)}) copy-start(bf16[1,768,1024]{2,1,0:T(8,128)(2,1)} %param.21) | copy-start | bytes 4718596
  13.3 6.0 %collective-permute-start.1 = (bf16[48,1024]{1,0:T(8,128)(2,1)S(1)}, bf16[48,1024]{1,0:T(8,128)(2,1)S(1)}, u32[]{:S(2)}, u32[]{:S(2)}) collective-permute-start(bf16[48,1024]{1,0:T(8,128)(2,1)S(1)} %get-tuple-element.15), channel_id=1, source_target_pairs={{0,2},{2,0},{1,3},{3,1},{4,6},{6,4},{5,7},{7,5},{8,10},{10,8},{9,1... | collective-permute-start | bytes 294920 | tf_op jit(solution)/shard_map/ppermute | solution.py:46
  19.4 24.3 %copy-start.9 = (f32[24,1]{0,1:T(1,128)S(1)}, f32[24,1]{0,1:T(1,128)}, u32[]{:S(2)}) copy-start(f32[24,1]{0,1:T(1,128)} %param.23) | copy-start | bytes 292
  34.1 4.0 %collective-permute-start.2 = (bf16[48,384]{1,0:T(8,128)(2,1)S(1)}, bf16[48,384]{1,0:T(8,128)(2,1)S(1)}, u32[]{:S(2)}, u32[]{:S(2)}) collective-permute-start(bf16[48,384]{1,0:T(8,128)(2,1)S(1)} %shard_map.121.rest_0_), channel_id=1, source_target_pairs={{0,2},{2,0},{1,3},{3,1},{4,6},{6,4},{5,7},{7,5},{8,10},{10,8},{9,1... | collective-permute-start | bytes 110600 | tf_op jit(solution)/shard_map/ppermute | solution.py:46
  39.9 10.1 %all-to-all-start.1 = ((bf16[8,8,1024]{2,1,0:T(8,128)(2,1)}), bf16[8,8,1024]{2,1,0:T(8,128)(2,1)S(1)}, u32[]{:S(2)}, u32[]{:S(2)}) async-start(bf16[8,8,1024]{2,1,0:T(8,128)(2,1)} %bitcast.8), calls=%async_computation.1 | async-start | bytes 262144 | tf_op jit(solution)/shard_map/all_to_all | solution.py:341
  43.2 1.4 %collective-permute-start.3 = (f32[24,1024]{1,0:T(8,128)S(1)}, f32[24,1024]{1,0:T(8,128)S(1)}, u32[]{:S(2)}, u32[]{:S(2)}) collective-permute-start(f32[24,1024]{1,0:T(8,128)S(1)} %get-tuple-element.18), channel_id=1, source_target_pairs={{0,1},{1,0},{2,3},{3,2},{4,5},{5,4},{6,7},{7,6},{8,9},{9,8},{10,11... | collective-permute-start | bytes 294920 | tf_op jit(solution)/shard_map/ppermute | solution.py:52

commit v3 on v2

v3 whole, which is shorter than its diff:
```python
import functools
import math

import jax
import jax.numpy as jnp
from jax import lax
from jax.experimental import pallas as pl
from jax.experimental.pallas import tpu as pltpu
from jax.sharding import PartitionSpec as P

SUBLANES = 8
LANES = 128
F32 = jnp.float32
BF16 = jnp.bfloat16
VMEM = pl.BlockSpec(memory_space=pltpu.VMEM)
SMEM = pl.BlockSpec(memory_space=pltpu.SMEM)
HBM = pl.BlockSpec(memory_space=pltpu.HBM)


def iota(shape, axis):
    return lax.broadcasted_iota(jnp.int32, shape, axis)


def dot(a, b):
    return jnp.dot(a, b, preferred_element_type=F32)


def dot_t(a, b):
    return lax.dot_general(a, b, (((1,), (1,)), ((), ())), preferred_element_type=F32)


def call(body, outs, operands, in_specs=None, flops=0):
    size = sum(math.prod(o.shape) * o.dtype.itemsize for o in [*operands, *outs])
    return pl.pallas_call(
        body,
        out_shape=outs,
        in_specs=in_specs or [VMEM] * len(operands),
        out_specs=[VMEM] * len(outs),
        compiler_params=pltpu.CompilerParams(vmem_limit_bytes=min(size * 2 + (8 << 20), 48 << 20)),
        cost_estimate=pl.CostEstimate(flops=flops, bytes_accessed=size, transcendentals=0),
    )(*operands)


def from_others(value, axis):
    size = lax.axis_size(axis)
    return [
        lax.ppermute(value, axis, [(i, (i + step) % size) for i in range(size)])
        for step in range(1, size)
    ]


def swap(value, axis):
    return lax.ppermute(value, axis, [(0, 1), (1, 0)])


def attention_body(
    capacity, place, q, k, v, fresh, lengths, residual, routed, weight, ext, kept, loaded, *scratch
):
    q_here, k_here, v_here, fresh_here, lengths_here, residual_here, routed_here, sems = scratch
    rows, heads, length, size = k.shape
    width = q.shape[1]
    batches = [slice(i, i + SUBLANES) for i in range(0, rows, SUBLANES)]
    count = 0

    def start(source, target):
        nonlocal count
        copy = pltpu.make_async_copy(source, target, sems.at[count])
        copy.start()
        count += 1
        return copy

    early = [
        start(lengths, lengths_here),
        start(q, q_here),
        start(fresh, fresh_here),
    ]
    key_copies = [start(k.at[b], k_here.at[b]) for b in batches]
    value_copies = [start(v.at[b], v_here.at[b]) for b in batches]
    late = [start(routed, routed_here), start(residual, residual_here)]
    weight_copy = start(weight, loaded)

    group = width // (heads * size)
    scale = 1.0 / math.sqrt(size)
    many = SUBLANES * group
    shape = (many, SUBLANES * length)
    row_request = lax.rem(iota(shape, 0), SUBLANES)
    column = iota(shape, 1)
    same = row_request == lax.div(column, length)
    position = lax.rem(column, length)
    diagonal = iota((rows, rows), 0) == iota((rows, rows), 1)

    def as_column(line):
        return jnp.sum(jnp.where(diagonal, line.astype(F32), 0.0), -1, keepdims=True)

    for copy in early:
        copy.wait()
    limits = as_column(lengths_here[...]).astype(jnp.int32)
    q_all = q_here[...].astype(F32)
    units = [(b, head) for b in range(len(batches)) for head in range(heads)]
    scores, owns, own_values = [], [], []
    for b, head in units:
        if head == 0:
            key_copies[b].wait()
            limit = jnp.concatenate([limits[batches[b], :]] * group, 0)
            valid = same & (position < limit)
        at = head * group * size
        query = jnp.concatenate(
            [q_all[batches[b], at + g * size : at + (g + 1) * size] for g in range(group)], 0
        )
        own_key = fresh_here[batches[b], 0, head * size : (head + 1) * size].astype(F32)
        keys = k_here[batches[b], head].reshape(SUBLANES * length, size)
        scores.append(jnp.where(valid, dot_t(query.astype(BF16), keys) * scale, -1e30))
        owns.append(
            jnp.sum(query * jnp.concatenate([own_key] * group, 0), -1, keepdims=True) * scale
        )
    probs, own_probs = [], []
    for score, own in zip(scores, owns):
        top = jnp.maximum(jnp.max(score, -1, keepdims=True), own)
        raw = jnp.exp(score - top)
        own_raw = jnp.exp(own - top)
        inverse = 1.0 / (jnp.sum(raw, -1, keepdims=True) + own_raw)
        probs.append((raw * inverse).astype(BF16))
        own_probs.append((own_raw * inverse).astype(BF16).astype(F32))
    for (b, head), prob, own_prob in zip(units, probs, own_probs):
        if head == 0:
            value_copies[b].wait()
        at = head * group * size
        own_value = fresh_here[batches[b], 1, head * size : (head + 1) * size].astype(F32)
        values = v_here[batches[b], head].reshape(SUBLANES * length, size)
        out = dot(prob, values) + own_prob * jnp.concatenate([own_value] * group, 0)
        for g in range(group):
            ext[batches[b], at + g * size : at + (g + 1) * size] = out[
                g * SUBLANES : (g + 1) * SUBLANES
            ].astype(BF16)
    for copy in late:
        copy.wait()
    deep = place[0]
    half = kept.shape[1]
    kept[...] = residual_here[:, pl.ds(pl.multiple_of(deep * half, LANES), half)]
    ext[:, width : width + half] = residual_here[
        :, pl.ds(pl.multiple_of((1 - deep) * half, LANES), half)
    ]
    picks = routed.shape[0]
    lane = iota((rows, LANES), 1).astype(F32)
    chosen = [as_column(routed_here[j : j + 1, :]) for j in range(picks)]
    hits = jnp.zeros((rows, LANES), F32)
    for expert in chosen:
        hits = hits + (expert == lane).astype(F32)
    earlier = (iota((rows, rows), 1) < iota((rows, rows), 0)).astype(BF16)
    before = dot(earlier, hits.astype(BF16))
    notes = jnp.zeros((rows, LANES), F32)
    for j, expert in enumerate(chosen):
        slot = jnp.sum(jnp.where(expert == lane, before, 0.0), -1, keepdims=True)
        slot = slot + (deep * capacity).astype(F32)
        notes = jnp.where(lane == j, expert, notes)
        notes = jnp.where(lane == picks + j, slot, notes)
    ext[:, width + half :] = notes.astype(BF16)
    weight_copy.wait()


def project_body(own, other, weight, total, short):
    depth = weight.shape[0]
    both = jnp.concatenate([own[:, :depth], other[:, :depth]], 0)
    out = dot(both, weight[...])
    total[...] = out
    short[...] = out.astype(BF16)


def blocks_of(refs, count):
    if len(refs) == count:
        return list(refs)
    size = refs[0].shape[0] // count
    return [refs[0].at[pl.ds(i * size, size)] for i in range(count)]


def step_to(expert, wide, direct):
    chip = lax.shift_right_logical(expert, 1)
    return chip ^ wide if direct else chip


def pack_body(picks, chips, direct, place, own, other, kept, total, *rest):
    narrow_parts, (*packed, mine, lent) = rest[: -2 - packed_count(chips, direct)], rest[
        -2 - packed_count(chips, direct) :
    ]
    rows = own.shape[0]
    half = total.shape[1]
    mixed = total[...]
    for part in narrow_parts:
        mixed = mixed + part[...].astype(F32)
    width = own.shape[1] - half - LANES
    mixed_own = mixed[:rows] + kept[...].astype(F32)
    mixed_other = mixed[rows:] + other[:, width : width + half].astype(F32)
    mine[...] = mixed_own
    lent[...] = mixed_other
    mixed = jnp.concatenate([mixed_own, mixed_other], 0).astype(BF16)
    notes = jnp.concatenate([own[:, width + half :], other[:, width + half :]], 0).astype(F32)
    notes = notes.astype(jnp.int32)
    deep, wide = place[0], place[2]
    column = iota((2 * rows, chips * 3 * SUBLANES), 1)
    picked = jnp.zeros(column.shape, F32)
    for j in range(picks):
        expert = notes[:, j : j + 1]
        slot = notes[:, picks + j : picks + j + 1]
        across = (expert & 1) ^ deep
        at = jnp.where(
            slot < SUBLANES,
            across * SUBLANES + slot,
            2 * SUBLANES + across * (SUBLANES // 2) + slot - SUBLANES,
        )
        target = step_to(expert, wide, direct) * (3 * SUBLANES) + at
        picked = picked + (column == target).astype(F32)
    out = dot(jnp.transpose(picked).astype(BF16), mixed).astype(BF16)
    for i, block in enumerate(blocks_of(packed, chips)):
        block[...] = out[i * 3 * SUBLANES : (i + 1) * 3 * SUBLANES]


def packed_count(chips, direct):
    return chips if direct else 1


def tail_body(chips, *refs):
    *blocks, out = refs
    size = out.shape[0] // chips
    for i, block in enumerate(blocks_of(blocks, chips)):
        out[i * size : (i + 1) * size] = block[SUBLANES:]


def hidden_body(chips, place, *refs):
    *blocks, crossed, gain, gate_up, hidden, rows_ref = refs
    half = crossed.shape[1]
    edge = SUBLANES // 2
    deep = place[0]
    kept_at = pl.multiple_of(deep * half, LANES)
    crossed_at = pl.multiple_of((1 - deep) * half, LANES)
    kept = [block[...].astype(F32) for block in blocks_of(blocks, chips)]
    came = crossed[...].astype(F32)
    first = iota((SUBLANES, half), 0) < edge
    for i in range(chips):
        at = 2 * SUBLANES * i
        rows_ref[i * SUBLANES : (i + 1) * SUBLANES, pl.ds(kept_at, half)] = kept[i][:SUBLANES]
        rows_ref[i * SUBLANES : (i + 1) * SUBLANES, pl.ds(crossed_at, half)] = came[
            at : at + SUBLANES
        ]
    for i in range(0, chips, 2):
        to = chips * SUBLANES + i * edge
        at = 2 * SUBLANES * i
        rows_ref[to : to + SUBLANES, pl.ds(kept_at, half)] = jnp.where(
            first,
            kept[i][2 * SUBLANES :],
            pltpu.roll(kept[i + 1][2 * SUBLANES :], edge, 0),
        )
        rows_ref[to : to + SUBLANES, pl.ds(crossed_at, half)] = jnp.where(
            first,
            pltpu.roll(came[at + SUBLANES : at + 2 * SUBLANES], edge, 0),
            came[at + 3 * SUBLANES : at + 4 * SUBLANES],
        )
    rows = rows_ref[...]
    scale = lax.rsqrt(jnp.mean(rows * rows, -1, keepdims=True) + 1e-06)
    normed = (rows * scale * gain[...]).astype(BF16)
    gate = dot_t(normed, gate_up[0])
    up = dot_t(normed, gate_up[1])
    hidden[...] = (gate / (1.0 + jnp.exp(-gate)) * up).astype(BF16)


def down_body(capacity, chips, parts, place, *rest):
    pieces, weight, outs = rest[:parts], rest[parts], rest[parts + 1 :]
    deep, narrow = place[0], place[1]
    depth = pieces[0].shape[1]
    rows = pieces[0].shape[0]
    shape = (chips * 2 * SUBLANES, rows)
    row = iota(shape, 0)
    chip = lax.div(row, 2 * SUBLANES)
    source = lax.rem(lax.div(row, SUBLANES), 2) ^ deep
    slot = lax.rem(row, SUBLANES)
    full = source * capacity + slot
    column = jnp.where(
        full < SUBLANES,
        chip * SUBLANES + full,
        chips * SUBLANES + chip * (SUBLANES // 2) + full - SUBLANES,
    )
    order = ((column == iota(shape, 1)) & (slot < capacity)).astype(BF16)
    total = None
    for step in range(parts):
        owner = lax.rem(narrow + parts - step, parts)
        piece = dot(order, pieces[step][...]).astype(BF16)
        term = dot(piece, weight[pl.ds(pl.multiple_of(owner * depth, LANES), depth), :])
        total = term if total is None else total + term
    total = total.astype(BF16)
    for i, block in enumerate(blocks_of(outs, chips)):
        block[...] = total[i * 2 * SUBLANES : (i + 1) * 2 * SUBLANES]


def combine_body(capacity, per_half, chips, direct, place, *refs):
    *blocks, crossed, own, mine, borrowed, router, out = refs
    rows, share = out.shape
    picks = router.shape[0]
    deep, narrow, wide = place[0], place[1], place[2]
    notes = own[:, own.shape[1] - LANES :].astype(F32).astype(jnp.int32)
    diagonal = iota((rows, rows), 0) == iota((rows, rows), 1)
    lines = router[...]
    lines = lines / jnp.sum(lines, 0, keepdims=True)
    column = iota((rows, 2 * chips * SUBLANES), 1)
    left = pl.multiple_of(lax.rem(narrow, per_half) * share, LANES)
    here = lax.div(narrow, per_half) == deep
    total = jnp.where(here, mine[:, pl.ds(left, share)], borrowed[:, pl.ds(left, share)])
    value = jnp.concatenate(
        [block[:SUBLANES].astype(F32) for block in blocks_of(blocks, chips)]
        + [crossed[...].astype(F32)],
        0,
    ).astype(BF16)
    for j in range(picks):
        expert = notes[:, j : j + 1]
        slot = notes[:, picks + j : picks + j + 1] - deep * capacity
        across = (expert & 1) ^ deep
        target = (across * chips + step_to(expert, wide, direct)) * SUBLANES + slot
        weight = jnp.sum(jnp.where(diagonal, lines[j : j + 1, :], 0.0), -1, keepdims=True)
        total = total + dot((column == target).astype(BF16), value) * weight
    out[...] = total.astype(BF16)


def exchange(blocks, direct, chips, name):
    if not direct:
        (whole,) = blocks
        out = lax.all_to_all(
            whole.reshape(chips, -1, whole.shape[1]), "wide", split_axis=0, concat_axis=0, tiled=True
        )
        return [out.reshape(whole.shape)]
    out = [blocks[0]]
    for step in range(1, chips):
        with jax.named_scope(name + str(step)):
            out.append(lax.ppermute(blocks[step], "wide", [(i, i ^ step) for i in range(chips)]))
    return out


def shards(
    queries,
    cache_keys,
    cache_values,
    fresh_pairs,
    lengths,
    residual,
    norm_gain,
    output_weight,
    expert_gate_up,
    expert_down,
    routed_experts,
    router_weights,
):
    rows, full_width = residual.shape
    head_width, half = output_weight.shape
    narrow_count = lax.axis_size("narrow")
    wide_count = lax.axis_size("wide")
    share = full_width // narrow_count
    picks = routed_experts.shape[1]
    capacity = rows // 4
    experts = wide_count * 2
    assert lax.axis_size("deep") == 2 and half % share == 0 and half * 2 == full_width
    assert rows % SUBLANES == 0 and 2 * capacity - SUBLANES == SUBLANES // 2
    assert wide_count % 2 == 0 and 2 * picks <= LANES and experts <= LANES
    direct = wide_count <= 4 and wide_count & (wide_count - 1) == 0
    row_slots = wide_count * 2 * capacity
    place = jnp.stack([lax.axis_index(name) for name in ("deep", "narrow", "wide")])
    place = place.astype(jnp.int32)
    sds = jax.ShapeDtypeStruct

    def blocks_shape(tiles, width):
        if direct:
            return [sds((tiles * SUBLANES, width), BF16)] * wide_count
        return [sds((wide_count * tiles * SUBLANES, width), BF16)]

    sources = [
        queries,
        cache_keys,
        cache_values,
        fresh_pairs,
        lengths[None, :],
        residual,
        routed_experts.T,
    ]
    ext, kept, loaded = pl.pallas_call(
        functools.partial(attention_body, capacity),
        out_shape=[
            sds((rows, head_width + half + LANES), BF16),
            sds((rows, half), BF16),
            sds(output_weight.shape, BF16),
        ],
        in_specs=[SMEM] + [HBM] * (len(sources) + 1),
        out_specs=[VMEM] * 3,
        scratch_shapes=[pltpu.VMEM(x.shape, x.dtype) for x in sources]
        + [pltpu.SemaphoreType.DMA((2 * (rows // SUBLANES) + 6,))],
        compiler_params=pltpu.CompilerParams(vmem_limit_bytes=24 << 20),
        cost_estimate=pl.CostEstimate(flops=0, bytes_accessed=6 << 20, transcendentals=0),
    )(place, *sources, output_weight)
    other = swap(ext, "deep")
    total, short = call(
        project_body,
        [sds((2 * rows, half), F32), sds((2 * rows, half), BF16)],
        [ext, other, loaded],
        flops=4 * rows * head_width * half,
    )
    parts = from_others(short, "narrow")
    *packed, mine, lent = call(
        functools.partial(pack_body, picks, wide_count, direct),
        [*blocks_shape(3, half), sds((rows, half), F32), sds((rows, half), F32)],
        [place, ext, other, kept, total, *parts],
        [SMEM] + [VMEM] * (4 + len(parts)),
    )
    borrowed = swap(lent, "deep")
    arrived = exchange(packed, direct, wide_count, "send")
    (passing,) = call(
        functools.partial(tail_body, wide_count),
        [sds((wide_count * 2 * SUBLANES, half), BF16)],
        arrived,
    )
    crossed = swap(passing, "deep")
    gate_up = pltpu.with_memory_space_constraint(expert_gate_up[0], pltpu.VMEM)
    hidden_width = gate_up.shape[1]
    operands = [place, *arrived, crossed, norm_gain[None, :], gate_up]
    hidden = pl.pallas_call(
        functools.partial(hidden_body, wide_count),
        out_shape=[sds((row_slots, hidden_width), BF16)],
        in_specs=[SMEM] + [VMEM] * (len(operands) - 1),
        out_specs=[VMEM],
        scratch_shapes=[pltpu.VMEM((row_slots, full_width), F32)],
        compiler_params=pltpu.CompilerParams(vmem_limit_bytes=40 << 20),
        cost_estimate=pl.CostEstimate(
            flops=4 * row_slots * hidden_width * full_width,
            bytes_accessed=4 * hidden_width * full_width,
            transcendentals=0,
        ),
    )(*operands)[0]
    pieces = [hidden, *from_others(hidden, "narrow")]
    expert_rows = call(
        functools.partial(down_body, capacity, wide_count, len(pieces)),
        blocks_shape(2, share),
        [place, *pieces, pltpu.with_memory_space_constraint(expert_down[0], pltpu.VMEM)],
        [SMEM] + [VMEM] * (len(pieces) + 1),
        flops=2 * row_slots * share * hidden_width * narrow_count,
    )
    returned = exchange(expert_rows, direct, wide_count, "back")
    (passing,) = call(
        functools.partial(tail_body, wide_count),
        [sds((wide_count * SUBLANES, share), BF16)],
        returned,
    )
    crossed = swap(passing, "deep")
    (out,) = call(
        functools.partial(combine_body, capacity, half // share, wide_count, direct),
        [sds((rows, share), BF16)],
        [place, *returned, crossed, ext, mine, borrowed, router_weights.T],
        [SMEM] + [VMEM] * (len(returned) + 5),
    )
    return out


def solution(mesh):
    in_specs = (
        P(("group", "wide", "deep"), "narrow"),
        P(("group", "wide", "deep"), "narrow", None, None),
        P(("group", "wide", "deep"), "narrow", None, None),
        P(("group", "wide", "deep"), None, "narrow"),
        P(("group", "wide", "deep")),
        P(("group", "wide", "deep"), None),
        P(),
        P("narrow", "deep"),
        P(("wide", "deep"), None, "narrow", None),
        P(("wide", "deep"), None, "narrow"),
        P(("group", "wide", "deep"), None),
        P(("group", "wide", "deep"), None),
    )
    out_specs = P(("group", "wide", "deep"), "narrow")
    return jax.shard_map(shards, mesh=mesh, in_specs=in_specs, out_specs=out_specs, check_vma=False)
```

time: 51.9 us -> 50 us (0.963)
  blocking collectives: 13.2 us -> 0 us
  starting transfers between devices: 8.76 us -> 14 us
  waiting for transfers between devices: 12.8 us -> 17.6 us
  Pallas kernels: 8.2 us -> 9.89 us
    all_to_all x1 -> x0, blocking collectives: 13.2 us -> none  [shards(): lax.all_to_all(packed.reshape(experts, SUBLANES, packed_width), ('wide',...]
    ppermute x0 -> x6, starting transfers between devices: none -> 8.92 us  [exchange(): lax.ppermute(blocks[step], 'wide', [(i, i ^ step) for i in range(chips)])]
    ppermute x0 -> x6, waiting for transfers between devices: none -> 8.39 us  [exchange(): lax.ppermute(blocks[step], 'wide', [(i, i ^ step) for i in range(chips)])]
    all_to_all x1 -> x0, waiting for transfers between devices: 5.26 us -> none  [shards(): lax.all_to_all(expert_rows.reshape(experts, SUBLANES, share), ('wide', 'd...]
    pallas_call x1 -> x2, Pallas kernels: 1.09 us -> 5.45 us  [the longest x1 3.8 us: shards(): pl.pallas_call(functools.partial(attention_body, capacity), out_shape=[sd...]
    all_to_all x1 -> x0, starting transfers between devices: 3.37 us -> none  [shards(): lax.all_to_all(expert_rows.reshape(experts, SUBLANES, share), ('wide', 'd...]
    pallas_call x5 -> x6, Pallas kernels: 7.11 us -> 4.44 us  [call(): pl.pallas_call(body, out_shape=outs, in_specs=in_specs or [VMEM] * len(op...]
    ppermute x2 -> x4, waiting for transfers between devices: 1.95 us -> 3.59 us  [swap(): return lax.ppermute(value, axis, [(0, 1), (1, 0)])]
  transfers between devices with their start and end apart: 5 -> 12, of which waited for: 5 -> 9; matrix products, arithmetic and copies ran while one was open for 0% -> 0% of each run, Pallas kernels for 0% -> 0%
where the time goes in v3:
time: 50 us; the launch traced here: 49.7 us
  waiting for transfers between devices  17.6 us (35%)
  starting transfers between devices  14 us (28%)
  Pallas kernels  9.89 us (20%)
  local copies, waits for them, and re-layouts  8.03 us (16%)
    ppermute x6, starting transfers between devices, exchange(): lax.ppermute(blocks[step], 'wide', [(i, i ^ step) for i in range(chips)])  8.92 us
    ppermute x6, waiting for transfers between devices, exchange(): lax.ppermute(blocks[step], 'wide', [(i, i ^ step) for i in range(chips)])  8.39 us
    unnamed x24, local copies, waits for them, and re-layouts  8.03 us
    ppermute x2, waiting for transfers between devices, from_others(): lax.ppermute(value, axis, [(i, (i + step) % size) for i in range(size)])  5.57 us
    ppermute x2, starting transfers between devices, from_others(): lax.ppermute(value, axis, [(i, (i + step) % size) for i in range(size)])  4.45 us
    pallas_call x6, Pallas kernels, call(): pl.pallas_call(body, out_shape=outs, in_specs=in_specs or [VMEM] * len(op...  4.44 us
    pallas_call x1, Pallas kernels, shards(): pl.pallas_call(functools.partial(attention_body, capacity), out_shape=[sd...  3.8 us
    ppermute x4, waiting for transfers between devices, swap(): return lax.ppermute(value, axis, [(0, 1), (1, 0)])  3.59 us
  transfers between devices with their start and end apart: 12, of which 9 were waited for; matrix products, arithmetic and copies ran while one was open for 0% of the time, Pallas kernels for 0%

profile of v3, /device:TPU:0, one launch (start us, length us, event | category | flops | bytes accessed | tf_op | source)
XLA Modules:
  0.0 49.7 jit_solution(3889717587183313904)
XLA Ops:
  0.0 0.1 pad_add_fusion.place
  0.1 2.2 %copy-done = bf16[2048,1024]{1,0:T(8,128)(2,1)S(1)} copy-done((bf16[2048,1024]{1,0:T(8,128)(2,1)S(1)}, bf16[2048,1024]{1,0:T(8,128)(2,1)}, u32[]{:S(2)}) %copy-start) | copy-done | bytes 4194328
  2.3 1.0 %copy-done.3 = bf16[24,2,32,128]{3,2,1,0:T(8,128)(2,1)S(1)} copy-done((bf16[24,2,32,128]{3,2,1,0:T(8,128)(2,1)S(1)}, bf16[24,2,32,128]{3,2,1,0:T(8,128)(2,1)}, u32[]{:S(2)}) %copy-start.3) | copy-done | bytes 393240
  3.3 1.0 %copy-done.4 = bf16[24,2,32,128]{3,2,1,0:T(8,128)(2,1)S(1)} copy-done((bf16[24,2,32,128]{3,2,1,0:T(8,128)(2,1)S(1)}, bf16[24,2,32,128]{3,2,1,0:T(8,128)(2,1)}, u32[]{:S(2)}) %copy-start.4) | copy-done | bytes 393240
  4.3 0.9 %copy-done.5 = bf16[24,2048]{1,0:T(8,128)(2,1)S(1)} copy-done((bf16[24,2048]{1,0:T(8,128)(2,1)S(1)}, bf16[24,2048]{1,0:T(8,128)(2,1)}, u32[]{:S(2)}) %copy-start.5) | copy-done | bytes 98328
  5.2 0.9 %copy-done.6 = bf16[24,2048]{1,0:T(8,128)(2,1)S(1)} copy-done((bf16[24,2048]{1,0:T(8,128)(2,1)S(1)}, bf16[24,2048]{1,0:T(8,128)(2,1)}, u32[]{:S(2)}) %copy-start.6) | copy-done | bytes 98328
  6.0 0.7 %copy-done.7 = bf16[24,2,256]{2,1,0:T(2,128)(2,1)S(1)} copy-done((bf16[24,2,256]{2,1,0:T(2,128)(2,1)S(1)}, bf16[24,2,256]{2,1,0:T(2,128)(2,1)}, u32[]{:S(2)}) %copy-start.7) | copy-done | bytes 24600
  6.8 0.7 %copy-done.9 = s32[24]{0:T(128)S(1)} copy-done((s32[24]{0:T(128)S(1)}, s32[24]{0:T(128)}, u32[]{:S(2)}) %copy-start.9) | copy-done | bytes 120
  7.4 0.7 %copy-done.10 = s32[24,1]{0,1:T(1,128)S(1)} copy-done((s32[24,1]{0,1:T(1,128)S(1)}, s32[24,1]{0,1:T(1,128)}, u32[]{:S(2)}) %copy-start.10) | copy-done | bytes 120
  8.1 3.8 %shard_map.118 = (bf16[24,3200]{1,0:T(8,128)(2,1)S(1)}, bf16[24,1024]{1,0:T(8,128)(2,1)S(1)}, bf16[2048,1024]{1,0:T(8,128)(2,1)S(1)}) custom-call(s32[3]{0:T(128)S(1)} %pad_add_fusion.place, bf16[24,2048]{1,0:T(8,128)(2,1)S(1)} %copy-done.5, bf16[24,2,32,128]{3,2,1,0:T(8,128)(2,1)S(1)} %copy-done.3, bf16[24,2,32,128]{3,2,1,0:T(8,128)(2,1)S(1)} %copy-done.4, ...), custom_call_target="tpu_custom_call" | custom-call | bytes 6291456 | tf_op jit(solution)/shard_map/pallas_call | solution.py:380
  11.9 0.6 %collective-permute-start = (bf16[24,3200]{1,0:T(8,128)(2,1)S(1)}, bf16[24,3200]{1,0:T(8,128)(2,1)S(1)}, u32[]{:S(2)}, u32[]{:S(2)}) collective-permute-start(bf16[24,3200]{1,0:T(8,128)(2,1)S(1)} %get-tuple-element.20.own.refs_5_), channel_id=1, source_target_pairs={{0,1},{1,0},{2,3},{3,2},{4,5},{5,4},{6,7},{7,6},{8,9},{9,8},{10,11... | collective-permute-start | bytes 460808 | tf_op jit(solution)/shard_map/ppermute | solution.py:53
  12.5 1.0 %collective-permute-done.other = bf16[24,3200]{1,0:T(8,128)(2,1)S(1)} collective-permute-done((bf16[24,3200]{1,0:T(8,128)(2,1)S(1)}, bf16[24,3200]{1,0:T(8,128)(2,1)S(1)}, u32[]{:S(2)}, u32[]{:S(2)}) %collective-permute-start) | collective-permute-done | bytes 153632 | tf_op jit(solution)/shard_map/ppermute | solution.py:53
  13.5 0.8 %shard_map.119 = (f32[48,1024]{1,0:T(8,128)S(1)}, bf16[48,1024]{1,0:T(8,128)(2,1)S(1)}) custom-call(bf16[24,3200]{1,0:T(8,128)(2,1)S(1)} %get-tuple-element.20.own.refs_5_, bf16[24,3200]{1,0:T(8,128)(2,1)S(1)} %collective-permute-done.other, bf16[2048,1024]{1,0:T(8,128)(2,1)S(1)} %get-tuple-element.22.weight), custom_call_target="tpu_custom_call" | custom-call | flops 201326592 | bytes 4796416 | tf_op jit(solution)/shard_map/pallas_call | solution.py:34
  14.3 2.9 %collective-permute-start.1 = (bf16[48,1024]{1,0:T(8,128)(2,1)S(1)}, bf16[48,1024]{1,0:T(8,128)(2,1)S(1)}, u32[]{:S(2)}, u32[]{:S(2)}) collective-permute-start(bf16[48,1024]{1,0:T(8,128)(2,1)S(1)} %get-tuple-element.24), channel_id=1, source_target_pairs={{0,2},{2,0},{1,3},{3,1},{4,6},{6,4},{5,7},{7,5},{8,10},{10,8},{9,1... | collective-permute-start | bytes 294920 | tf_op jit(solution)/shard_map/ppermute | solution.py:47
  17.2 3.1 %collective-permute-done.1.rest_0_ = bf16[48,1024]{1,0:T(8,128)(2,1)S(1)} collective-permute-done((bf16[48,1024]{1,0:T(8,128)(2,1)S(1)}, bf16[48,1024]{1,0:T(8,128)(2,1)S(1)}, u32[]{:S(2)}, u32[]{:S(2)}) %collective-permute-start.1) | collective-permute-done | bytes 98336 | tf_op jit(solution)/shard_map/ppermute | solution.py:47
  20.3 1.1 %shard_map.120 = (bf16[24,1024]{1,0:T(8,128)(2,1)S(1)}, bf16[24,1024]{1,0:T(8,128)(2,1)S(1)}, bf16[24,1024]{1,0:T(8,128)(2,1)S(1)}, bf16[24,1024]{1,0:T(8,128)(2...) custom-call(s32[3]{0:T(128)S(1)} %pad_add_fusion.place, bf16[24,3200]{1,0:T(8,128)(2,1)S(1)} %get-tuple-element.20.own.refs_5_, ...), custom_call_target="tpu_custom_call" | custom-call | bytes 1044492 | tf_op jit(solution)/shard_map/pallas_call | solution.py:34
  21.4 1.9 %collective-permute-start.2 = (bf16[24,1024]{1,0:T(8,128)(2,1)S(1)}, bf16[24,1024]{1,0:T(8,128)(2,1)S(1)}, u32[]{:S(2)}, u32[]{:S(2)}) collective-permute-start(bf16[24,1024]{1,0:T(8,128)(2,1)S(1)} %get-tuple-element.26), channel_id=1, source_target_pairs={{0,4},{4,0},{8,12},{12,8},{1,5},{5,1},{9,13},{13,9},{2,6},{6,2},{1... | collective-permute-start | bytes 147464 | tf_op jit(solution)/shard_map/send1/ppermute | solution.py:331
  23.3 2.6 %collective-permute-start.3 = (bf16[24,1024]{1,0:T(8,128)(2,1)S(1)}, bf16[24,1024]{1,0:T(8,128)(2,1)S(1)}, u32[]{:S(2)}, u32[]{:S(2)}) collective-permute-start(bf16[24,1024]{1,0:T(8,128)(2,1)S(1)} %get-tuple-element.27), channel_id=1, source_target_pairs={{0,8},{4,12},{8,0},{12,4},{1,9},{5,13},{9,1},{13,5},{2,10},{6,14},... | collective-permute-start | bytes 147464 | tf_op jit(solution)/shard_map/send2/ppermute | solution.py:331
  25.9 2.9 %collective-permute-done.3.refs_2_ = bf16[24,1024]{1,0:T(8,128)(2,1)S(1)} collective-permute-done((bf16[24,1024]{1,0:T(8,128)(2,1)S(1)}, bf16[24,1024]{1,0:T(8,128)(2,1)S(1)}, u32[]{:S(2)}, u32[]{:S(2)}) %collective-permute-start.3) | collective-permute-done | bytes 49184 | tf_op jit(solution)/shard_map/send2/ppermute | solution.py:331
  28.8 3.0 %collective-permute-done.4.refs_3_ = bf16[24,1024]{1,0:T(8,128)(2,1)S(1)} collective-permute-done((bf16[24,1024]{1,0:T(8,128)(2,1)S(1)}, bf16[24,1024]{1,0:T(8,128)(2,1)S(1)}, u32[]{:S(2)}, u32[]{:S(2)}) %collective-permute-start.4) | collective-permute-done | bytes 49184 | tf_op jit(solution)/shard_map/send3/ppermute | solution.py:331
  31.8 0.1 collective-permute-start.5
  31.9 1.3 %collective-permute-done.5.refs_4_ = bf16[64,1024]{1,0:T(8,128)(2,1)S(1)} collective-permute-done((bf16[64,1024]{1,0:T(8,128)(2,1)S(1)}, bf16[64,1024]{1,0:T(8,128)(2,1)S(1)}, u32[]{:S(2)}, u32[]{:S(2)}) %collective-permute-start.5) | collective-permute-done | bytes 131104 | tf_op jit(solution)/shard_map/ppermute | solution.py:53
  33.2 1.6 %shard_map.122.rest_0_ = bf16[48,384]{1,0:T(8,128)(2,1)S(1)} custom-call(s32[3]{0:T(128)S(1)} %pad_add_fusion.place, bf16[24,1024]{1,0:T(8,128)(2,1)S(1)} %get-tuple-element.25.refs_0_, bf16[24,1024]{1,0:T(8,128)(2,1)S(1)} %collective-permute-done.2.refs_1_, bf16[24,1024]{1,0:T(8,128)(2,1)S(1)} %collective-permute-done.3.refs_2_, ...), custom_call_target="tpu_custom_call" | custom-call | flops 150994944 | bytes 3145728 | tf_op jit(solution)/shard_map/pallas_call | solution.py:419
  34.9 1.6 %collective-permute-start.6 = (bf16[48,384]{1,0:T(8,128)(2,1)S(1)}, bf16[48,384]{1,0:T(8,128)(2,1)S(1)}, u32[]{:S(2)}, u32[]{:S(2)}) collective-permute-start(bf16[48,384]{1,0:T(8,128)(2,1)S(1)} %shard_map.122.rest_0_), channel_id=1, source_target_pairs={{0,2},{2,0},{1,3},{3,1},{4,6},{6,4},{5,7},{7,5},{8,10},{10,8},{9,1... | collective-permute-start | bytes 110600 | tf_op jit(solution)/shard_map/ppermute | solution.py:47
  36.4 2.5 %collective-permute-done.6.rest_1_ = bf16[48,384]{1,0:T(8,128)(2,1)S(1)} collective-permute-done((bf16[48,384]{1,0:T(8,128)(2,1)S(1)}, bf16[48,384]{1,0:T(8,128)(2,1)S(1)}, u32[]{:S(2)}, u32[]{:S(2)}) %collective-permute-start.6) | collective-permute-done | bytes 36896 | tf_op jit(solution)/shard_map/ppermute | solution.py:47
  38.9 1.1 %shard_map.123 = (bf16[16,1024]{1,0:T(8,128)(2,1)S(1)}, bf16[16,1024]{1,0:T(8,128)(2,1)S(1)}, bf16[16,1024]{1,0:T(8,128)(2,1)S(1)}, bf16[16,1024]{1,0:T(8,128)(2,1)S(1)}) custom-call(s32[3]{0:T(128)S(1)} %pad_add_fusion.place, bf16[48,384]{1,0:T(8,128)(2,1)S(1)} %shard_map.122.rest_0_, bf16[48,384]{1,0:T(8,128)(2,1)S(1)} %collective-permute-done.6.rest_1_, ...), custom_call_target="tpu_custom_call" | custom-call | flops 75497472 | bytes 1777676 | tf_op jit(solution)/shard_map/pallas_call | solution.py:34
  40.1 1.2 %collective-permute-start.8 = (bf16[16,1024]{1,0:T(8,128)(2,1)S(1)}, bf16[16,1024]{1,0:T(8,128)(2,1)S(1)}, u32[]{:S(2)}, u32[]{:S(2)}) collective-permute-start(bf16[16,1024]{1,0:T(8,128)(2,1)S(1)} %get-tuple-element.31), channel_id=1, source_target_pairs={{0,8},{4,12},{8,0},{12,4},{1,9},{5,13},{9,1},{13,5},{2,10},{6,14},... | collective-permute-start | bytes 98312 | tf_op jit(solution)/shard_map/back2/ppermute | solution.py:331
  41.2 3.2 %collective-permute-start.9 = (bf16[16,1024]{1,0:T(8,128)(2,1)S(1)}, bf16[16,1024]{1,0:T(8,128)(2,1)S(1)}, u32[]{:S(2)}, u32[]{:S(2)}) collective-permute-start(bf16[16,1024]{1,0:T(8,128)(2,1)S(1)} %get-tuple-element.32), channel_id=1, source_target_pairs={{0,12},{4,8},{8,4},{12,0},{1,13},{5,9},{9,5},{13,1},{2,14},{6,10},... | collective-permute-start | bytes 98312 | tf_op jit(solution)/shard_map/back3/ppermute | solution.py:331
  44.4 0.5 %collective-permute-done.8.refs_2_ = bf16[16,1024]{1,0:T(8,128)(2,1)S(1)} collective-permute-done((bf16[16,1024]{1,0:T(8,128)(2,1)S(1)}, bf16[16,1024]{1,0:T(8,128)(2,1)S(1)}, u32[]{:S(2)}, u32[]{:S(2)}) %collective-permute-start.8) | collective-permute-done | bytes 32800 | tf_op jit(solution)/shard_map/back2/ppermute | solution.py:331
  44.9 2.0 %collective-permute-done.9.refs_3_ = bf16[16,1024]{1,0:T(8,128)(2,1)S(1)} collective-permute-done((bf16[16,1024]{1,0:T(8,128)(2,1)S(1)}, bf16[16,1024]{1,0:T(8,128)(2,1)S(1)}, u32[]{:S(2)}, u32[]{:S(2)}) %collective-permute-start.9) | collective-permute-done | bytes 32800 | tf_op jit(solution)/shard_map/back3/ppermute | solution.py:331
  47.0 1.2 %collective-permute-done.10.refs_4_ = bf16[32,1024]{1,0:T(8,128)(2,1)S(1)} collective-permute-done((bf16[32,1024]{1,0:T(8,128)(2,1)S(1)}, bf16[32,1024]{1,0:T(8,128)(2,1)S(1)}, u32[]{:S(2)}, u32[]{:S(2)}) %collective-permute-start.10) | collective-permute-done | bytes 65568 | tf_op jit(solution)/shard_map/ppermute | solution.py:53
  48.2 1.4 %shard_map.125 = bf16[24,1024]{1,0:T(8,128)(2,1)} custom-call(s32[3]{0:T(128)S(1)} %pad_add_fusion.place, bf16[16,1024]{1,0:T(8,128)(2,1)S(1)} %get-tuple-element.29.refs_0_, bf16[16,1024]{1,0:T(8,128)(2,1)S(1)} %collective-permute-done.7.refs_1_, bf16[16,1024]{1,0:T(8,128)(2,1)S(1)} %collective-permute-done.8.refs_2_, ...), custom_call_target="tpu_custom_call" | custom-call | bytes 596076 | tf_op jit(solution)/shard_map/pallas_call | solution.py:34
  (25 shorter events, 0.1 us)
Async XLA Ops:
  0.1 2.2 %copy-start = (bf16[2048,1024]{1,0:T(8,128)(2,1)S(1)}, bf16[2048,1024]{1,0:T(8,128)(2,1)}, u32[]{:S(2)}) copy-start(bf16[2048,1024]{1,0:T(8,128)(2,1)} %weight.1) | copy-start | bytes 12582916
  2.3 1.0 %copy-start.3 = (bf16[24,2,32,128]{3,2,1,0:T(8,128)(2,1)S(1)}, bf16[24,2,32,128]{3,2,1,0:T(8,128)(2,1)}, u32[]{:S(2)}) copy-start(bf16[24,2,32,128]{3,2,1,0:T(8,128)(2,1)} %k.1) | copy-start | bytes 1179652
  3.3 1.0 %copy-start.4 = (bf16[24,2,32,128]{3,2,1,0:T(8,128)(2,1)S(1)}, bf16[24,2,32,128]{3,2,1,0:T(8,128)(2,1)}, u32[]{:S(2)}) copy-start(bf16[24,2,32,128]{3,2,1,0:T(8,128)(2,1)} %v.1) | copy-start | bytes 1179652
  4.3 0.9 %copy-start.5 = (bf16[24,2048]{1,0:T(8,128)(2,1)S(1)}, bf16[24,2048]{1,0:T(8,128)(2,1)}, u32[]{:S(2)}) copy-start(bf16[24,2048]{1,0:T(8,128)(2,1)} %q.1) | copy-start | bytes 294916
  5.2 0.9 %copy-start.6 = (bf16[24,2048]{1,0:T(8,128)(2,1)S(1)}, bf16[24,2048]{1,0:T(8,128)(2,1)}, u32[]{:S(2)}) copy-start(bf16[24,2048]{1,0:T(8,128)(2,1)} %residual.1) | copy-start | bytes 294916
  6.0 0.7 %copy-start.7 = (bf16[24,2,256]{2,1,0:T(2,128)(2,1)S(1)}, bf16[24,2,256]{2,1,0:T(2,128)(2,1)}, u32[]{:S(2)}) copy-start(bf16[24,2,256]{2,1,0:T(2,128)(2,1)} %fresh.1) | copy-start | bytes 73732
  6.8 0.7 %copy-start.9 = (s32[24]{0:T(128)S(1)}, s32[24]{0:T(128)}, u32[]{:S(2)}) copy-start(s32[24]{0:T(128)} %param.16) | copy-start | bytes 292
  7.4 0.7 %copy-start.10 = (s32[24,1]{0,1:T(1,128)S(1)}, s32[24,1]{0,1:T(1,128)}, u32[]{:S(2)}) copy-start(s32[24,1]{0,1:T(1,128)} %param.22) | copy-start | bytes 292
  8.1 25.1 %copy-start.1 = (bf16[1,2,384,2048]{3,2,1,0:T(8,128)(2,1)S(1)}, bf16[1,2,384,2048]{3,2,1,0:T(8,128)(2,1)}, u32[]{:S(2)}) copy-start(bf16[1,2,384,2048]{3,2,1,0:T(8,128)(2,1)} %param.20) | copy-start | bytes 9437188
  8.1 25.1 %copy-start.8 = (f32[2048]{0:T(1024)S(1)}, f32[2048]{0:T(1024)}, u32[]{:S(2)}) copy-start(f32[2048]{0:T(1024)} %param.18) | copy-start | bytes 24580
  11.9 1.6 %collective-permute-start = (bf16[24,3200]{1,0:T(8,128)(2,1)S(1)}, bf16[24,3200]{1,0:T(8,128)(2,1)S(1)}, u32[]{:S(2)}, u32[]{:S(2)}) collective-permute-start(bf16[24,3200]{1,0:T(8,128)(2,1)S(1)} %get-tuple-element.20.own.refs_5_), channel_id=1, source_target_pairs={{0,1},{1,0},{2,3},{3,2},{4,5},{5,4},{6,7},{7,6},{8,9},{9,8},{10,11... | collective-permute-start | bytes 460808 | tf_op jit(solution)/shard_map/ppermute | solution.py:53
  13.5 25.4 %copy-start.2 = (bf16[1,768,1024]{2,1,0:T(8,128)(2,1)S(1)}, bf16[1,768,1024]{2,1,0:T(8,128)(2,1)}, u32[]{:S(2)}) copy-start(bf16[1,768,1024]{2,1,0:T(8,128)(2,1)} %param.21) | copy-start | bytes 4718596
  14.3 33.9 %copy-start.11 = (f32[24,1]{0,1:T(1,128)S(1)}, f32[24,1]{0,1:T(1,128)}, u32[]{:S(2)}) copy-start(f32[24,1]{0,1:T(1,128)} %param.23) | copy-start | bytes 292
  14.3 6.0 %collective-permute-start.1 = (bf16[48,1024]{1,0:T(8,128)(2,1)S(1)}, bf16[48,1024]{1,0:T(8,128)(2,1)S(1)}, u32[]{:S(2)}, u32[]{:S(2)}) collective-permute-start(bf16[48,1024]{1,0:T(8,128)(2,1)S(1)} %get-tuple-element.24), channel_id=1, source_target_pairs={{0,2},{2,0},{1,3},{3,1},{4,6},{6,4},{5,7},{7,5},{8,10},{10,8},{9,1... | collective-permute-start | bytes 294920 | tf_op jit(solution)/shard_map/ppermute | solution.py:47
  21.4 4.5 %collective-permute-start.2 = (bf16[24,1024]{1,0:T(8,128)(2,1)S(1)}, bf16[24,1024]{1,0:T(8,128)(2,1)S(1)}, u32[]{:S(2)}, u32[]{:S(2)}) collective-permute-start(bf16[24,1024]{1,0:T(8,128)(2,1)S(1)} %get-tuple-element.26), channel_id=1, source_target_pairs={{0,4},{4,0},{8,12},{12,8},{1,5},{5,1},{9,13},{13,9},{2,6},{6,2},{1... | collective-permute-start | bytes 147464 | tf_op jit(solution)/shard_map/send1/ppermute | solution.py:331
  23.3 5.5 %collective-permute-start.3 = (bf16[24,1024]{1,0:T(8,128)(2,1)S(1)}, bf16[24,1024]{1,0:T(8,128)(2,1)S(1)}, u32[]{:S(2)}, u32[]{:S(2)}) collective-permute-start(bf16[24,1024]{1,0:T(8,128)(2,1)S(1)} %get-tuple-element.27), channel_id=1, source_target_pairs={{0,8},{4,12},{8,0},{12,4},{1,9},{5,13},{9,1},{13,5},{2,10},{6,14},... | collective-permute-start | bytes 147464 | tf_op jit(solution)/shard_map/send2/ppermute | solution.py:331
  25.9 5.9 %collective-permute-start.4 = (bf16[24,1024]{1,0:T(8,128)(2,1)S(1)}, bf16[24,1024]{1,0:T(8,128)(2,1)S(1)}, u32[]{:S(2)}, u32[]{:S(2)}) collective-permute-start(bf16[24,1024]{1,0:T(8,128)(2,1)S(1)} %get-tuple-element.28), channel_id=1, source_target_pairs={{0,12},{4,8},{8,4},{12,0},{1,13},{5,9},{9,5},{13,1},{2,14},{6,10},... | collective-permute-start | bytes 147464 | tf_op jit(solution)/shard_map/send3/ppermute | solution.py:331
  31.8 1.4 %collective-permute-start.5 = (bf16[64,1024]{1,0:T(8,128)(2,1)S(1)}, bf16[64,1024]{1,0:T(8,128)(2,1)S(1)}, u32[]{:S(2)}, u32[]{:S(2)}) collective-permute-start(bf16[64,1024]{1,0:T(8,128)(2,1)S(1)} %shard_map.121), channel_id=1, source_target_pairs={{0,1},{1,0},{2,3},{3,2},{4,5},{5,4},{6,7},{7,6},{8,9},{9,8},{10,11... | collective-permute-start | bytes 393224 | tf_op jit(solution)/shard_map/ppermute | solution.py:53
  34.9 4.0 %collective-permute-start.6 = (bf16[48,384]{1,0:T(8,128)(2,1)S(1)}, bf16[48,384]{1,0:T(8,128)(2,1)S(1)}, u32[]{:S(2)}, u32[]{:S(2)}) collective-permute-start(bf16[48,384]{1,0:T(8,128)(2,1)S(1)} %shard_map.122.rest_0_), channel_id=1, source_target_pairs={{0,2},{2,0},{1,3},{3,1},{4,6},{6,4},{5,7},{7,5},{8,10},{10,8},{9,1... | collective-permute-start | bytes 110600 | tf_op jit(solution)/shard_map/ppermute | solution.py:47
  40.0 4.5 %collective-permute-start.7 = (bf16[16,1024]{1,0:T(8,128)(2,1)S(1)}, bf16[16,1024]{1,0:T(8,128)(2,1)S(1)}, u32[]{:S(2)}, u32[]{:S(2)}) collective-permute-start(bf16[16,1024]{1,0:T(8,128)(2,1)S(1)} %get-tuple-element.30), channel_id=1, source_target_pairs={{0,4},{4,0},{8,12},{12,8},{1,5},{5,1},{9,13},{13,9},{2,6},{6,2},{1... | collective-permute-start | bytes 98312 | tf_op jit(solution)/shard_map/back1/ppermute | solution.py:331
  40.1 4.9 %collective-permute-start.8 = (bf16[16,1024]{1,0:T(8,128)(2,1)S(1)}, bf16[16,1024]{1,0:T(8,128)(2,1)S(1)}, u32[]{:S(2)}, u32[]{:S(2)}) collective-permute-start(bf16[16,1024]{1,0:T(8,128)(2,1)S(1)} %get-tuple-element.31), channel_id=1, source_target_pairs={{0,8},{4,12},{8,0},{12,4},{1,9},{5,13},{9,1},{13,5},{2,10},{6,14},... | collective-permute-start | bytes 98312 | tf_op jit(solution)/shard_map/back2/ppermute | solution.py:331
  41.2 5.7 %collective-permute-start.9 = (bf16[16,1024]{1,0:T(8,128)(2,1)S(1)}, bf16[16,1024]{1,0:T(8,128)(2,1)S(1)}, u32[]{:S(2)}, u32[]{:S(2)}) collective-permute-start(bf16[16,1024]{1,0:T(8,128)(2,1)S(1)} %get-tuple-element.32), channel_id=1, source_target_pairs={{0,12},{4,8},{8,4},{12,0},{1,13},{5,9},{9,5},{13,1},{2,14},{6,10},... | collective-permute-start | bytes 98312 | tf_op jit(solution)/shard_map/back3/ppermute | solution.py:331
  44.4 2.5 %collective-permute-start.11 = (f32[24,1024]{1,0:T(8,128)S(1)}, f32[24,1024]{1,0:T(8,128)S(1)}, u32[]{:S(2)}, u32[]{:S(2)}) collective-permute-start(f32[24,1024]{1,0:T(8,128)S(1)} %get-tuple-element.34), channel_id=1, source_target_pairs={{0,1},{1,0},{2,3},{3,2},{4,5},{5,4},{6,7},{7,6},{8,9},{9,8},{10,11... | collective-permute-start | bytes 294920 | tf_op jit(solution)/shard_map/ppermute | solution.py:53
  47.0 1.3 %collective-permute-start.10 = (bf16[32,1024]{1,0:T(8,128)(2,1)S(1)}, bf16[32,1024]{1,0:T(8,128)(2,1)S(1)}, u32[]{:S(2)}, u32[]{:S(2)}) collective-permute-start(bf16[32,1024]{1,0:T(8,128)(2,1)S(1)} %shard_map.124), channel_id=1, source_target_pairs={{0,1},{1,0},{2,3},{3,2},{4,5},{5,4},{6,7},{7,6},{8,9},{9,8},{10,11... | collective-permute-start | bytes 196616 | tf_op jit(solution)/shard_map/ppermute | solution.py:53

commit v4 on v3

--- a/solution.py
+++ b/solution.py
@@ -8,12 +8,12 @@
 from jax.experimental.pallas import tpu as pltpu
 from jax.sharding import PartitionSpec as P
 
+
 SUBLANES = 8
 LANES = 128
 F32 = jnp.float32
 BF16 = jnp.bfloat16
 VMEM = pl.BlockSpec(memory_space=pltpu.VMEM)
-SMEM = pl.BlockSpec(memory_space=pltpu.SMEM)
 HBM = pl.BlockSpec(memory_space=pltpu.HBM)
 
 
@@ -29,12 +29,12 @@
     return lax.dot_general(a, b, (((1,), (1,)), ((), ())), preferred_element_type=F32)
 
 
-def call(body, outs, operands, in_specs=None, flops=0):
+def call(body, outs, operands, flops=0):
     size = sum(math.prod(o.shape) * o.dtype.itemsize for o in [*operands, *outs])
     return pl.pallas_call(
         body,
         out_shape=outs,
-        in_specs=in_specs or [VMEM] * len(operands),
+        in_specs=[VMEM] * len(operands),
         out_specs=[VMEM] * len(outs),
         compiler_params=pltpu.CompilerParams(vmem_limit_bytes=min(size * 2 + (8 << 20), 48 << 20)),
         cost_estimate=pl.CostEstimate(flops=flops, bytes_accessed=size, transcendentals=0),
@@ -54,7 +54,7 @@
 
 
 def attention_body(
-    capacity, place, q, k, v, fresh, lengths, residual, routed, weight, ext, kept, loaded, *scratch
+    capacity, q, k, v, fresh, lengths, residual, routed, weight, ext, kept, loaded, *scratch
 ):
     q_here, k_here, v_here, fresh_here, lengths_here, residual_here, routed_here, sems = scratch
     rows, heads, length, size = k.shape
@@ -97,7 +97,7 @@
     limits = as_column(lengths_here[...]).astype(jnp.int32)
     q_all = q_here[...].astype(F32)
     units = [(b, head) for b in range(len(batches)) for head in range(heads)]
-    scores, owns, own_values = [], [], []
+    scores, owns = [], []
     for b, head in units:
         if head == 0:
             key_copies[b].wait()
@@ -134,7 +134,7 @@
             ].astype(BF16)
     for copy in late:
         copy.wait()
-    deep = place[0]
+    deep = lax.axis_index("deep")
     half = kept.shape[1]
     kept[...] = residual_here[:, pl.ds(pl.multiple_of(deep * half, LANES), half)]
     ext[:, width : width + half] = residual_here[
@@ -166,6 +166,10 @@
     short[...] = out.astype(BF16)
 
 
+def goes_direct(chips):
+    return chips <= 4 and chips & (chips - 1) == 0
+
+
 def blocks_of(refs, count):
     if len(refs) == count:
         return list(refs)
@@ -178,7 +182,7 @@
     return chip ^ wide if direct else chip
 
 
-def pack_body(picks, chips, direct, place, own, other, kept, total, *rest):
+def pack_body(picks, chips, direct, own, other, kept, total, *rest):
     narrow_parts, (*packed, mine, lent) = rest[: -2 - packed_count(chips, direct)], rest[
         -2 - packed_count(chips, direct) :
     ]
@@ -195,7 +199,7 @@
     mixed = jnp.concatenate([mixed_own, mixed_other], 0).astype(BF16)
     notes = jnp.concatenate([own[:, width + half :], other[:, width + half :]], 0).astype(F32)
     notes = notes.astype(jnp.int32)
-    deep, wide = place[0], place[2]
+    deep, wide = lax.axis_index("deep"), lax.axis_index("wide")
     column = iota((2 * rows, chips * 3 * SUBLANES), 1)
     picked = jnp.zeros(column.shape, F32)
     for j in range(picks):
@@ -225,11 +229,11 @@
         out[i * size : (i + 1) * size] = block[SUBLANES:]
 
 
-def hidden_body(chips, place, *refs):
+def hidden_body(chips, *refs):
     *blocks, crossed, gain, gate_up, hidden, rows_ref = refs
     half = crossed.shape[1]
     edge = SUBLANES // 2
-    deep = place[0]
+    deep = lax.axis_index("deep")
     kept_at = pl.multiple_of(deep * half, LANES)
     crossed_at = pl.multiple_of((1 - deep) * half, LANES)
     kept = [block[...].astype(F32) for block in blocks_of(blocks, chips)]
@@ -262,9 +266,9 @@
     hidden[...] = (gate / (1.0 + jnp.exp(-gate)) * up).astype(BF16)
 
 
-def down_body(capacity, chips, parts, place, *rest):
+def down_body(capacity, chips, parts, *rest):
     pieces, weight, outs = rest[:parts], rest[parts], rest[parts + 1 :]
-    deep, narrow = place[0], place[1]
+    deep, narrow = lax.axis_index("deep"), lax.axis_index("narrow")
     depth = pieces[0].shape[1]
     rows = pieces[0].shape[0]
     shape = (chips * 2 * SUBLANES, rows)
@@ -290,11 +294,11 @@
         block[...] = total[i * 2 * SUBLANES : (i + 1) * 2 * SUBLANES]
 
 
-def combine_body(capacity, per_half, chips, direct, place, *refs):
+def combine_body(capacity, per_half, chips, direct, *refs):
     *blocks, crossed, own, mine, borrowed, router, out = refs
     rows, share = out.shape
     picks = router.shape[0]
-    deep, narrow, wide = place[0], place[1], place[2]
+    deep, narrow, wide = (lax.axis_index(name) for name in ("deep", "narrow", "wide"))
     notes = own[:, own.shape[1] - LANES :].astype(F32).astype(jnp.int32)
     diagonal = iota((rows, rows), 0) == iota((rows, rows), 1)
     lines = router[...]
@@ -318,7 +322,7 @@
     out[...] = total.astype(BF16)
 
 
-def exchange(blocks, direct, chips, name):
+def exchange(blocks, direct, chips):
     if not direct:
         (whole,) = blocks
         out = lax.all_to_all(
@@ -327,8 +331,7 @@
         return [out.reshape(whole.shape)]
     out = [blocks[0]]
     for step in range(1, chips):
-        with jax.named_scope(name + str(step)):
-            out.append(lax.ppermute(blocks[step], "wide", [(i, i ^ step) for i in range(chips)]))
+        out.append(lax.ppermute(blocks[step], "wide", [(i, i ^ step) for i in range(chips)]))
     return out
 
 
@@ -357,10 +360,8 @@
     assert lax.axis_size("deep") == 2 and half % share == 0 and half * 2 == full_width
     assert rows % SUBLANES == 0 and 2 * capacity - SUBLANES == SUBLANES // 2
     assert wide_count % 2 == 0 and 2 * picks <= LANES and experts <= LANES
-    direct = wide_count <= 4 and wide_count & (wide_count - 1) == 0
+    direct = goes_direct(wide_count)
     row_slots = wide_count * 2 * capacity
-    place = jnp.stack([lax.axis_index(name) for name in ("deep", "narrow", "wide")])
-    place = place.astype(jnp.int32)
     sds = jax.ShapeDtypeStruct
 
     def blocks_shape(tiles, width):
@@ -384,13 +385,13 @@
             sds((rows, half), BF16),
             sds(output_weight.shape, BF16),
         ],
-        in_specs=[SMEM] + [HBM] * (len(sources) + 1),
+        in_specs=[HBM] * (len(sources) + 1),
         out_specs=[VMEM] * 3,
         scratch_shapes=[pltpu.VMEM(x.shape, x.dtype) for x in sources]
         + [pltpu.SemaphoreType.DMA((2 * (rows // SUBLANES) + 6,))],
         compiler_params=pltpu.CompilerParams(vmem_limit_bytes=24 << 20),
         cost_estimate=pl.CostEstimate(flops=0, bytes_accessed=6 << 20, transcendentals=0),
-    )(place, *sources, output_weight)
+    )(*[pltpu.with_memory_space_constraint(x, pltpu.HBM) for x in [*sources, output_weight]])
     other = swap(ext, "deep")
     total, short = call(
         project_body,
@@ -402,11 +403,10 @@
     *packed, mine, lent = call(
         functools.partial(pack_body, picks, wide_count, direct),
         [*blocks_shape(3, half), sds((rows, half), F32), sds((rows, half), F32)],
-        [place, ext, other, kept, total, *parts],
-        [SMEM] + [VMEM] * (4 + len(parts)),
+        [ext, other, kept, total, *parts],
     )
     borrowed = swap(lent, "deep")
-    arrived = exchange(packed, direct, wide_count, "send")
+    arrived = exchange(packed, direct, wide_count)
     (passing,) = call(
         functools.partial(tail_body, wide_count),
         [sds((wide_count * 2 * SUBLANES, half), BF16)],
@@ -415,11 +415,11 @@
     crossed = swap(passing, "deep")
     gate_up = pltpu.with_memory_space_constraint(expert_gate_up[0], pltpu.VMEM)
     hidden_width = gate_up.shape[1]
-    operands = [place, *arrived, crossed, norm_gain[None, :], gate_up]
+    operands = [*arrived, crossed, norm_gain[None, :], gate_up]
     hidden = pl.pallas_call(
         functools.partial(hidden_body, wide_count),
         out_shape=[sds((row_slots, hidden_width), BF16)],
-        in_specs=[SMEM] + [VMEM] * (len(operands) - 1),
+        in_specs=[VMEM] * len(operands),
         out_specs=[VMEM],
         scratch_shapes=[pltpu.VMEM((row_slots, full_width), F32)],
         compiler_params=pltpu.CompilerParams(vmem_limit_bytes=40 << 20),
@@ -433,11 +433,10 @@
     expert_rows = call(
         functools.partial(down_body, capacity, wide_count, len(pieces)),
         blocks_shape(2, share),
-        [place, *pieces, pltpu.with_memory_space_constraint(expert_down[0], pltpu.VMEM)],
-        [SMEM] + [VMEM] * (len(pieces) + 1),
+        [*pieces, pltpu.with_memory_space_constraint(expert_down[0], pltpu.VMEM)],
         flops=2 * row_slots * share * hidden_width * narrow_count,
     )
-    returned = exchange(expert_rows, direct, wide_count, "back")
+    returned = exchange(expert_rows, direct, wide_count)
     (passing,) = call(
         functools.partial(tail_body, wide_count),
         [sds((wide_count * SUBLANES, share), BF16)],
@@ -447,8 +446,7 @@
     (out,) = call(
         functools.partial(combine_body, capacity, half // share, wide_count, direct),
         [sds((rows, share), BF16)],
-        [place, *returned, crossed, ext, mine, borrowed, router_weights.T],
-        [SMEM] + [VMEM] * (len(returned) + 5),
+        [*returned, crossed, ext, mine, borrowed, router_weights.T],
     )
     return out
 
@@ -469,4 +467,5 @@
         P(("group", "wide", "deep"), None),
     )
     out_specs = P(("group", "wide", "deep"), "narrow")
+
     return jax.shard_map(shards, mesh=mesh, in_specs=in_specs, out_specs=out_specs, check_vma=False)

time: 50 us -> 38.7 us (0.77)
  local copies, waits for them, and re-layouts: 8.03 us -> 0.02 us
  Pallas kernels: 9.89 us -> 6.84 us
    unnamed x24 -> x8, local copies, waits for them, and re-layouts: 8.03 us -> 0.02 us
    pallas_call x6, Pallas kernels: 4.44 us -> 2.81 us  [call(): pl.pallas_call(body, out_shape=outs, in_specs=[VMEM] * len(operands), out...]
    pallas_call x1, Pallas kernels: 3.8 us -> 2.88 us  [shards(): pl.pallas_call(functools.partial(attention_body, capacity), out_shape=[sd...]
    pallas_call x1, Pallas kernels: 1.65 us -> 1.14 us  [shards(): pl.pallas_call(functools.partial(hidden_body, wide_count), out_shape=[sds...]
where the time goes in v4:
time: 38.7 us; the launch traced here: 38.5 us
  waiting for transfers between devices  17.6 us (45%)
  starting transfers between devices  14 us (36%)
  Pallas kernels  6.84 us (18%)
    ppermute x6, starting transfers between devices, exchange(): lax.ppermute(blocks[step], 'wide', [(i, i ^ step) for i in range(chips)])  8.93 us
    ppermute x6, waiting for transfers between devices, exchange(): lax.ppermute(blocks[step], 'wide', [(i, i ^ step) for i in range(chips)])  8.39 us
    ppermute x2, waiting for transfers between devices, from_others(): lax.ppermute(value, axis, [(i, (i + step) % size) for i in range(size)])  5.57 us
    ppermute x2, starting transfers between devices, from_others(): lax.ppermute(value, axis, [(i, (i + step) % size) for i in range(size)])  4.46 us
    ppermute x4, waiting for transfers between devices, swap(): return lax.ppermute(value, axis, [(0, 1), (1, 0)])  3.59 us
    pallas_call x1, Pallas kernels, shards(): pl.pallas_call(functools.partial(attention_body, capacity), out_shape=[sd...  2.88 us
    pallas_call x6, Pallas kernels, call(): pl.pallas_call(body, out_shape=outs, in_specs=[VMEM] * len(operands), out...  2.81 us
    pallas_call x1, Pallas kernels, shards(): pl.pallas_call(functools.partial(hidden_body, wide_count), out_shape=[sds...  1.14 us
  transfers between devices with their start and end apart: 12, of which 9 were waited for; matrix products, arithmetic and copies ran while one was open for 0% of the time, Pallas kernels for 0%

profile of v4, /device:TPU:0, one launch (start us, length us, event | category | flops | bytes accessed | tf_op | source)
XLA Modules:
  0.0 38.5 jit_solution(6863024749431590142)
XLA Ops:
  0.0 2.9 %shard_map.118 = (bf16[24,3200]{1,0:T(8,128)(2,1)S(1)}, bf16[24,1024]{1,0:T(8,128)(2,1)S(1)}, bf16[2048,1024]{1,0:T(8,128)(2,1)S(1)}) custom-call(bf16[24,2048]{1,0:T(8,128)(2,1)} %q.1, bf16[24,2,32,128]{3,2,1,0:T(8,128)(2,1)} %k.1, bf16[24,2,32,128]{3,2,1,0:T(8,128)(2,1)} %v.1, bf16[24,2,256]{2,1,0:T(2,128)(2,1)} %fresh.1, s32[1,24]{1,0:T(1,128)} %bitcast.10, ...), custom_call_target="tpu_custom_call" | custom-call | bytes 6291456 | tf_op jit(solution)/shard_map/pallas_call | solution.py:381
  2.9 0.6 %collective-permute-start = (bf16[24,3200]{1,0:T(8,128)(2,1)S(1)}, bf16[24,3200]{1,0:T(8,128)(2,1)S(1)}, u32[]{:S(2)}, u32[]{:S(2)}) collective-permute-start(bf16[24,3200]{1,0:T(8,128)(2,1)S(1)} %get-tuple-element.20.own.refs_5_), channel_id=1, source_target_pairs={{0,1},{1,0},{2,3},{3,2},{4,5},{5,4},{6,7},{7,6},{8,9},{9,8},{10,11... | collective-permute-start | bytes 460808 | tf_op jit(solution)/shard_map/ppermute | solution.py:53
  3.5 1.0 %collective-permute-done.other = bf16[24,3200]{1,0:T(8,128)(2,1)S(1)} collective-permute-done((bf16[24,3200]{1,0:T(8,128)(2,1)S(1)}, bf16[24,3200]{1,0:T(8,128)(2,1)S(1)}, u32[]{:S(2)}, u32[]{:S(2)}) %collective-permute-start) | collective-permute-done | bytes 153632 | tf_op jit(solution)/shard_map/ppermute | solution.py:53
  4.5 0.8 %shard_map.119 = (f32[48,1024]{1,0:T(8,128)S(1)}, bf16[48,1024]{1,0:T(8,128)(2,1)S(1)}) custom-call(bf16[24,3200]{1,0:T(8,128)(2,1)S(1)} %get-tuple-element.20.own.refs_5_, bf16[24,3200]{1,0:T(8,128)(2,1)S(1)} %collective-permute-done.other, bf16[2048,1024]{1,0:T(8,128)(2,1)S(1)} %get-tuple-element.22.weight), custom_call_target="tpu_custom_call" | custom-call | flops 201326592 | bytes 4796416 | tf_op jit(solution)/shard_map/pallas_call | solution.py:34
  5.3 0.0 copy-start.3
  5.3 2.9 %collective-permute-start.1 = (bf16[48,1024]{1,0:T(8,128)(2,1)S(1)}, bf16[48,1024]{1,0:T(8,128)(2,1)S(1)}, u32[]{:S(2)}, u32[]{:S(2)}) collective-permute-start(bf16[48,1024]{1,0:T(8,128)(2,1)S(1)} %get-tuple-element.24), channel_id=1, source_target_pairs={{0,2},{2,0},{1,3},{3,1},{4,6},{6,4},{5,7},{7,5},{8,10},{10,8},{9,1... | collective-permute-start | bytes 294920 | tf_op jit(solution)/shard_map/ppermute | solution.py:47
  8.2 3.1 %collective-permute-done.1.rest_0_ = bf16[48,1024]{1,0:T(8,128)(2,1)S(1)} collective-permute-done((bf16[48,1024]{1,0:T(8,128)(2,1)S(1)}, bf16[48,1024]{1,0:T(8,128)(2,1)S(1)}, u32[]{:S(2)}, u32[]{:S(2)}) %collective-permute-start.1) | collective-permute-done | bytes 98336 | tf_op jit(solution)/shard_map/ppermute | solution.py:47
  11.3 0.5 %shard_map.120 = (bf16[24,1024]{1,0:T(8,128)(2,1)S(1)}, bf16[24,1024]{1,0:T(8,128)(2,1)S(1)}, bf16[24,1024]{1,0:T(8,128)(2,1)S(1)}, bf16[24,1024]{1,0:T(8,128)(2...) custom-call(bf16[24,3200]{1,0:T(8,128)(2,1)S(1)} %get-tuple-element.20.own.refs_5_, ...), custom_call_target="tpu_custom_call" | custom-call | bytes 1044480 | tf_op jit(solution)/shard_map/pallas_call | solution.py:34
  11.9 1.9 %collective-permute-start.2 = (bf16[24,1024]{1,0:T(8,128)(2,1)S(1)}, bf16[24,1024]{1,0:T(8,128)(2,1)S(1)}, u32[]{:S(2)}, u32[]{:S(2)}) collective-permute-start(bf16[24,1024]{1,0:T(8,128)(2,1)S(1)} %get-tuple-element.26), channel_id=1, source_target_pairs={{0,4},{4,0},{8,12},{12,8},{1,5},{5,1},{9,13},{13,9},{2,6},{6,2},{1... | collective-permute-start | bytes 147464 | tf_op jit(solution)/shard_map/ppermute | solution.py:334
  13.8 2.6 %collective-permute-start.3 = (bf16[24,1024]{1,0:T(8,128)(2,1)S(1)}, bf16[24,1024]{1,0:T(8,128)(2,1)S(1)}, u32[]{:S(2)}, u32[]{:S(2)}) collective-permute-start(bf16[24,1024]{1,0:T(8,128)(2,1)S(1)} %get-tuple-element.27), channel_id=1, source_target_pairs={{0,8},{4,12},{8,0},{12,4},{1,9},{5,13},{9,1},{13,5},{2,10},{6,14},... | collective-permute-start | bytes 147464 | tf_op jit(solution)/shard_map/ppermute | solution.py:334
  16.4 0.0 collective-permute-start.4
  16.4 0.0 collective-permute-done.2.refs_1_
  16.4 2.9 %collective-permute-done.3.refs_2_ = bf16[24,1024]{1,0:T(8,128)(2,1)S(1)} collective-permute-done((bf16[24,1024]{1,0:T(8,128)(2,1)S(1)}, bf16[24,1024]{1,0:T(8,128)(2,1)S(1)}, u32[]{:S(2)}, u32[]{:S(2)}) %collective-permute-start.3) | collective-permute-done | bytes 49184 | tf_op jit(solution)/shard_map/ppermute | solution.py:334
  19.3 3.0 %collective-permute-done.4.refs_3_ = bf16[24,1024]{1,0:T(8,128)(2,1)S(1)} collective-permute-done((bf16[24,1024]{1,0:T(8,128)(2,1)S(1)}, bf16[24,1024]{1,0:T(8,128)(2,1)S(1)}, u32[]{:S(2)}, u32[]{:S(2)}) %collective-permute-start.4) | collective-permute-done | bytes 49184 | tf_op jit(solution)/shard_map/ppermute | solution.py:334
  22.3 0.1 collective-permute-start.5
  22.3 1.3 %collective-permute-done.5.refs_4_ = bf16[64,1024]{1,0:T(8,128)(2,1)S(1)} collective-permute-done((bf16[64,1024]{1,0:T(8,128)(2,1)S(1)}, bf16[64,1024]{1,0:T(8,128)(2,1)S(1)}, u32[]{:S(2)}, u32[]{:S(2)}) %collective-permute-start.5) | collective-permute-done | bytes 131104 | tf_op jit(solution)/shard_map/ppermute | solution.py:53
  23.7 0.0 copy-done
  23.7 1.1 %shard_map.122.rest_0_ = bf16[48,384]{1,0:T(8,128)(2,1)S(1)} custom-call(bf16[24,1024]{1,0:T(8,128)(2,1)S(1)} %get-tuple-element.25.refs_0_, bf16[24,1024]{1,0:T(8,128)(2,1)S(1)} %collective-permute-done.2.refs_1_, bf16[24,1024]{1,0:T(8,128)(2,1)S(1)} %collective-permute-done.3.refs_2_, bf16[24,1024]{1,0:T(8,128)(2,1)S(1)} %collective-permute-done.4.refs_3_, ...), custom_call_target="tpu_custom_call" | custom-call | flops 150994944 | bytes 3145728 | tf_op jit(solution)/shard_map/pallas_call | solution.py:419
  24.8 1.6 %collective-permute-start.6 = (bf16[48,384]{1,0:T(8,128)(2,1)S(1)}, bf16[48,384]{1,0:T(8,128)(2,1)S(1)}, u32[]{:S(2)}, u32[]{:S(2)}) collective-permute-start(bf16[48,384]{1,0:T(8,128)(2,1)S(1)} %shard_map.122.rest_0_), channel_id=1, source_target_pairs={{0,2},{2,0},{1,3},{3,1},{4,6},{6,4},{5,7},{7,5},{8,10},{10,8},{9,1... | collective-permute-start | bytes 110600 | tf_op jit(solution)/shard_map/ppermute | solution.py:47
  26.4 2.5 %collective-permute-done.6.rest_1_ = bf16[48,384]{1,0:T(8,128)(2,1)S(1)} collective-permute-done((bf16[48,384]{1,0:T(8,128)(2,1)S(1)}, bf16[48,384]{1,0:T(8,128)(2,1)S(1)}, u32[]{:S(2)}, u32[]{:S(2)}) %collective-permute-start.6) | collective-permute-done | bytes 36896 | tf_op jit(solution)/shard_map/ppermute | solution.py:47
  28.8 0.5 %shard_map.123 = (bf16[16,1024]{1,0:T(8,128)(2,1)S(1)}, bf16[16,1024]{1,0:T(8,128)(2,1)S(1)}, bf16[16,1024]{1,0:T(8,128)(2,1)S(1)}, bf16[16,1024]{1,0:T(8,128)(2,1)S(1)}) custom-call(bf16[48,384]{1,0:T(8,128)(2,1)S(1)} %shard_map.122.rest_0_, bf16[48,384]{1,0:T(8,128)(2,1)S(1)} %collective-permute-done.6.rest_1_, bf16[768,1024]{1,0:T(8,128)(2,1)S(1)} %bitcast.7), custom_call_target="tpu_custom_call" | custom-call | flops 75497472 | bytes 1777664 | tf_op jit(solution)/shard_map/pallas_call | solution.py:34
  29.4 0.1 collective-permute-start.7
  29.5 1.2 %collective-permute-start.8 = (bf16[16,1024]{1,0:T(8,128)(2,1)S(1)}, bf16[16,1024]{1,0:T(8,128)(2,1)S(1)}, u32[]{:S(2)}, u32[]{:S(2)}) collective-permute-start(bf16[16,1024]{1,0:T(8,128)(2,1)S(1)} %get-tuple-element.31), channel_id=1, source_target_pairs={{0,8},{4,12},{8,0},{12,4},{1,9},{5,13},{9,1},{13,5},{2,10},{6,14},... | collective-permute-start | bytes 98312 | tf_op jit(solution)/shard_map/ppermute | solution.py:334
  30.6 3.2 %collective-permute-start.9 = (bf16[16,1024]{1,0:T(8,128)(2,1)S(1)}, bf16[16,1024]{1,0:T(8,128)(2,1)S(1)}, u32[]{:S(2)}, u32[]{:S(2)}) collective-permute-start(bf16[16,1024]{1,0:T(8,128)(2,1)S(1)} %get-tuple-element.32), channel_id=1, source_target_pairs={{0,12},{4,8},{8,4},{12,0},{1,13},{5,9},{9,5},{13,1},{2,14},{6,10},... | collective-permute-start | bytes 98312 | tf_op jit(solution)/shard_map/ppermute | solution.py:334
  33.8 0.0 collective-permute-start.11
  33.8 0.0 collective-permute-done.7.refs_1_
  33.8 0.5 %collective-permute-done.8.refs_2_ = bf16[16,1024]{1,0:T(8,128)(2,1)S(1)} collective-permute-done((bf16[16,1024]{1,0:T(8,128)(2,1)S(1)}, bf16[16,1024]{1,0:T(8,128)(2,1)S(1)}, u32[]{:S(2)}, u32[]{:S(2)}) %collective-permute-start.8) | collective-permute-done | bytes 32800 | tf_op jit(solution)/shard_map/ppermute | solution.py:334
  34.3 2.0 %collective-permute-done.9.refs_3_ = bf16[16,1024]{1,0:T(8,128)(2,1)S(1)} collective-permute-done((bf16[16,1024]{1,0:T(8,128)(2,1)S(1)}, bf16[16,1024]{1,0:T(8,128)(2,1)S(1)}, u32[]{:S(2)}, u32[]{:S(2)}) %collective-permute-start.9) | collective-permute-done | bytes 32800 | tf_op jit(solution)/shard_map/ppermute | solution.py:334
  36.4 0.0 collective-permute-start.10
  36.4 0.0 collective-permute-done.11.refs_7_
  36.4 1.2 %collective-permute-done.10.refs_4_ = bf16[32,1024]{1,0:T(8,128)(2,1)S(1)} collective-permute-done((bf16[32,1024]{1,0:T(8,128)(2,1)S(1)}, bf16[32,1024]{1,0:T(8,128)(2,1)S(1)}, u32[]{:S(2)}, u32[]{:S(2)}) %collective-permute-start.10) | collective-permute-done | bytes 65568 | tf_op jit(solution)/shard_map/ppermute | solution.py:53
  37.6 0.9 %shard_map.125 = bf16[24,1024]{1,0:T(8,128)(2,1)} custom-call(bf16[16,1024]{1,0:T(8,128)(2,1)S(1)} %get-tuple-element.29.refs_0_, bf16[16,1024]{1,0:T(8,128)(2,1)S(1)} %collective-permute-done.7.refs_1_, bf16[16,1024]{1,0:T(8,128)(2,1)S(1)} %collective-permute-done.8.refs_2_, bf16[16,1024]{1,0:T(8,128)(2,1)S(1)} %collective-permute-done.9.refs_3_, ...), custom_call_target="tpu_custom_call" | custom-call | bytes 596064 | tf_op jit(solution)/shard_map/pallas_call | solution.py:34
  (8 shorter events, 0.0 us)
Async XLA Ops:
  0.0 23.7 %copy-start = (bf16[1,2,384,2048]{3,2,1,0:T(8,128)(2,1)S(1)}, bf16[1,2,384,2048]{3,2,1,0:T(8,128)(2,1)}, u32[]{:S(2)}) copy-start(bf16[1,2,384,2048]{3,2,1,0:T(8,128)(2,1)} %param.20) | copy-start | bytes 9437188
  0.0 23.7 %copy-start.2 = (f32[2048]{0:T(1024)S(1)}, f32[2048]{0:T(1024)}, u32[]{:S(2)}) copy-start(f32[2048]{0:T(1024)} %param.18) | copy-start | bytes 24580
  2.9 1.6 %collective-permute-start = (bf16[24,3200]{1,0:T(8,128)(2,1)S(1)}, bf16[24,3200]{1,0:T(8,128)(2,1)S(1)}, u32[]{:S(2)}, u32[]{:S(2)}) collective-permute-start(bf16[24,3200]{1,0:T(8,128)(2,1)S(1)} %get-tuple-element.20.own.refs_5_), channel_id=1, source_target_pairs={{0,1},{1,0},{2,3},{3,2},{4,5},{5,4},{6,7},{7,6},{8,9},{9,8},{10,11... | collective-permute-start | bytes 460808 | tf_op jit(solution)/shard_map/ppermute | solution.py:53
  4.5 24.4 %copy-start.1 = (bf16[1,768,1024]{2,1,0:T(8,128)(2,1)S(1)}, bf16[1,768,1024]{2,1,0:T(8,128)(2,1)}, u32[]{:S(2)}) copy-start(bf16[1,768,1024]{2,1,0:T(8,128)(2,1)} %param.21) | copy-start | bytes 4718596
  5.3 32.3 %copy-start.3 = (f32[24,1]{0,1:T(1,128)S(1)}, f32[24,1]{0,1:T(1,128)}, u32[]{:S(2)}) copy-start(f32[24,1]{0,1:T(1,128)} %param.23) | copy-start | bytes 292
  5.3 6.0 %collective-permute-start.1 = (bf16[48,1024]{1,0:T(8,128)(2,1)S(1)}, bf16[48,1024]{1,0:T(8,128)(2,1)S(1)}, u32[]{:S(2)}, u32[]{:S(2)}) collective-permute-start(bf16[48,1024]{1,0:T(8,128)(2,1)S(1)} %get-tuple-element.24), channel_id=1, source_target_pairs={{0,2},{2,0},{1,3},{3,1},{4,6},{6,4},{5,7},{7,5},{8,10},{10,8},{9,1... | collective-permute-start | bytes 294920 | tf_op jit(solution)/shard_map/ppermute | solution.py:47
  11.9 4.5 %collective-permute-start.2 = (bf16[24,1024]{1,0:T(8,128)(2,1)S(1)}, bf16[24,1024]{1,0:T(8,128)(2,1)S(1)}, u32[]{:S(2)}, u32[]{:S(2)}) collective-permute-start(bf16[24,1024]{1,0:T(8,128)(2,1)S(1)} %get-tuple-element.26), channel_id=1, source_target_pairs={{0,4},{4,0},{8,12},{12,8},{1,5},{5,1},{9,13},{13,9},{2,6},{6,2},{1... | collective-permute-start | bytes 147464 | tf_op jit(solution)/shard_map/ppermute | solution.py:334
  13.8 5.5 %collective-permute-start.3 = (bf16[24,1024]{1,0:T(8,128)(2,1)S(1)}, bf16[24,1024]{1,0:T(8,128)(2,1)S(1)}, u32[]{:S(2)}, u32[]{:S(2)}) collective-permute-start(bf16[24,1024]{1,0:T(8,128)(2,1)S(1)} %get-tuple-element.27), channel_id=1, source_target_pairs={{0,8},{4,12},{8,0},{12,4},{1,9},{5,13},{9,1},{13,5},{2,10},{6,14},... | collective-permute-start | bytes 147464 | tf_op jit(solution)/shard_map/ppermute | solution.py:334
  16.4 5.9 %collective-permute-start.4 = (bf16[24,1024]{1,0:T(8,128)(2,1)S(1)}, bf16[24,1024]{1,0:T(8,128)(2,1)S(1)}, u32[]{:S(2)}, u32[]{:S(2)}) collective-permute-start(bf16[24,1024]{1,0:T(8,128)(2,1)S(1)} %get-tuple-element.28), channel_id=1, source_target_pairs={{0,12},{4,8},{8,4},{12,0},{1,13},{5,9},{9,5},{13,1},{2,14},{6,10},... | collective-permute-start | bytes 147464 | tf_op jit(solution)/shard_map/ppermute | solution.py:334
  22.3 1.4 %collective-permute-start.5 = (bf16[64,1024]{1,0:T(8,128)(2,1)S(1)}, bf16[64,1024]{1,0:T(8,128)(2,1)S(1)}, u32[]{:S(2)}, u32[]{:S(2)}) collective-permute-start(bf16[64,1024]{1,0:T(8,128)(2,1)S(1)} %shard_map.121), channel_id=1, source_target_pairs={{0,1},{1,0},{2,3},{3,2},{4,5},{5,4},{6,7},{7,6},{8,9},{9,8},{10,11... | collective-permute-start | bytes 393224 | tf_op jit(solution)/shard_map/ppermute | solution.py:53
  24.8 4.0 %collective-permute-start.6 = (bf16[48,384]{1,0:T(8,128)(2,1)S(1)}, bf16[48,384]{1,0:T(8,128)(2,1)S(1)}, u32[]{:S(2)}, u32[]{:S(2)}) collective-permute-start(bf16[48,384]{1,0:T(8,128)(2,1)S(1)} %shard_map.122.rest_0_), channel_id=1, source_target_pairs={{0,2},{2,0},{1,3},{3,1},{4,6},{6,4},{5,7},{7,5},{8,10},{10,8},{9,1... | collective-permute-start | bytes 110600 | tf_op jit(solution)/shard_map/ppermute | solution.py:47
  29.4 4.5 %collective-permute-start.7 = (bf16[16,1024]{1,0:T(8,128)(2,1)S(1)}, bf16[16,1024]{1,0:T(8,128)(2,1)S(1)}, u32[]{:S(2)}, u32[]{:S(2)}) collective-permute-start(bf16[16,1024]{1,0:T(8,128)(2,1)S(1)} %get-tuple-element.30), channel_id=1, source_target_pairs={{0,4},{4,0},{8,12},{12,8},{1,5},{5,1},{9,13},{13,9},{2,6},{6,2},{1... | collective-permute-start | bytes 98312 | tf_op jit(solution)/shard_map/ppermute | solution.py:334
  29.5 4.9 %collective-permute-start.8 = (bf16[16,1024]{1,0:T(8,128)(2,1)S(1)}, bf16[16,1024]{1,0:T(8,128)(2,1)S(1)}, u32[]{:S(2)}, u32[]{:S(2)}) collective-permute-start(bf16[16,1024]{1,0:T(8,128)(2,1)S(1)} %get-tuple-element.31), channel_id=1, source_target_pairs={{0,8},{4,12},{8,0},{12,4},{1,9},{5,13},{9,1},{13,5},{2,10},{6,14},... | collective-permute-start | bytes 98312 | tf_op jit(solution)/shard_map/ppermute | solution.py:334
  30.6 5.7 %collective-permute-start.9 = (bf16[16,1024]{1,0:T(8,128)(2,1)S(1)}, bf16[16,1024]{1,0:T(8,128)(2,1)S(1)}, u32[]{:S(2)}, u32[]{:S(2)}) collective-permute-start(bf16[16,1024]{1,0:T(8,128)(2,1)S(1)} %get-tuple-element.32), channel_id=1, source_target_pairs={{0,12},{4,8},{8,4},{12,0},{1,13},{5,9},{9,5},{13,1},{2,14},{6,10},... | collective-permute-start | bytes 98312 | tf_op jit(solution)/shard_map/ppermute | solution.py:334
  33.8 2.5 %collective-permute-start.11 = (f32[24,1024]{1,0:T(8,128)S(1)}, f32[24,1024]{1,0:T(8,128)S(1)}, u32[]{:S(2)}, u32[]{:S(2)}) collective-permute-start(f32[24,1024]{1,0:T(8,128)S(1)} %get-tuple-element.34), channel_id=1, source_target_pairs={{0,1},{1,0},{2,3},{3,2},{4,5},{5,4},{6,7},{7,6},{8,9},{9,8},{10,11... | collective-permute-start | bytes 294920 | tf_op jit(solution)/shard_map/ppermute | solution.py:53
  36.4 1.3 %collective-permute-start.10 = (bf16[32,1024]{1,0:T(8,128)(2,1)S(1)}, bf16[32,1024]{1,0:T(8,128)(2,1)S(1)}, u32[]{:S(2)}, u32[]{:S(2)}) collective-permute-start(bf16[32,1024]{1,0:T(8,128)(2,1)S(1)} %shard_map.124), channel_id=1, source_target_pairs={{0,1},{1,0},{2,3},{3,2},{4,5},{5,4},{6,7},{7,6},{8,9},{9,8},{10,11... | collective-permute-start | bytes 196616 | tf_op jit(solution)/shard_map/ppermute | solution.py:53

commit v5 on v4

--- a/solution.py
+++ b/solution.py
@@ -29,13 +29,14 @@
     return lax.dot_general(a, b, (((1,), (1,)), ((), ())), preferred_element_type=F32)
 
 
-def call(body, outs, operands, flops=0):
+def call(body, outs, operands, flops=0, scratch=()):
     size = sum(math.prod(o.shape) * o.dtype.itemsize for o in [*operands, *outs])
     return pl.pallas_call(
         body,
         out_shape=outs,
         in_specs=[VMEM] * len(operands),
         out_specs=[VMEM] * len(outs),
+        scratch_shapes=list(scratch),
         compiler_params=pltpu.CompilerParams(vmem_limit_bytes=min(size * 2 + (8 << 20), 48 << 20)),
         cost_estimate=pl.CostEstimate(flops=flops, bytes_accessed=size, transcendentals=0),
     )(*operands)
@@ -166,115 +167,162 @@
     short[...] = out.astype(BF16)
 
 
-def goes_direct(chips):
-    return chips <= 4 and chips & (chips - 1) == 0
-
-
-def blocks_of(refs, count):
-    if len(refs) == count:
-        return list(refs)
-    size = refs[0].shape[0] // count
-    return [refs[0].at[pl.ds(i * size, size)] for i in range(count)]
-
-
-def step_to(expert, wide, direct):
-    chip = lax.shift_right_logical(expert, 1)
-    return chip ^ wide if direct else chip
-
-
-def pack_body(picks, chips, direct, own, other, kept, total, *rest):
-    narrow_parts, (*packed, mine, lent) = rest[: -2 - packed_count(chips, direct)], rest[
-        -2 - packed_count(chips, direct) :
-    ]
+def routes_of(chips):
+    if chips == 2:
+        return [{0: 1, 1: 0}]
+    if chips == 4:
+        return [
+            {0: 3, 1: 2, 2: 1, 3: 0},
+            {0: 2, 1: 3, 2: 0, 3: 1},
+            {0: 1, 1: 0, 2: 3, 3: 2},
+        ]
+    return []
+
+
+def block_count(chips):
+    routes = routes_of(chips)
+    return len(routes) + 1 if routes else 1
+
+
+def store_blocks(refs, chips, tiles, value):
+    size = tiles * SUBLANES
+    routes = routes_of(chips)
+    if not routes:
+        refs[0][...] = value
+        return
+    wide = lax.axis_index("wide")
+    for here in range(chips):
+
+        @pl.when(wide == here)
+        def _(here=here):
+            for ref, route in zip(refs, [*routes, {here: here}]):
+                if here in route:
+                    to = route[here]
+                    ref[...] = value[to * size : (to + 1) * size]
+
+
+def each_source(refs, chips, use):
+    routes = routes_of(chips)
+    if not routes:
+        size = refs[0].shape[0] // chips
+        use([refs[0].at[pl.ds(i * size, size)] for i in range(chips)])
+        return
+    wide = lax.axis_index("wide")
+    for here in range(chips):
+
+        @pl.when(wide == here)
+        def _(here=here):
+            found = {}
+            for ref, route in zip(refs, [*routes, {here: here}]):
+                for source, to in route.items():
+                    if to == here:
+                        found[source] = ref
+            use([found[i] for i in range(chips)])
+
+
+def select_body(picks, chips, own, other, selector):
     rows = own.shape[0]
-    half = total.shape[1]
-    mixed = total[...]
-    for part in narrow_parts:
-        mixed = mixed + part[...].astype(F32)
-    width = own.shape[1] - half - LANES
-    mixed_own = mixed[:rows] + kept[...].astype(F32)
-    mixed_other = mixed[rows:] + other[:, width : width + half].astype(F32)
-    mine[...] = mixed_own
-    lent[...] = mixed_other
-    mixed = jnp.concatenate([mixed_own, mixed_other], 0).astype(BF16)
-    notes = jnp.concatenate([own[:, width + half :], other[:, width + half :]], 0).astype(F32)
-    notes = notes.astype(jnp.int32)
-    deep, wide = lax.axis_index("deep"), lax.axis_index("wide")
+    at = own.shape[1] - LANES
+    notes = jnp.concatenate([own[:, at:], other[:, at:]], 0).astype(F32).astype(jnp.int32)
+    deep = lax.axis_index("deep")
     column = iota((2 * rows, chips * 3 * SUBLANES), 1)
     picked = jnp.zeros(column.shape, F32)
     for j in range(picks):
         expert = notes[:, j : j + 1]
         slot = notes[:, picks + j : picks + j + 1]
         across = (expert & 1) ^ deep
-        at = jnp.where(
+        place = jnp.where(
             slot < SUBLANES,
             across * SUBLANES + slot,
             2 * SUBLANES + across * (SUBLANES // 2) + slot - SUBLANES,
         )
-        target = step_to(expert, wide, direct) * (3 * SUBLANES) + at
+        target = lax.shift_right_logical(expert, 1) * (3 * SUBLANES) + place
         picked = picked + (column == target).astype(F32)
-    out = dot(jnp.transpose(picked).astype(BF16), mixed).astype(BF16)
-    for i, block in enumerate(blocks_of(packed, chips)):
-        block[...] = out[i * 3 * SUBLANES : (i + 1) * 3 * SUBLANES]
-
-
-def packed_count(chips, direct):
-    return chips if direct else 1
+    selector[...] = jnp.transpose(picked).astype(BF16)
+
+
+def pack_body(chips, selector, other, kept, total, *rest):
+    count = block_count(chips) + 2
+    parts, (*packed, mine, lent) = rest[:-count], rest[-count:]
+    rows, half = kept.shape
+    mixed = total[...]
+    for part in parts:
+        mixed = mixed + part[...].astype(F32)
+    width = other.shape[1] - half - LANES
+    mixed_own = mixed[:rows] + kept[...].astype(F32)
+    mixed_other = mixed[rows:] + other[:, width : width + half].astype(F32)
+    mine[...] = mixed_own
+    lent[...] = mixed_other
+    mixed = jnp.concatenate([mixed_own, mixed_other], 0).astype(BF16)
+    store_blocks(packed, chips, 3, dot(selector[...], mixed).astype(BF16))
 
 
 def tail_body(chips, *refs):
     *blocks, out = refs
     size = out.shape[0] // chips
-    for i, block in enumerate(blocks_of(blocks, chips)):
-        out[i * size : (i + 1) * size] = block[SUBLANES:]
-
-
-def hidden_body(chips, *refs):
-    *blocks, crossed, gain, gate_up, hidden, rows_ref = refs
+
+    def use(found):
+        for i, block in enumerate(found):
+            out[i * size : (i + 1) * size] = block[SUBLANES:]
+
+    each_source(blocks, chips, use)
+
+
+def load_body(source, target, sem):
+    copy = pltpu.make_async_copy(source, target, sem)
+    copy.start()
+    copy.wait()
+
+
+def kept_body(chips, *refs):
+    *blocks, gain, weight, products, squares, rows_ref = refs
+    half = rows_ref.shape[1]
+    edge = SUBLANES // 2
+    first = iota((SUBLANES, half), 0) < edge
+
+    def use(found):
+        for i, block in enumerate(found):
+            rows_ref[i * SUBLANES : (i + 1) * SUBLANES] = block[:SUBLANES].astype(F32)
+        for i in range(0, chips, 2):
+            to = (chips + i // 2) * SUBLANES
+            tails = [block[2 * SUBLANES :].astype(F32) for block in found[i : i + 2]]
+            rows_ref[to : to + SUBLANES] = jnp.where(first, tails[0], pltpu.roll(tails[1], edge, 0))
+
+    each_source(blocks, chips, use)
+    at = pl.multiple_of(lax.axis_index("deep") * half, LANES)
+    rows = rows_ref[...]
+    squares[...] = jnp.sum(rows * rows, -1, keepdims=True)
+    scaled = (rows * gain[:, pl.ds(at, half)]).astype(BF16)
+    for i in range(2):
+        products[i] = dot_t(scaled, weight[i, :, pl.ds(at, half)])
+
+
+def hidden_body(chips, crossed, gain, weight, products, squares, hidden):
     half = crossed.shape[1]
     edge = SUBLANES // 2
-    deep = lax.axis_index("deep")
-    kept_at = pl.multiple_of(deep * half, LANES)
-    crossed_at = pl.multiple_of((1 - deep) * half, LANES)
-    kept = [block[...].astype(F32) for block in blocks_of(blocks, chips)]
+    first = iota((SUBLANES, half), 0) < edge
     came = crossed[...].astype(F32)
-    first = iota((SUBLANES, half), 0) < edge
-    for i in range(chips):
-        at = 2 * SUBLANES * i
-        rows_ref[i * SUBLANES : (i + 1) * SUBLANES, pl.ds(kept_at, half)] = kept[i][:SUBLANES]
-        rows_ref[i * SUBLANES : (i + 1) * SUBLANES, pl.ds(crossed_at, half)] = came[
-            at : at + SUBLANES
-        ]
-    for i in range(0, chips, 2):
-        to = chips * SUBLANES + i * edge
-        at = 2 * SUBLANES * i
-        rows_ref[to : to + SUBLANES, pl.ds(kept_at, half)] = jnp.where(
-            first,
-            kept[i][2 * SUBLANES :],
-            pltpu.roll(kept[i + 1][2 * SUBLANES :], edge, 0),
-        )
-        rows_ref[to : to + SUBLANES, pl.ds(crossed_at, half)] = jnp.where(
-            first,
-            pltpu.roll(came[at + SUBLANES : at + 2 * SUBLANES], edge, 0),
-            came[at + 3 * SUBLANES : at + 4 * SUBLANES],
-        )
-    rows = rows_ref[...]
-    scale = lax.rsqrt(jnp.mean(rows * rows, -1, keepdims=True) + 1e-06)
-    normed = (rows * scale * gain[...]).astype(BF16)
-    gate = dot_t(normed, gate_up[0])
-    up = dot_t(normed, gate_up[1])
+    tiles = [came[i * SUBLANES : (i + 1) * SUBLANES] for i in range(2 * chips)]
+    tails = [
+        jnp.where(first, pltpu.roll(tiles[2 * i + 1], edge, 0), tiles[2 * i + 3])
+        for i in range(0, chips, 2)
+    ]
+    rows = jnp.concatenate(tiles[::2] + tails, 0)
+    at = pl.multiple_of((1 - lax.axis_index("deep")) * half, LANES)
+    total = squares[...] + jnp.sum(rows * rows, -1, keepdims=True)
+    scale = lax.rsqrt(total / (2 * half) + 1e-06)
+    scaled = (rows * gain[:, pl.ds(at, half)]).astype(BF16)
+    gate = (products[0] + dot_t(scaled, weight[0, :, pl.ds(at, half)])) * scale
+    up = (products[1] + dot_t(scaled, weight[1, :, pl.ds(at, half)])) * scale
     hidden[...] = (gate / (1.0 + jnp.exp(-gate)) * up).astype(BF16)
 
 
-def down_body(capacity, chips, parts, *rest):
-    pieces, weight, outs = rest[:parts], rest[parts], rest[parts + 1 :]
-    deep, narrow = lax.axis_index("deep"), lax.axis_index("narrow")
-    depth = pieces[0].shape[1]
-    rows = pieces[0].shape[0]
-    shape = (chips * 2 * SUBLANES, rows)
+def ordered(capacity, chips, piece, step, parts, weight):
+    depth = piece.shape[1]
+    shape = (chips * 2 * SUBLANES, piece.shape[0])
     row = iota(shape, 0)
     chip = lax.div(row, 2 * SUBLANES)
-    source = lax.rem(lax.div(row, SUBLANES), 2) ^ deep
+    source = lax.rem(lax.div(row, SUBLANES), 2) ^ lax.axis_index("deep")
     slot = lax.rem(row, SUBLANES)
     full = source * capacity + slot
     column = jnp.where(
@@ -283,56 +331,75 @@
         chips * SUBLANES + chip * (SUBLANES // 2) + full - SUBLANES,
     )
     order = ((column == iota(shape, 1)) & (slot < capacity)).astype(BF16)
-    total = None
-    for step in range(parts):
-        owner = lax.rem(narrow + parts - step, parts)
-        piece = dot(order, pieces[step][...]).astype(BF16)
-        term = dot(piece, weight[pl.ds(pl.multiple_of(owner * depth, LANES), depth), :])
-        total = term if total is None else total + term
-    total = total.astype(BF16)
-    for i, block in enumerate(blocks_of(outs, chips)):
-        block[...] = total[i * 2 * SUBLANES : (i + 1) * 2 * SUBLANES]
-
-
-def combine_body(capacity, per_half, chips, direct, *refs):
-    *blocks, crossed, own, mine, borrowed, router, out = refs
-    rows, share = out.shape
+    owner = lax.rem(lax.axis_index("narrow") + parts - step, parts)
+    rows = dot(order, piece[...]).astype(BF16)
+    return dot(rows, weight[pl.ds(pl.multiple_of(owner * depth, LANES), depth), :])
+
+
+def begin_down_body(capacity, chips, parts, piece, weight, total):
+    total[...] = ordered(capacity, chips, piece, 0, parts, weight)
+
+
+def down_body(capacity, chips, parts, begun, *rest):
+    pieces, weight, outs = rest[: parts - 1], rest[parts - 1], rest[parts:]
+    total = begun[...]
+    for i, piece in enumerate(pieces):
+        total = total + ordered(capacity, chips, piece, i + 1, parts, weight)
+    store_blocks(outs, chips, 2, total.astype(BF16))
+
+
+def begin_combine_body(capacity, per_half, chips, *refs):
+    *blocks, own, mine, borrowed, router, total, selector, scales, value = refs
+    rows, share = total.shape
     picks = router.shape[0]
-    deep, narrow, wide = (lax.axis_index(name) for name in ("deep", "narrow", "wide"))
+    deep, narrow = lax.axis_index("deep"), lax.axis_index("narrow")
+
+    def use(found):
+        for i, block in enumerate(found):
+            value[i * SUBLANES : (i + 1) * SUBLANES] = block[:SUBLANES].astype(F32)
+
+    each_source(blocks, chips, use)
     notes = own[:, own.shape[1] - LANES :].astype(F32).astype(jnp.int32)
     diagonal = iota((rows, rows), 0) == iota((rows, rows), 1)
     lines = router[...]
     lines = lines / jnp.sum(lines, 0, keepdims=True)
-    column = iota((rows, 2 * chips * SUBLANES), 1)
+    column = iota((rows, chips * SUBLANES), 1)
     left = pl.multiple_of(lax.rem(narrow, per_half) * share, LANES)
     here = lax.div(narrow, per_half) == deep
-    total = jnp.where(here, mine[:, pl.ds(left, share)], borrowed[:, pl.ds(left, share)])
-    value = jnp.concatenate(
-        [block[:SUBLANES].astype(F32) for block in blocks_of(blocks, chips)]
-        + [crossed[...].astype(F32)],
-        0,
-    ).astype(BF16)
+    out = jnp.where(here, mine[:, pl.ds(left, share)], borrowed[:, pl.ds(left, share)])
     for j in range(picks):
         expert = notes[:, j : j + 1]
         slot = notes[:, picks + j : picks + j + 1] - deep * capacity
-        across = (expert & 1) ^ deep
-        target = (across * chips + step_to(expert, wide, direct)) * SUBLANES + slot
+        match = column == lax.shift_right_logical(expert, 1) * SUBLANES + slot
+        across = ((expert & 1) ^ deep) == 1
         weight = jnp.sum(jnp.where(diagonal, lines[j : j + 1, :], 0.0), -1, keepdims=True)
-        total = total + dot((column == target).astype(BF16), value) * weight
-    out[...] = total.astype(BF16)
-
-
-def exchange(blocks, direct, chips):
-    if not direct:
+        scales[j] = weight
+        selector[j] = (match & across).astype(BF16)
+        stays = (match & jnp.logical_not(across)).astype(BF16)
+        out = out + dot(stays, value[...].astype(BF16)) * weight
+    total[...] = out
+
+
+def combine_body(total, selector, scales, crossed, out):
+    value = total[...]
+    for j in range(selector.shape[0]):
+        value = value + dot(selector[j], crossed[...]) * scales[j]
+    out[...] = value.astype(BF16)
+
+
+def exchange(blocks, chips):
+    routes = routes_of(chips)
+    if not routes:
         (whole,) = blocks
         out = lax.all_to_all(
             whole.reshape(chips, -1, whole.shape[1]), "wide", split_axis=0, concat_axis=0, tiled=True
         )
         return [out.reshape(whole.shape)]
-    out = [blocks[0]]
-    for step in range(1, chips):
-        out.append(lax.ppermute(blocks[step], "wide", [(i, i ^ step) for i in range(chips)]))
-    return out
+    *leaving, stays = blocks
+    out = []
+    for block, route in zip(leaving, routes):
+        out.append(lax.ppermute(block, "wide", list(route.items())))
+    return [*out, stays]
 
 
 def shards(
@@ -360,13 +427,12 @@
     assert lax.axis_size("deep") == 2 and half % share == 0 and half * 2 == full_width
     assert rows % SUBLANES == 0 and 2 * capacity - SUBLANES == SUBLANES // 2
     assert wide_count % 2 == 0 and 2 * picks <= LANES and experts <= LANES
-    direct = goes_direct(wide_count)
     row_slots = wide_count * 2 * capacity
     sds = jax.ShapeDtypeStruct
 
     def blocks_shape(tiles, width):
-        if direct:
-            return [sds((tiles * SUBLANES, width), BF16)] * wide_count
+        if routes_of(wide_count):
+            return [sds((tiles * SUBLANES, width), BF16)] * block_count(wide_count)
         return [sds((wide_count * tiles * SUBLANES, width), BF16)]
 
     sources = [
@@ -400,54 +466,80 @@
         flops=4 * rows * head_width * half,
     )
     parts = from_others(short, "narrow")
+    (selector,) = call(
+        functools.partial(select_body, picks, wide_count),
+        [sds((wide_count * 3 * SUBLANES, 2 * rows), BF16)],
+        [ext, other],
+    )
+    gate_up = pl.pallas_call(
+        load_body,
+        out_shape=sds(expert_gate_up.shape[1:], BF16),
+        in_specs=[HBM],
+        out_specs=VMEM,
+        scratch_shapes=[pltpu.SemaphoreType.DMA],
+        compiler_params=pltpu.CompilerParams(vmem_limit_bytes=8 << 20),
+        cost_estimate=pl.CostEstimate(flops=0, bytes_accessed=4 << 20, transcendentals=0),
+    )(pltpu.with_memory_space_constraint(expert_gate_up[0], pltpu.HBM))
     *packed, mine, lent = call(
-        functools.partial(pack_body, picks, wide_count, direct),
+        functools.partial(pack_body, wide_count),
         [*blocks_shape(3, half), sds((rows, half), F32), sds((rows, half), F32)],
-        [ext, other, kept, total, *parts],
+        [selector, other, kept, total, *parts],
     )
     borrowed = swap(lent, "deep")
-    arrived = exchange(packed, direct, wide_count)
+    arrived = exchange(packed, wide_count)
     (passing,) = call(
         functools.partial(tail_body, wide_count),
         [sds((wide_count * 2 * SUBLANES, half), BF16)],
         arrived,
     )
     crossed = swap(passing, "deep")
-    gate_up = pltpu.with_memory_space_constraint(expert_gate_up[0], pltpu.VMEM)
     hidden_width = gate_up.shape[1]
-    operands = [*arrived, crossed, norm_gain[None, :], gate_up]
-    hidden = pl.pallas_call(
+    gain = norm_gain[None, :]
+    products, squares = call(
+        functools.partial(kept_body, wide_count),
+        [sds((2, row_slots, hidden_width), F32), sds((row_slots, 1), F32)],
+        [*arrived, gain, gate_up],
+        flops=2 * row_slots * hidden_width * full_width,
+        scratch=[pltpu.VMEM((row_slots, half), F32)],
+    )
+    (hidden,) = call(
         functools.partial(hidden_body, wide_count),
-        out_shape=[sds((row_slots, hidden_width), BF16)],
-        in_specs=[VMEM] * len(operands),
-        out_specs=[VMEM],
-        scratch_shapes=[pltpu.VMEM((row_slots, full_width), F32)],
-        compiler_params=pltpu.CompilerParams(vmem_limit_bytes=40 << 20),
-        cost_estimate=pl.CostEstimate(
-            flops=4 * row_slots * hidden_width * full_width,
-            bytes_accessed=4 * hidden_width * full_width,
-            transcendentals=0,
-        ),
-    )(*operands)[0]
-    pieces = [hidden, *from_others(hidden, "narrow")]
+        [sds((row_slots, hidden_width), BF16)],
+        [crossed, gain, gate_up, products, squares],
+        flops=2 * row_slots * hidden_width * full_width,
+    )
+    pieces = from_others(hidden, "narrow")
+    down = pltpu.with_memory_space_constraint(expert_down[0], pltpu.VMEM)
+    (begun,) = call(
+        functools.partial(begin_down_body, capacity, wide_count, narrow_count),
+        [sds((wide_count * 2 * SUBLANES, share), F32)],
+        [hidden, down],
+        flops=2 * row_slots * share * hidden_width,
+    )
     expert_rows = call(
-        functools.partial(down_body, capacity, wide_count, len(pieces)),
+        functools.partial(down_body, capacity, wide_count, narrow_count),
         blocks_shape(2, share),
-        [*pieces, pltpu.with_memory_space_constraint(expert_down[0], pltpu.VMEM)],
-        flops=2 * row_slots * share * hidden_width * narrow_count,
-    )
-    returned = exchange(expert_rows, direct, wide_count)
+        [begun, *pieces, down],
+        flops=2 * row_slots * share * hidden_width,
+    )
+    returned = exchange(expert_rows, wide_count)
     (passing,) = call(
         functools.partial(tail_body, wide_count),
         [sds((wide_count * SUBLANES, share), BF16)],
         returned,
     )
     crossed = swap(passing, "deep")
-    (out,) = call(
-        functools.partial(combine_body, capacity, half // share, wide_count, direct),
-        [sds((rows, share), BF16)],
-        [*returned, crossed, ext, mine, borrowed, router_weights.T],
-    )
+    combined = call(
+        functools.partial(begin_combine_body, capacity, half // share, wide_count),
+        [
+            sds((rows, share), F32),
+            sds((picks, rows, wide_count * SUBLANES), BF16),
+            sds((picks, rows, 1), F32),
+        ],
+        [*returned, ext, mine, borrowed, router_weights.T],
+        scratch=[pltpu.VMEM((wide_count * SUBLANES, share), F32)],
+    )
+    (out,) = call(combine_body, [sds((rows, share), BF16)], [*combined, crossed])
     return out
 
 

time: 38.7 us -> 37 us (0.956)
  waiting for transfers between devices: 17.6 us -> 13.2 us
  Pallas kernels: 6.84 us -> 9.14 us
    ppermute x6, waiting for transfers between devices: 8.39 us -> 6.66 us  [exchange(): out.append(lax.ppermute(block, 'wide', list(route.items())))]
    pallas_call x6 -> x11, Pallas kernels: 2.81 us -> 4.48 us  [call(): pl.pallas_call(body, out_shape=outs, in_specs=[VMEM] * len(operands), out...]
    ppermute x4, waiting for transfers between devices: 3.59 us -> 1.93 us  [swap(): return lax.ppermute(value, axis, [(0, 1), (1, 0)])]
    ppermute x2, waiting for transfers between devices: 5.57 us -> 4.62 us  [from_others(): lax.ppermute(value, axis, [(i, (i + step) % size) for i in range(size)])]
    pallas_call x1, Pallas kernels: 1.14 us -> 1.9 us  [shards(): pl.pallas_call(load_body, out_shape=sds(expert_gate_up.shape[1:], BF16),...]
  transfers between devices with their start and end apart: 12 -> 12, of which waited for: 9 -> 9; matrix products, arithmetic and copies ran while one was open for 0% -> 0% of each run, Pallas kernels for 0% -> 11%
where the time goes in v5:
time: 37 us; the launch traced here: 36.8 us
  starting transfers between devices  14.3 us (39%)
  waiting for transfers between devices  13.2 us (36%)
  Pallas kernels  9.14 us (25%)
    ppermute x6, starting transfers between devices, exchange(): out.append(lax.ppermute(block, 'wide', list(route.items())))  9.01 us
    ppermute x6, waiting for transfers between devices, exchange(): out.append(lax.ppermute(block, 'wide', list(route.items())))  6.66 us
    ppermute x2, waiting for transfers between devices, from_others(): lax.ppermute(value, axis, [(i, (i + step) % size) for i in range(size)])  4.62 us
    pallas_call x11, Pallas kernels, call(): pl.pallas_call(body, out_shape=outs, in_specs=[VMEM] * len(operands), out...  4.48 us
    ppermute x2, starting transfers between devices, from_others(): lax.ppermute(value, axis, [(i, (i + step) % size) for i in range(size)])  4.46 us
    pallas_call x1, Pallas kernels, shards(): pl.pallas_call(functools.partial(attention_body, capacity), out_shape=[sd...  2.76 us
    ppermute x4, waiting for transfers between devices, swap(): return lax.ppermute(value, axis, [(0, 1), (1, 0)])  1.93 us
    pallas_call x1, Pallas kernels, shards(): pl.pallas_call(load_body, out_shape=sds(expert_gate_up.shape[1:], BF16),...  1.9 us
  transfers between devices with their start and end apart: 12, of which 9 were waited for; matrix products, arithmetic and copies ran while one was open for 0% of the time, Pallas kernels for 11%

profile of v5, /device:TPU:0, one launch (start us, length us, event | category | flops | bytes accessed | tf_op | source)
XLA Modules:
  0.0 36.8 jit_solution(8606358078081254811)
XLA Ops:
  0.0 2.8 %shard_map.118 = (bf16[24,3200]{1,0:T(8,128)(2,1)S(1)}, bf16[24,1024]{1,0:T(8,128)(2,1)S(1)}, bf16[2048,1024]{1,0:T(8,128)(2,1)S(1)}) custom-call(bf16[24,2048]{1,0:T(8,128)(2,1)} %q.1, bf16[24,2,32,128]{3,2,1,0:T(8,128)(2,1)} %k.1, bf16[24,2,32,128]{3,2,1,0:T(8,128)(2,1)} %v.1, bf16[24,2,256]{2,1,0:T(2,128)(2,1)} %fresh.1, s32[1,24]{1,0:T(1,128)} %bitcast.12, ...), custom_call_target="tpu_custom_call" | custom-call | bytes 6291456 | tf_op jit(solution)/shard_map/pallas_call | solution.py:447
  2.8 0.6 %collective-permute-start = (bf16[24,3200]{1,0:T(8,128)(2,1)S(1)}, bf16[24,3200]{1,0:T(8,128)(2,1)S(1)}, u32[]{:S(2)}, u32[]{:S(2)}) collective-permute-start(bf16[24,3200]{1,0:T(8,128)(2,1)S(1)} %get-tuple-element.25.own.refs_4_), channel_id=1, source_target_pairs={{0,1},{1,0},{2,3},{3,2},{4,5},{5,4},{6,7},{7,6},{8,9},{9,8},{10,11... | collective-permute-start | bytes 460808 | tf_op jit(solution)/shard_map/ppermute | solution.py:54
  3.3 1.0 %collective-permute-done.other = bf16[24,3200]{1,0:T(8,128)(2,1)S(1)} collective-permute-done((bf16[24,3200]{1,0:T(8,128)(2,1)S(1)}, bf16[24,3200]{1,0:T(8,128)(2,1)S(1)}, u32[]{:S(2)}, u32[]{:S(2)}) %collective-permute-start) | collective-permute-done | bytes 153632 | tf_op jit(solution)/shard_map/ppermute | solution.py:54
  4.3 0.8 %shard_map.120 = (f32[48,1024]{1,0:T(8,128)S(1)}, bf16[48,1024]{1,0:T(8,128)(2,1)S(1)}) custom-call(bf16[24,3200]{1,0:T(8,128)(2,1)S(1)} %get-tuple-element.25.own.refs_4_, bf16[24,3200]{1,0:T(8,128)(2,1)S(1)} %collective-permute-done.other, bf16[2048,1024]{1,0:T(8,128)(2,1)S(1)} %get-tuple-element.27.weight), custom_call_target="tpu_custom_call" | custom-call | flops 201326592 | bytes 4796416 | tf_op jit(solution)/shard_map/pallas_call | solution.py:34
  5.2 2.9 %collective-permute-start.1 = (bf16[48,1024]{1,0:T(8,128)(2,1)S(1)}, bf16[48,1024]{1,0:T(8,128)(2,1)S(1)}, u32[]{:S(2)}, u32[]{:S(2)}) collective-permute-start(bf16[48,1024]{1,0:T(8,128)(2,1)S(1)} %get-tuple-element.29), channel_id=1, source_target_pairs={{0,2},{2,0},{1,3},{3,1},{4,6},{6,4},{5,7},{7,5},{8,10},{10,8},{9,1... | collective-permute-start | bytes 294920 | tf_op jit(solution)/shard_map/ppermute | solution.py:48
  8.1 0.4 shard_map.119.selector
  8.5 2.7 %collective-permute-done.1.rest_0_ = bf16[48,1024]{1,0:T(8,128)(2,1)S(1)} collective-permute-done((bf16[48,1024]{1,0:T(8,128)(2,1)S(1)}, bf16[48,1024]{1,0:T(8,128)(2,1)S(1)}, u32[]{:S(2)}, u32[]{:S(2)}) %collective-permute-start.1) | collective-permute-done | bytes 98336 | tf_op jit(solution)/shard_map/ppermute | solution.py:48
  11.2 0.2 shard_map.121
  11.4 3.9 %collective-permute-start.2 = (bf16[24,1024]{1,0:T(8,128)(2,1)S(1)}, bf16[24,1024]{1,0:T(8,128)(2,1)S(1)}, u32[]{:S(2)}, u32[]{:S(2)}) collective-permute-start(bf16[24,1024]{1,0:T(8,128)(2,1)S(1)} %get-tuple-element.30), channel_id=1, source_target_pairs={{0,12},{4,8},{8,4},{12,0},{1,13},{5,9},{9,5},{13,1},{2,14},{6,10},... | collective-permute-start | bytes 147464 | tf_op jit(solution)/shard_map/ppermute | solution.py:401
  15.4 0.6 %collective-permute-start.4 = (bf16[24,1024]{1,0:T(8,128)(2,1)S(1)}, bf16[24,1024]{1,0:T(8,128)(2,1)S(1)}, u32[]{:S(2)}, u32[]{:S(2)}) collective-permute-start(bf16[24,1024]{1,0:T(8,128)(2,1)S(1)} %get-tuple-element.32), channel_id=1, source_target_pairs={{0,4},{4,0},{8,12},{12,8},{1,5},{5,1},{9,13},{13,9},{2,6},{6,2},{1... | collective-permute-start | bytes 147464 | tf_op jit(solution)/shard_map/ppermute | solution.py:401
  16.0 2.0 %collective-permute-done.2.refs_0_ = bf16[24,1024]{1,0:T(8,128)(2,1)S(1)} collective-permute-done((bf16[24,1024]{1,0:T(8,128)(2,1)S(1)}, bf16[24,1024]{1,0:T(8,128)(2,1)S(1)}, u32[]{:S(2)}, u32[]{:S(2)}) %collective-permute-start.2) | collective-permute-done | bytes 49184 | tf_op jit(solution)/shard_map/ppermute | solution.py:401
  18.0 2.3 %collective-permute-done.3.refs_1_ = bf16[24,1024]{1,0:T(8,128)(2,1)S(1)} collective-permute-done((bf16[24,1024]{1,0:T(8,128)(2,1)S(1)}, bf16[24,1024]{1,0:T(8,128)(2,1)S(1)}, u32[]{:S(2)}, u32[]{:S(2)}) %collective-permute-start.3) | collective-permute-done | bytes 49184 | tf_op jit(solution)/shard_map/ppermute | solution.py:401
  20.4 0.1 collective-permute-start.5
  20.5 1.9 %shard_map.123.refs_5_.weight = bf16[2,384,2048]{2,1,0:T(8,128)(2,1)S(1)} custom-call(bf16[2,384,2048]{2,1,0:T(8,128)(2,1)} %bitcast.11), custom_call_target="tpu_custom_call" | custom-call | bytes 4194304 | tf_op jit(solution)/shard_map/pallas_call | solution.py:474
  22.4 0.0 copy-start
  22.4 0.6 %shard_map.124 = (f32[2,48,384]{2,1,0:T(8,128)S(1)}, f32[48,1]{1,0:T(8,128)S(1)}) custom-call(bf16[24,1024]{1,0:T(8,128)(2,1)S(1)} %collective-permute-done.2.refs_0_, bf16[24,1024]{1,0:T(8,128)(2,1)S(1)} %collective-permute-done.3.refs_1_, bf16[24,1024]{1,0:T(8,128)(2,1)S(1)} %collective-permute-done.4.refs_2_, ...), custom_call_target="tpu_custom_call" | custom-call | flops 75497472 | bytes 3498176 | tf_op jit(solution)/shard_map/pallas_call | solution.py:34
  23.0 0.0 copy-start.2
  23.0 0.6 %shard_map.125.piece = bf16[48,384]{1,0:T(8,128)(2,1)S(1)} custom-call(bf16[64,1024]{1,0:T(8,128)(2,1)S(1)} %collective-permute-done.5.crossed, f32[1,2048]{1,0:T(1,128)S(1)} %bitcast.9, bf16[2,384,2048]{2,1,0:T(8,128)(2,1)S(1)} %shard_map.123.refs_5_.weight, f32[2,48,384]{2,1,0:T(8,128)S(1)} %get-tuple-element.34.products, ...), custom_call_target="tpu_custom_call" | custom-call | flops 75497472 | bytes 3469504 | tf_op jit(solution)/shard_map/pallas_call | solution.py:34
  23.6 1.6 %collective-permute-start.6 = (bf16[48,384]{1,0:T(8,128)(2,1)S(1)}, bf16[48,384]{1,0:T(8,128)(2,1)S(1)}, u32[]{:S(2)}, u32[]{:S(2)}) collective-permute-start(bf16[48,384]{1,0:T(8,128)(2,1)S(1)} %shard_map.125.piece), channel_id=1, source_target_pairs={{0,2},{2,0},{1,3},{3,1},{4,6},{6,4},{5,7},{7,5},{8,10},{10,8},{9,1... | collective-permute-start | bytes 110600 | tf_op jit(solution)/shard_map/ppermute | solution.py:48
  25.2 0.2 collective-permute-start.10
  25.4 0.4 shard_map.126.begun
  25.8 1.9 %collective-permute-done.6.rest_0_ = bf16[48,384]{1,0:T(8,128)(2,1)S(1)} collective-permute-done((bf16[48,384]{1,0:T(8,128)(2,1)S(1)}, bf16[48,384]{1,0:T(8,128)(2,1)S(1)}, u32[]{:S(2)}, u32[]{:S(2)}) %collective-permute-start.6) | collective-permute-done | bytes 36896 | tf_op jit(solution)/shard_map/ppermute | solution.py:48
  27.7 0.4 %shard_map.127 = (bf16[16,1024]{1,0:T(8,128)(2,1)S(1)}, bf16[16,1024]{1,0:T(8,128)(2,1)S(1)}, bf16[16,1024]{1,0:T(8,128)(2,1)S(1)}, bf16[16,1024]{1,0:T(8,128)(2,1)S(1)}) custom-call(f32[64,1024]{1,0:T(8,128)S(1)} %shard_map.126.begun, bf16[48,384]{1,0:T(8,128)(2,1)S(1)} %collective-permute-done.6.rest_0_, bf16[768,1024]{1,0:T(8,128)(2,1)S(1)} %bitcast.7), custom_call_target="tpu_custom_call" | custom-call | flops 37748736 | bytes 2002944 | tf_op jit(solution)/shard_map/pallas_call | solution.py:34
  28.1 1.7 %collective-permute-start.7 = (bf16[16,1024]{1,0:T(8,128)(2,1)S(1)}, bf16[16,1024]{1,0:T(8,128)(2,1)S(1)}, u32[]{:S(2)}, u32[]{:S(2)}) collective-permute-start(bf16[16,1024]{1,0:T(8,128)(2,1)S(1)} %get-tuple-element.36), channel_id=1, source_target_pairs={{0,12},{4,8},{8,4},{12,0},{1,13},{5,9},{9,5},{13,1},{2,14},{6,10},... | collective-permute-start | bytes 98312 | tf_op jit(solution)/shard_map/ppermute | solution.py:401
  29.7 0.5 %collective-permute-start.8 = (bf16[16,1024]{1,0:T(8,128)(2,1)S(1)}, bf16[16,1024]{1,0:T(8,128)(2,1)S(1)}, u32[]{:S(2)}, u32[]{:S(2)}) collective-permute-start(bf16[16,1024]{1,0:T(8,128)(2,1)S(1)} %get-tuple-element.37), channel_id=1, source_target_pairs={{0,8},{4,12},{8,0},{12,4},{1,9},{5,13},{9,1},{13,5},{2,10},{6,14},... | collective-permute-start | bytes 98312 | tf_op jit(solution)/shard_map/ppermute | solution.py:401
  30.2 2.3 %collective-permute-start.9 = (bf16[16,1024]{1,0:T(8,128)(2,1)S(1)}, bf16[16,1024]{1,0:T(8,128)(2,1)S(1)}, u32[]{:S(2)}, u32[]{:S(2)}) collective-permute-start(bf16[16,1024]{1,0:T(8,128)(2,1)S(1)} %get-tuple-element.38), channel_id=1, source_target_pairs={{0,4},{4,0},{8,12},{12,8},{1,5},{5,1},{9,13},{13,9},{2,6},{6,2},{1... | collective-permute-start | bytes 98312 | tf_op jit(solution)/shard_map/ppermute | solution.py:401
  32.5 1.7 %collective-permute-done.7.refs_0_ = bf16[16,1024]{1,0:T(8,128)(2,1)S(1)} collective-permute-done((bf16[16,1024]{1,0:T(8,128)(2,1)S(1)}, bf16[16,1024]{1,0:T(8,128)(2,1)S(1)}, u32[]{:S(2)}, u32[]{:S(2)}) %collective-permute-start.7) | collective-permute-done | bytes 32800 | tf_op jit(solution)/shard_map/ppermute | solution.py:401
  34.2 0.4 %collective-permute-done.8.refs_1_ = bf16[16,1024]{1,0:T(8,128)(2,1)S(1)} collective-permute-done((bf16[16,1024]{1,0:T(8,128)(2,1)S(1)}, bf16[16,1024]{1,0:T(8,128)(2,1)S(1)}, u32[]{:S(2)}, u32[]{:S(2)}) %collective-permute-start.8) | collective-permute-done | bytes 32800 | tf_op jit(solution)/shard_map/ppermute | solution.py:401
  34.5 0.3 collective-permute-done.9.refs_2_
  34.9 0.3 shard_map.128
  35.2 0.9 %collective-permute-done.11.crossed = bf16[32,1024]{1,0:T(8,128)(2,1)S(1)} collective-permute-done((bf16[32,1024]{1,0:T(8,128)(2,1)S(1)}, bf16[32,1024]{1,0:T(8,128)(2,1)S(1)}, u32[]{:S(2)}, u32[]{:S(2)}) %collective-permute-start.11) | collective-permute-done | bytes 65568 | tf_op jit(solution)/shard_map/ppermute | solution.py:54
  36.1 0.8 %shard_map.130 = bf16[24,1024]{1,0:T(8,128)(2,1)} custom-call(f32[24,1024]{1,0:T(8,128)S(1)} %get-tuple-element.42.total, bf16[1,24,32]{2,1,0:T(8,128)(2,1)S(1)} %get-tuple-element.43.selector, f32[1,24,1]{2,1,0:T(8,128)S(1)} %get-tuple-element.44.scales, bf16[32,1024]{1,0:T(8,128)(2,1)S(1)} %collective-permute-done.11.crossed), custom_call_target="tpu_custom_call" | custom-call | bytes 214624 | tf_op jit(solution)/shard_map/pallas_call | solution.py:34
  (11 shorter events, 0.1 us)
Async XLA Ops:
  2.8 1.6 %collective-permute-start = (bf16[24,3200]{1,0:T(8,128)(2,1)S(1)}, bf16[24,3200]{1,0:T(8,128)(2,1)S(1)}, u32[]{:S(2)}, u32[]{:S(2)}) collective-permute-start(bf16[24,3200]{1,0:T(8,128)(2,1)S(1)} %get-tuple-element.25.own.refs_4_), channel_id=1, source_target_pairs={{0,1},{1,0},{2,3},{3,2},{4,5},{5,4},{6,7},{7,6},{8,9},{9,8},{10,11... | collective-permute-start | bytes 460808 | tf_op jit(solution)/shard_map/ppermute | solution.py:54
  5.2 6.0 %collective-permute-start.1 = (bf16[48,1024]{1,0:T(8,128)(2,1)S(1)}, bf16[48,1024]{1,0:T(8,128)(2,1)S(1)}, u32[]{:S(2)}, u32[]{:S(2)}) collective-permute-start(bf16[48,1024]{1,0:T(8,128)(2,1)S(1)} %get-tuple-element.29), channel_id=1, source_target_pairs={{0,2},{2,0},{1,3},{3,1},{4,6},{6,4},{5,7},{7,5},{8,10},{10,8},{9,1... | collective-permute-start | bytes 294920 | tf_op jit(solution)/shard_map/ppermute | solution.py:48
  11.4 6.6 %collective-permute-start.2 = (bf16[24,1024]{1,0:T(8,128)(2,1)S(1)}, bf16[24,1024]{1,0:T(8,128)(2,1)S(1)}, u32[]{:S(2)}, u32[]{:S(2)}) collective-permute-start(bf16[24,1024]{1,0:T(8,128)(2,1)S(1)} %get-tuple-element.30), channel_id=1, source_target_pairs={{0,12},{4,8},{8,4},{12,0},{1,13},{5,9},{9,5},{13,1},{2,14},{6,10},... | collective-permute-start | bytes 147464 | tf_op jit(solution)/shard_map/ppermute | solution.py:401
  15.3 5.0 %collective-permute-start.3 = (bf16[24,1024]{1,0:T(8,128)(2,1)S(1)}, bf16[24,1024]{1,0:T(8,128)(2,1)S(1)}, u32[]{:S(2)}, u32[]{:S(2)}) collective-permute-start(bf16[24,1024]{1,0:T(8,128)(2,1)S(1)} %get-tuple-element.31), channel_id=1, source_target_pairs={{0,8},{4,12},{8,0},{12,4},{1,9},{5,13},{9,1},{13,5},{2,10},{6,14},... | collective-permute-start | bytes 147464 | tf_op jit(solution)/shard_map/ppermute | solution.py:401
  15.4 5.0 %collective-permute-start.4 = (bf16[24,1024]{1,0:T(8,128)(2,1)S(1)}, bf16[24,1024]{1,0:T(8,128)(2,1)S(1)}, u32[]{:S(2)}, u32[]{:S(2)}) collective-permute-start(bf16[24,1024]{1,0:T(8,128)(2,1)S(1)} %get-tuple-element.32), channel_id=1, source_target_pairs={{0,4},{4,0},{8,12},{12,8},{1,5},{5,1},{9,13},{13,9},{2,6},{6,2},{1... | collective-permute-start | bytes 147464 | tf_op jit(solution)/shard_map/ppermute | solution.py:401
  20.4 2.7 %collective-permute-start.5 = (bf16[64,1024]{1,0:T(8,128)(2,1)S(1)}, bf16[64,1024]{1,0:T(8,128)(2,1)S(1)}, u32[]{:S(2)}, u32[]{:S(2)}) collective-permute-start(bf16[64,1024]{1,0:T(8,128)(2,1)S(1)} %shard_map.122), channel_id=1, source_target_pairs={{0,1},{1,0},{2,3},{3,2},{4,5},{5,4},{6,7},{7,6},{8,9},{9,8},{10,11... | collective-permute-start | bytes 393224 | tf_op jit(solution)/shard_map/ppermute | solution.py:54
  20.4 1.9 %copy-start.1 = (f32[2048]{0:T(1024)S(1)}, f32[2048]{0:T(1024)}, u32[]{:S(2)}) copy-start(f32[2048]{0:T(1024)} %param.18) | copy-start | bytes 24580
  22.4 3.0 %copy-start = (bf16[1,768,1024]{2,1,0:T(8,128)(2,1)S(1)}, bf16[1,768,1024]{2,1,0:T(8,128)(2,1)}, u32[]{:S(2)}) copy-start(bf16[1,768,1024]{2,1,0:T(8,128)(2,1)} %param.21) | copy-start | bytes 4718596
  23.0 11.8 %copy-start.2 = (f32[24,1]{0,1:T(1,128)S(1)}, f32[24,1]{0,1:T(1,128)}, u32[]{:S(2)}) copy-start(f32[24,1]{0,1:T(1,128)} %param.23) | copy-start | bytes 292
  23.6 4.0 %collective-permute-start.6 = (bf16[48,384]{1,0:T(8,128)(2,1)S(1)}, bf16[48,384]{1,0:T(8,128)(2,1)S(1)}, u32[]{:S(2)}, u32[]{:S(2)}) collective-permute-start(bf16[48,384]{1,0:T(8,128)(2,1)S(1)} %shard_map.125.piece), channel_id=1, source_target_pairs={{0,2},{2,0},{1,3},{3,1},{4,6},{6,4},{5,7},{7,5},{8,10},{10,8},{9,1... | collective-permute-start | bytes 110600 | tf_op jit(solution)/shard_map/ppermute | solution.py:48
  25.2 9.6 %collective-permute-start.10 = (f32[24,1024]{1,0:T(8,128)S(1)}, f32[24,1024]{1,0:T(8,128)S(1)}, u32[]{:S(2)}, u32[]{:S(2)}) collective-permute-start(f32[24,1024]{1,0:T(8,128)S(1)} %get-tuple-element.41), channel_id=1, source_target_pairs={{0,1},{1,0},{2,3},{3,2},{4,5},{5,4},{6,7},{7,6},{8,9},{9,8},{10,11... | collective-permute-start | bytes 294920 | tf_op jit(solution)/shard_map/ppermute | solution.py:54
  28.1 6.1 %collective-permute-start.7 = (bf16[16,1024]{1,0:T(8,128)(2,1)S(1)}, bf16[16,1024]{1,0:T(8,128)(2,1)S(1)}, u32[]{:S(2)}, u32[]{:S(2)}) collective-permute-start(bf16[16,1024]{1,0:T(8,128)(2,1)S(1)} %get-tuple-element.36), channel_id=1, source_target_pairs={{0,12},{4,8},{8,4},{12,0},{1,13},{5,9},{9,5},{13,1},{2,14},{6,10},... | collective-permute-start | bytes 98312 | tf_op jit(solution)/shard_map/ppermute | solution.py:401
  29.7 4.8 %collective-permute-start.8 = (bf16[16,1024]{1,0:T(8,128)(2,1)S(1)}, bf16[16,1024]{1,0:T(8,128)(2,1)S(1)}, u32[]{:S(2)}, u32[]{:S(2)}) collective-permute-start(bf16[16,1024]{1,0:T(8,128)(2,1)S(1)} %get-tuple-element.37), channel_id=1, source_target_pairs={{0,8},{4,12},{8,0},{12,4},{1,9},{5,13},{9,1},{13,5},{2,10},{6,14},... | collective-permute-start | bytes 98312 | tf_op jit(solution)/shard_map/ppermute | solution.py:401
  30.2 4.6 %collective-permute-start.9 = (bf16[16,1024]{1,0:T(8,128)(2,1)S(1)}, bf16[16,1024]{1,0:T(8,128)(2,1)S(1)}, u32[]{:S(2)}, u32[]{:S(2)}) collective-permute-start(bf16[16,1024]{1,0:T(8,128)(2,1)S(1)} %get-tuple-element.38), channel_id=1, source_target_pairs={{0,4},{4,0},{8,12},{12,8},{1,5},{5,1},{9,13},{13,9},{2,6},{6,2},{1... | collective-permute-start | bytes 98312 | tf_op jit(solution)/shard_map/ppermute | solution.py:401
  34.8 1.3 %collective-permute-start.11 = (bf16[32,1024]{1,0:T(8,128)(2,1)S(1)}, bf16[32,1024]{1,0:T(8,128)(2,1)S(1)}, u32[]{:S(2)}, u32[]{:S(2)}) collective-permute-start(bf16[32,1024]{1,0:T(8,128)(2,1)S(1)} %shard_map.129), channel_id=1, source_target_pairs={{0,1},{1,0},{2,3},{3,2},{4,5},{5,4},{6,7},{7,6},{8,9},{9,8},{10,11... | collective-permute-start | bytes 196616 | tf_op jit(solution)/shard_map/ppermute | solution.py:54

commit v6 on v5

--- a/solution.py
+++ b/solution.py
@@ -9,6 +9,10 @@
 from jax.sharding import PartitionSpec as P
 
 
+ORDERS = {
+    "send": [(2, 3, 0, 1), (1, 2, 3, 0), (3, 0, 1, 2)],
+    "back": [(1, 3, 0, 2), (3, 2, 1, 0), (2, 0, 3, 1)],
+}
 SUBLANES = 8
 LANES = 128
 F32 = jnp.float32
@@ -71,14 +75,15 @@
         return copy
 
     early = [
+        start(routed, routed_here),
         start(lengths, lengths_here),
         start(q, q_here),
         start(fresh, fresh_here),
     ]
     key_copies = [start(k.at[b], k_here.at[b]) for b in batches]
     value_copies = [start(v.at[b], v_here.at[b]) for b in batches]
-    late = [start(routed, routed_here), start(residual, residual_here)]
-    weight_copy = start(weight, loaded)
+    residual_copy = start(residual, residual_here)
+    weight_copy = start(weight.at[pl.ds(0, loaded.shape[0])], loaded)
 
     group = width // (heads * size)
     scale = 1.0 / math.sqrt(size)
@@ -93,7 +98,25 @@
     def as_column(line):
         return jnp.sum(jnp.where(diagonal, line.astype(F32), 0.0), -1, keepdims=True)
 
-    for copy in early:
+    deep = lax.axis_index("deep")
+    half = kept.shape[1]
+    early[0].wait()
+    picks = routed.shape[0]
+    lane = iota((rows, LANES), 1).astype(F32)
+    chosen = [as_column(routed_here[j : j + 1, :]) for j in range(picks)]
+    hits = jnp.zeros((rows, LANES), F32)
+    for expert in chosen:
+        hits = hits + (expert == lane).astype(F32)
+    earlier = (iota((rows, rows), 1) < iota((rows, rows), 0)).astype(BF16)
+    before = dot(earlier, hits.astype(BF16))
+    notes = jnp.zeros((rows, LANES), F32)
+    for j, expert in enumerate(chosen):
+        slot = jnp.sum(jnp.where(expert == lane, before, 0.0), -1, keepdims=True)
+        slot = slot + (deep * capacity).astype(F32)
+        notes = jnp.where(lane == j, expert, notes)
+        notes = jnp.where(lane == picks + j, slot, notes)
+    ext[:, width + half :] = notes.astype(BF16)
+    for copy in early[1:]:
         copy.wait()
     limits = as_column(lengths_here[...]).astype(jnp.int32)
     q_all = q_here[...].astype(F32)
@@ -133,94 +156,21 @@
             ext[batches[b], at + g * size : at + (g + 1) * size] = out[
                 g * SUBLANES : (g + 1) * SUBLANES
             ].astype(BF16)
-    for copy in late:
-        copy.wait()
-    deep = lax.axis_index("deep")
-    half = kept.shape[1]
+    residual_copy.wait()
     kept[...] = residual_here[:, pl.ds(pl.multiple_of(deep * half, LANES), half)]
     ext[:, width : width + half] = residual_here[
         :, pl.ds(pl.multiple_of((1 - deep) * half, LANES), half)
     ]
-    picks = routed.shape[0]
-    lane = iota((rows, LANES), 1).astype(F32)
-    chosen = [as_column(routed_here[j : j + 1, :]) for j in range(picks)]
-    hits = jnp.zeros((rows, LANES), F32)
-    for expert in chosen:
-        hits = hits + (expert == lane).astype(F32)
-    earlier = (iota((rows, rows), 1) < iota((rows, rows), 0)).astype(BF16)
-    before = dot(earlier, hits.astype(BF16))
-    notes = jnp.zeros((rows, LANES), F32)
-    for j, expert in enumerate(chosen):
-        slot = jnp.sum(jnp.where(expert == lane, before, 0.0), -1, keepdims=True)
-        slot = slot + (deep * capacity).astype(F32)
-        notes = jnp.where(lane == j, expert, notes)
-        notes = jnp.where(lane == picks + j, slot, notes)
-    ext[:, width + half :] = notes.astype(BF16)
     weight_copy.wait()
 
 
-def project_body(own, other, weight, total, short):
-    depth = weight.shape[0]
+def project_body(picks, chips, own, other, first, second, total, short, selector):
+    edge = first.shape[0]
+    depth = edge + second.shape[0]
     both = jnp.concatenate([own[:, :depth], other[:, :depth]], 0)
-    out = dot(both, weight[...])
+    out = dot(both[:, :edge], first[...]) + dot(both[:, edge:], second[...])
     total[...] = out
     short[...] = out.astype(BF16)
-
-
-def routes_of(chips):
-    if chips == 2:
-        return [{0: 1, 1: 0}]
-    if chips == 4:
-        return [
-            {0: 3, 1: 2, 2: 1, 3: 0},
-            {0: 2, 1: 3, 2: 0, 3: 1},
-            {0: 1, 1: 0, 2: 3, 3: 2},
-        ]
-    return []
-
-
-def block_count(chips):
-    routes = routes_of(chips)
-    return len(routes) + 1 if routes else 1
-
-
-def store_blocks(refs, chips, tiles, value):
-    size = tiles * SUBLANES
-    routes = routes_of(chips)
-    if not routes:
-        refs[0][...] = value
-        return
-    wide = lax.axis_index("wide")
-    for here in range(chips):
-
-        @pl.when(wide == here)
-        def _(here=here):
-            for ref, route in zip(refs, [*routes, {here: here}]):
-                if here in route:
-                    to = route[here]
-                    ref[...] = value[to * size : (to + 1) * size]
-
-
-def each_source(refs, chips, use):
-    routes = routes_of(chips)
-    if not routes:
-        size = refs[0].shape[0] // chips
-        use([refs[0].at[pl.ds(i * size, size)] for i in range(chips)])
-        return
-    wide = lax.axis_index("wide")
-    for here in range(chips):
-
-        @pl.when(wide == here)
-        def _(here=here):
-            found = {}
-            for ref, route in zip(refs, [*routes, {here: here}]):
-                for source, to in route.items():
-                    if to == here:
-                        found[source] = ref
-            use([found[i] for i in range(chips)])
-
-
-def select_body(picks, chips, own, other, selector):
     rows = own.shape[0]
     at = own.shape[1] - LANES
     notes = jnp.concatenate([own[:, at:], other[:, at:]], 0).astype(F32).astype(jnp.int32)
@@ -241,8 +191,79 @@
     selector[...] = jnp.transpose(picked).astype(BF16)
 
 
-def pack_body(chips, selector, other, kept, total, *rest):
-    count = block_count(chips) + 2
+def routes_of(chips, name):
+    orders = ORDERS[name] if chips == 4 else [(1, 0)] if chips == 2 else []
+    return [dict(enumerate(order)) for order in orders]
+
+
+def block_count(chips, name):
+    routes = routes_of(chips, name)
+    return len(routes) + 1 if routes else 1
+
+
+def store_blocks(refs, chips, name, tiles, value, first=0):
+    size = tiles * SUBLANES
+    routes = routes_of(chips, name)
+    if not routes:
+        refs[0][...] = value
+        return
+    wide = lax.axis_index("wide")
+    for here in range(chips):
+
+        @pl.when(wide == here)
+        def _(here=here):
+            for ref, route in zip(refs, [*routes[first:], {here: here}]):
+                if here in route:
+                    to = route[here]
+                    ref[...] = value[to * size : (to + 1) * size]
+
+
+def each_source(refs, chips, name, use, parts=1):
+    routes = routes_of(chips, name)
+    if parts > 1:
+        refs = [list(refs[:parts]), *refs[parts:]]
+    if not routes:
+        size = refs[0].shape[0] // chips
+        use([refs[0].at[pl.ds(i * size, size)] for i in range(chips)])
+        return
+    wide = lax.axis_index("wide")
+    for here in range(chips):
+
+        @pl.when(wide == here)
+        def _(here=here):
+            found = {}
+            for ref, route in zip(refs, [*routes, {here: here}]):
+                for source, to in route.items():
+                    if to == here:
+                        found[source] = ref
+            use([found[i] for i in range(chips)])
+
+
+def far_body(chips, selector, other, kept, total, out):
+    _, half = kept.shape
+    width = other.shape[1] - half - LANES
+    added = jnp.concatenate([kept[...], other[:, width : width + half]], 0).astype(F32)
+    mixed = total[...] + jnp.where(lax.axis_index("narrow") == 0, added, 0.0)
+    mixed = mixed.astype(BF16)
+    size = 3 * SUBLANES
+    for here, to in routes_of(chips, "send")[0].items():
+
+        @pl.when(lax.axis_index("wide") == here)
+        def _(to=to):
+            out[...] = dot(selector[to * size : (to + 1) * size], mixed).astype(BF16)
+
+
+def summed(blocks):
+    if not isinstance(blocks, list):
+        return blocks
+    total = blocks[0][...].astype(F32)
+    for block in blocks[1:]:
+        total = total + block[...].astype(F32)
+    return total.astype(BF16)
+
+
+def pack_body(chips, first, selector, other, kept, total, *rest):
+    count = block_count(chips, "send") - first + 2
     parts, (*packed, mine, lent) = rest[:-count], rest[-count:]
     rows, half = kept.shape
     mixed = total[...]
@@ -254,33 +275,47 @@
     mine[...] = mixed_own
     lent[...] = mixed_other
     mixed = jnp.concatenate([mixed_own, mixed_other], 0).astype(BF16)
-    store_blocks(packed, chips, 3, dot(selector[...], mixed).astype(BF16))
-
-
-def tail_body(chips, *refs):
+    store_blocks(packed, chips, "send", 3, dot(selector[...], mixed).astype(BF16), first)
+
+
+def tail_body(chips, name, parts, *refs):
     *blocks, out = refs
     size = out.shape[0] // chips
 
     def use(found):
         for i, block in enumerate(found):
-            out[i * size : (i + 1) * size] = block[SUBLANES:]
-
-    each_source(blocks, chips, use)
-
-
-def load_body(source, target, sem):
-    copy = pltpu.make_async_copy(source, target, sem)
+            out[i * size : (i + 1) * size] = summed(block)[SUBLANES:]
+
+    each_source(blocks, chips, name, use, parts)
+
+
+def load_body(start, source, target, sem):
+    copy = pltpu.make_async_copy(source.at[pl.ds(start, target.shape[0])], target, sem)
     copy.start()
     copy.wait()
 
 
-def kept_body(chips, *refs):
+def load(array, start):
+    shape = (array.shape[0] - start, *array.shape[1:])
+    return pl.pallas_call(
+        functools.partial(load_body, start),
+        out_shape=jax.ShapeDtypeStruct(shape, array.dtype),
+        in_specs=[HBM],
+        out_specs=VMEM,
+        scratch_shapes=[pltpu.SemaphoreType.DMA],
+        compiler_params=pltpu.CompilerParams(vmem_limit_bytes=8 << 20),
+        cost_estimate=pl.CostEstimate(flops=0, bytes_accessed=4 << 20, transcendentals=0),
+    )(pltpu.with_memory_space_constraint(array, pltpu.HBM))
+
+
+def kept_body(chips, parts, *refs):
     *blocks, gain, weight, products, squares, rows_ref = refs
     half = rows_ref.shape[1]
     edge = SUBLANES // 2
     first = iota((SUBLANES, half), 0) < edge
 
     def use(found):
+        found = [summed(block) for block in found]
         for i, block in enumerate(found):
             rows_ref[i * SUBLANES : (i + 1) * SUBLANES] = block[:SUBLANES].astype(F32)
         for i in range(0, chips, 2):
@@ -288,7 +323,7 @@
             tails = [block[2 * SUBLANES :].astype(F32) for block in found[i : i + 2]]
             rows_ref[to : to + SUBLANES] = jnp.where(first, tails[0], pltpu.roll(tails[1], edge, 0))
 
-    each_source(blocks, chips, use)
+    each_source(blocks, chips, "send", use, parts)
     at = pl.multiple_of(lax.axis_index("deep") * half, LANES)
     rows = rows_ref[...]
     squares[...] = jnp.sum(rows * rows, -1, keepdims=True)
@@ -345,7 +380,7 @@
     total = begun[...]
     for i, piece in enumerate(pieces):
         total = total + ordered(capacity, chips, piece, i + 1, parts, weight)
-    store_blocks(outs, chips, 2, total.astype(BF16))
+    store_blocks(outs, chips, "back", 2, total.astype(BF16))
 
 
 def begin_combine_body(capacity, per_half, chips, *refs):
@@ -358,7 +393,7 @@
         for i, block in enumerate(found):
             value[i * SUBLANES : (i + 1) * SUBLANES] = block[:SUBLANES].astype(F32)
 
-    each_source(blocks, chips, use)
+    each_source(blocks, chips, "back", use)
     notes = own[:, own.shape[1] - LANES :].astype(F32).astype(jnp.int32)
     diagonal = iota((rows, rows), 0) == iota((rows, rows), 1)
     lines = router[...]
@@ -387,8 +422,15 @@
     out[...] = value.astype(BF16)
 
 
-def exchange(blocks, chips):
-    routes = routes_of(chips)
+def exchange_by(routes, blocks):
+    out = []
+    for block, route in zip(blocks, routes):
+        out.append(lax.ppermute(block, "wide", list(route.items())))
+    return out
+
+
+def exchange(blocks, chips, name):
+    routes = routes_of(chips, name)
     if not routes:
         (whole,) = blocks
         out = lax.all_to_all(
@@ -396,10 +438,7 @@
         )
         return [out.reshape(whole.shape)]
     *leaving, stays = blocks
-    out = []
-    for block, route in zip(leaving, routes):
-        out.append(lax.ppermute(block, "wide", list(route.items())))
-    return [*out, stays]
+    return [*exchange_by(routes, leaving), stays]
 
 
 def shards(
@@ -431,8 +470,8 @@
     sds = jax.ShapeDtypeStruct
 
     def blocks_shape(tiles, width):
-        if routes_of(wide_count):
-            return [sds((tiles * SUBLANES, width), BF16)] * block_count(wide_count)
+        if routes_of(wide_count, "send"):
+            return [sds((tiles * SUBLANES, width), BF16)] * block_count(wide_count, "send")
         return [sds((wide_count * tiles * SUBLANES, width), BF16)]
 
     sources = [
@@ -449,7 +488,7 @@
         out_shape=[
             sds((rows, head_width + half + LANES), BF16),
             sds((rows, half), BF16),
-            sds(output_weight.shape, BF16),
+            sds((head_width // 4 * 3, half), BF16),
         ],
         in_specs=[HBM] * (len(sources) + 1),
         out_specs=[VMEM] * 3,
@@ -459,36 +498,44 @@
         cost_estimate=pl.CostEstimate(flops=0, bytes_accessed=6 << 20, transcendentals=0),
     )(*[pltpu.with_memory_space_constraint(x, pltpu.HBM) for x in [*sources, output_weight]])
     other = swap(ext, "deep")
-    total, short = call(
-        project_body,
-        [sds((2 * rows, half), F32), sds((2 * rows, half), BF16)],
-        [ext, other, loaded],
+    rest = load(output_weight, head_width // 4 * 3)
+    total, short, selector = call(
+        functools.partial(project_body, picks, wide_count),
+        [
+            sds((2 * rows, half), F32),
+            sds((2 * rows, half), BF16),
+            sds((wide_count * 3 * SUBLANES, 2 * rows), BF16),
+        ],
+        [ext, other, loaded, rest],
         flops=4 * rows * head_width * half,
     )
     parts = from_others(short, "narrow")
-    (selector,) = call(
-        functools.partial(select_body, picks, wide_count),
-        [sds((wide_count * 3 * SUBLANES, 2 * rows), BF16)],
-        [ext, other],
-    )
-    gate_up = pl.pallas_call(
-        load_body,
-        out_shape=sds(expert_gate_up.shape[1:], BF16),
-        in_specs=[HBM],
-        out_specs=VMEM,
-        scratch_shapes=[pltpu.SemaphoreType.DMA],
-        compiler_params=pltpu.CompilerParams(vmem_limit_bytes=8 << 20),
-        cost_estimate=pl.CostEstimate(flops=0, bytes_accessed=4 << 20, transcendentals=0),
-    )(pltpu.with_memory_space_constraint(expert_gate_up[0], pltpu.HBM))
+    routes = routes_of(wide_count, "send")
+    ahead = 1 if routes else 0
+    far = []
+    if ahead:
+        far = list(call(
+            functools.partial(far_body, wide_count),
+            [sds((3 * SUBLANES, half), BF16)],
+            [selector, other, kept, total],
+        ))
+        far = exchange_by(routes[:1], far)
     *packed, mine, lent = call(
-        functools.partial(pack_body, wide_count),
-        [*blocks_shape(3, half), sds((rows, half), F32), sds((rows, half), F32)],
+        functools.partial(pack_body, wide_count, ahead),
+        [*blocks_shape(3, half)[ahead:], sds((rows, half), F32), sds((rows, half), F32)],
         [selector, other, kept, total, *parts],
     )
     borrowed = swap(lent, "deep")
-    arrived = exchange(packed, wide_count)
+    if ahead:
+        arrived = [*exchange_by(routes[1:], packed[:-1]), packed[-1]]
+        far = [*far, *from_others(far[0], "narrow")]
+        arrived = [*far, *arrived]
+    else:
+        arrived = exchange(packed, wide_count, "send")
+    pieces_of_far = max(len(far), 1)
+    gate_up = load(expert_gate_up[0], 0)
     (passing,) = call(
-        functools.partial(tail_body, wide_count),
+        functools.partial(tail_body, wide_count, "send", pieces_of_far),
         [sds((wide_count * 2 * SUBLANES, half), BF16)],
         arrived,
     )
@@ -496,7 +543,7 @@
     hidden_width = gate_up.shape[1]
     gain = norm_gain[None, :]
     products, squares = call(
-        functools.partial(kept_body, wide_count),
+        functools.partial(kept_body, wide_count, pieces_of_far),
         [sds((2, row_slots, hidden_width), F32), sds((row_slots, 1), F32)],
         [*arrived, gain, gate_up],
         flops=2 * row_slots * hidden_width * full_width,
@@ -522,9 +569,9 @@
         [begun, *pieces, down],
         flops=2 * row_slots * share * hidden_width,
     )
-    returned = exchange(expert_rows, wide_count)
+    returned = exchange(expert_rows, wide_count, "back")
     (passing,) = call(
-        functools.partial(tail_body, wide_count),
+        functools.partial(tail_body, wide_count, "back", 1),
         [sds((wide_count * SUBLANES, share), BF16)],
         returned,
     )

time: 37 us -> 38.6 us (1.043)
  starting transfers between devices: 14.3 us -> 17.6 us
  waiting for transfers between devices: 13.2 us -> 10.7 us
  Pallas kernels: 9.14 us -> 9.91 us
    ppermute x6, starting transfers between devices: 9.01 us -> 12.2 us  [exchange_by(): out.append(lax.ppermute(block, 'wide', list(route.items())))]
    ppermute x2 -> x3, waiting for transfers between devices: 4.62 us -> 1.56 us  [from_others(): lax.ppermute(value, axis, [(i, (i + step) % size) for i in range(size)])]
    ppermute x6, waiting for transfers between devices: 6.66 us -> 8.24 us  [exchange_by(): out.append(lax.ppermute(block, 'wide', list(route.items())))]
    pallas_call x1 -> x2, Pallas kernels: 1.9 us -> 3.14 us  [load(): pl.pallas_call(functools.partial(load_body, start), out_shape=jax.ShapeDt...]
    ppermute x4, waiting for transfers between devices: 1.93 us -> 0.91 us  [swap(): return lax.ppermute(value, axis, [(0, 1), (1, 0)])]
    ppermute x2 -> x3, starting transfers between devices: 4.46 us -> 4.56 us  [from_others(): lax.ppermute(value, axis, [(i, (i + step) % size) for i in range(size)])]
  transfers between devices with their start and end apart: 12 -> 13, of which waited for: 9 -> 6; matrix products, arithmetic and copies ran while one was open for 0% -> 0% of each run, Pallas kernels for 11% -> 14%
where the time goes in v6:
time: 38.6 us; the launch traced here: 38.4 us
  starting transfers between devices  17.6 us (46%)
  waiting for transfers between devices  10.7 us (28%)
  Pallas kernels  9.91 us (26%)
    ppermute x6, starting transfers between devices, exchange_by(): out.append(lax.ppermute(block, 'wide', list(route.items())))  12.2 us
    ppermute x6, waiting for transfers between devices, exchange_by(): out.append(lax.ppermute(block, 'wide', list(route.items())))  8.24 us
    ppermute x3, starting transfers between devices, from_others(): lax.ppermute(value, axis, [(i, (i + step) % size) for i in range(size)])  4.56 us
    pallas_call x11, Pallas kernels, call(): pl.pallas_call(body, out_shape=outs, in_specs=[VMEM] * len(operands), out...  4.3 us
    pallas_call x2, Pallas kernels, load(): pl.pallas_call(functools.partial(load_body, start), out_shape=jax.ShapeDt...  3.14 us
    pallas_call x1, Pallas kernels, shards(): pl.pallas_call(functools.partial(attention_body, capacity), out_shape=[sd...  2.47 us
    ppermute x3, waiting for transfers between devices, from_others(): lax.ppermute(value, axis, [(i, (i + step) % size) for i in range(size)])  1.56 us
    ppermute x4, waiting for transfers between devices, swap(): return lax.ppermute(value, axis, [(0, 1), (1, 0)])  0.91 us
  transfers between devices with their start and end apart: 13, of which 6 were waited for; matrix products, arithmetic and copies ran while one was open for 0% of the time, Pallas kernels for 14%

profile of v6, /device:TPU:0, one launch (start us, length us, event | category | flops | bytes accessed | tf_op | source)
XLA Modules:
  0.0 38.4 jit_solution(11299362617181135056)
XLA Ops:
  0.0 2.5 %shard_map.118 = (bf16[24,3200]{1,0:T(8,128)(2,1)S(1)}, bf16[24,1024]{1,0:T(8,128)(2,1)S(1)}, bf16[1536,1024]{1,0:T(8,128)(2,1)S(1)}) custom-call(bf16[24,2048]{1,0:T(8,128)(2,1)} %q.1, bf16[24,2,32,128]{3,2,1,0:T(8,128)(2,1)} %k.1, bf16[24,2,32,128]{3,2,1,0:T(8,128)(2,1)} %v.1, bf16[24,2,256]{2,1,0:T(2,128)(2,1)} %fresh.1, s32[1,24]{1,0:T(1,128)} %bitcast.12, ...), custom_call_target="tpu_custom_call" | custom-call | bytes 6291456 | tf_op jit(solution)/shard_map/pallas_call | solution.py:486
  2.5 0.6 %collective-permute-start = (bf16[24,3200]{1,0:T(8,128)(2,1)S(1)}, bf16[24,3200]{1,0:T(8,128)(2,1)S(1)}, u32[]{:S(2)}, u32[]{:S(2)}) collective-permute-start(bf16[24,3200]{1,0:T(8,128)(2,1)S(1)} %get-tuple-element.25.own.refs_4_), channel_id=1, source_target_pairs={{0,1},{1,0},{2,3},{3,2},{4,5},{5,4},{6,7},{7,6},{8,9},{9,8},{10,11... | collective-permute-start | bytes 460808 | tf_op jit(solution)/shard_map/ppermute | solution.py:58
  3.0 1.2 %shard_map.119.second = bf16[512,1024]{1,0:T(8,128)(2,1)S(1)} custom-call(bf16[2048,1024]{1,0:T(8,128)(2,1)} %source.1), custom_call_target="tpu_custom_call" | custom-call | bytes 4194304 | tf_op jit(solution)/shard_map/pallas_call | solution.py:300
  4.3 0.8 %shard_map.120 = (f32[48,1024]{1,0:T(8,128)S(1)}, bf16[48,1024]{1,0:T(8,128)(2,1)S(1)}, bf16[96,48]{1,0:T(8,128)(2,1)S(1)}) custom-call(bf16[24,3200]{1,0:T(8,128)(2,1)S(1)} %get-tuple-element.25.own.refs_4_, bf16[24,3200]{1,0:T(8,128)(2,1)S(1)} %collective-permute-done.other, bf16[1536,1024]{1,0:T(8,128)(2,1)S(1)} %get-tuple-element.26.first, ...), custom_call_target="tpu_custom_call" | custom-call | flops 201326592 | bytes 4805632 | tf_op jit(solution)/shard_map/pallas_call | solution.py:38
  5.1 2.7 %collective-permute-start.3 = (bf16[48,1024]{1,0:T(8,128)(2,1)S(1)}, bf16[48,1024]{1,0:T(8,128)(2,1)S(1)}, u32[]{:S(2)}, u32[]{:S(2)}) collective-permute-start(bf16[48,1024]{1,0:T(8,128)(2,1)S(1)} %get-tuple-element.30), channel_id=1, source_target_pairs={{0,2},{2,0},{1,3},{3,1},{4,6},{6,4},{5,7},{7,5},{8,10},{10,8},{9,1... | collective-permute-start | bytes 294920 | tf_op jit(solution)/shard_map/ppermute | solution.py:52
  7.8 0.2 shard_map.121
  8.0 2.6 %collective-permute-start.1 = (bf16[24,1024]{1,0:T(8,128)(2,1)S(1)}, bf16[24,1024]{1,0:T(8,128)(2,1)S(1)}, u32[]{:S(2)}, u32[]{:S(2)}) collective-permute-start(bf16[24,1024]{1,0:T(8,128)(2,1)S(1)} %shard_map.121), channel_id=1, source_target_pairs={{0,8},{4,12},{8,0},{12,4},{1,9},{5,13},{9,1},{13,5},{2,10},{6,14},... | collective-permute-start | bytes 147464 | tf_op jit(solution)/shard_map/ppermute | solution.py:428
  10.6 3.5 %collective-permute-done.1.refs_0_ = bf16[24,1024]{1,0:T(8,128)(2,1)S(1)} collective-permute-done((bf16[24,1024]{1,0:T(8,128)(2,1)S(1)}, bf16[24,1024]{1,0:T(8,128)(2,1)S(1)}, u32[]{:S(2)}, u32[]{:S(2)}) %collective-permute-start.1) | collective-permute-done | bytes 49184 | tf_op jit(solution)/shard_map/ppermute | solution.py:428
  14.1 0.2 shard_map.122
  14.3 1.1 %collective-permute-start.4 = (bf16[24,1024]{1,0:T(8,128)(2,1)S(1)}, bf16[24,1024]{1,0:T(8,128)(2,1)S(1)}, u32[]{:S(2)}, u32[]{:S(2)}) collective-permute-start(bf16[24,1024]{1,0:T(8,128)(2,1)S(1)} %get-tuple-element.31), channel_id=1, source_target_pairs={{0,4},{4,8},{8,12},{12,0},{1,5},{5,9},{9,13},{13,1},{2,6},{6,10},{... | collective-permute-start | bytes 147464 | tf_op jit(solution)/shard_map/ppermute | solution.py:428
  15.4 2.8 %collective-permute-start.5 = (bf16[24,1024]{1,0:T(8,128)(2,1)S(1)}, bf16[24,1024]{1,0:T(8,128)(2,1)S(1)}, u32[]{:S(2)}, u32[]{:S(2)}) collective-permute-start(bf16[24,1024]{1,0:T(8,128)(2,1)S(1)} %get-tuple-element.32), channel_id=1, source_target_pairs={{0,12},{4,0},{8,4},{12,8},{1,13},{5,1},{9,5},{13,9},{2,14},{6,2},{... | collective-permute-start | bytes 147464 | tf_op jit(solution)/shard_map/ppermute | solution.py:428
  18.2 2.5 %collective-permute-done.4.refs_2_ = bf16[24,1024]{1,0:T(8,128)(2,1)S(1)} collective-permute-done((bf16[24,1024]{1,0:T(8,128)(2,1)S(1)}, bf16[24,1024]{1,0:T(8,128)(2,1)S(1)}, u32[]{:S(2)}, u32[]{:S(2)}) %collective-permute-start.4) | collective-permute-done | bytes 49184 | tf_op jit(solution)/shard_map/ppermute | solution.py:428
  20.7 0.1 collective-permute-start.6
  20.8 0.0 copy-start.1
  20.8 1.9 %shard_map.124.refs_6_.weight = bf16[2,384,2048]{2,1,0:T(8,128)(2,1)S(1)} custom-call(bf16[2,384,2048]{2,1,0:T(8,128)(2,1)} %bitcast.11), custom_call_target="tpu_custom_call" | custom-call | bytes 4194304 | tf_op jit(solution)/shard_map/pallas_call | solution.py:300
  22.7 0.0 copy-start
  22.7 0.6 %shard_map.125 = (f32[2,48,384]{2,1,0:T(8,128)S(1)}, f32[48,1]{1,0:T(8,128)S(1)}) custom-call(bf16[24,1024]{1,0:T(8,128)(2,1)S(1)} %collective-permute-done.1.refs_0_, bf16[24,1024]{1,0:T(8,128)(2,1)S(1)} %collective-permute-done.2.refs_1_, bf16[24,1024]{1,0:T(8,128)(2,1)S(1)} %collective-permute-done.4.refs_2_, ...), custom_call_target="tpu_custom_call" | custom-call | flops 75497472 | bytes 3547328 | tf_op jit(solution)/shard_map/pallas_call | solution.py:38
  23.4 0.0 copy-start.2
  23.4 0.6 %shard_map.126.piece = bf16[48,384]{1,0:T(8,128)(2,1)S(1)} custom-call(bf16[64,1024]{1,0:T(8,128)(2,1)S(1)} %collective-permute-done.6.crossed, f32[1,2048]{1,0:T(1,128)S(1)} %bitcast.9, bf16[2,384,2048]{2,1,0:T(8,128)(2,1)S(1)} %shard_map.124.refs_6_.weight, f32[2,48,384]{2,1,0:T(8,128)S(1)} %get-tuple-element.34.products, ...), custom_call_target="tpu_custom_call" | custom-call | flops 75497472 | bytes 3469504 | tf_op jit(solution)/shard_map/pallas_call | solution.py:38
  24.0 1.9 %collective-permute-start.7 = (bf16[48,384]{1,0:T(8,128)(2,1)S(1)}, bf16[48,384]{1,0:T(8,128)(2,1)S(1)}, u32[]{:S(2)}, u32[]{:S(2)}) collective-permute-start(bf16[48,384]{1,0:T(8,128)(2,1)S(1)} %shard_map.126.piece), channel_id=1, source_target_pairs={{0,2},{2,0},{1,3},{3,1},{4,6},{6,4},{5,7},{7,5},{8,10},{10,8},{9,1... | collective-permute-start | bytes 110600 | tf_op jit(solution)/shard_map/ppermute | solution.py:52
  25.9 0.2 collective-permute-start.11
  26.1 0.4 shard_map.127.begun
  26.5 1.6 %collective-permute-done.7.rest_0_ = bf16[48,384]{1,0:T(8,128)(2,1)S(1)} collective-permute-done((bf16[48,384]{1,0:T(8,128)(2,1)S(1)}, bf16[48,384]{1,0:T(8,128)(2,1)S(1)}, u32[]{:S(2)}, u32[]{:S(2)}) %collective-permute-start.7) | collective-permute-done | bytes 36896 | tf_op jit(solution)/shard_map/ppermute | solution.py:52
  28.0 0.4 shard_map.128
  28.4 2.1 %collective-permute-start.10 = (bf16[16,1024]{1,0:T(8,128)(2,1)S(1)}, bf16[16,1024]{1,0:T(8,128)(2,1)S(1)}, u32[]{:S(2)}, u32[]{:S(2)}) collective-permute-start(bf16[16,1024]{1,0:T(8,128)(2,1)S(1)} %get-tuple-element.38), channel_id=1, source_target_pairs={{0,8},{4,0},{8,12},{12,4},{1,9},{5,1},{9,13},{13,5},{2,10},{6,2},{... | collective-permute-start | bytes 98312 | tf_op jit(solution)/shard_map/ppermute | solution.py:428
  30.5 0.0 collective-permute-start.8
  30.5 3.6 %collective-permute-start.9 = (bf16[16,1024]{1,0:T(8,128)(2,1)S(1)}, bf16[16,1024]{1,0:T(8,128)(2,1)S(1)}, u32[]{:S(2)}, u32[]{:S(2)}) collective-permute-start(bf16[16,1024]{1,0:T(8,128)(2,1)S(1)} %get-tuple-element.37), channel_id=1, source_target_pairs={{0,12},{4,8},{8,4},{12,0},{1,13},{5,9},{9,5},{13,1},{2,14},{6,10},... | collective-permute-start | bytes 98312 | tf_op jit(solution)/shard_map/ppermute | solution.py:428
  34.1 1.3 %collective-permute-done.8.refs_0_ = bf16[16,1024]{1,0:T(8,128)(2,1)S(1)} collective-permute-done((bf16[16,1024]{1,0:T(8,128)(2,1)S(1)}, bf16[16,1024]{1,0:T(8,128)(2,1)S(1)}, u32[]{:S(2)}, u32[]{:S(2)}) %collective-permute-start.8) | collective-permute-done | bytes 32800 | tf_op jit(solution)/shard_map/ppermute | solution.py:428
  35.4 1.0 %collective-permute-done.9.refs_1_ = bf16[16,1024]{1,0:T(8,128)(2,1)S(1)} collective-permute-done((bf16[16,1024]{1,0:T(8,128)(2,1)S(1)}, bf16[16,1024]{1,0:T(8,128)(2,1)S(1)}, u32[]{:S(2)}, u32[]{:S(2)}) %collective-permute-start.9) | collective-permute-done | bytes 32800 | tf_op jit(solution)/shard_map/ppermute | solution.py:428
  36.4 0.3 shard_map.129
  36.7 0.9 %collective-permute-done.12.crossed = bf16[32,1024]{1,0:T(8,128)(2,1)S(1)} collective-permute-done((bf16[32,1024]{1,0:T(8,128)(2,1)S(1)}, bf16[32,1024]{1,0:T(8,128)(2,1)S(1)}, u32[]{:S(2)}, u32[]{:S(2)}) %collective-permute-start.12) | collective-permute-done | bytes 65568 | tf_op jit(solution)/shard_map/ppermute | solution.py:58
  37.6 0.8 %shard_map.131 = bf16[24,1024]{1,0:T(8,128)(2,1)} custom-call(f32[24,1024]{1,0:T(8,128)S(1)} %get-tuple-element.42.total, bf16[1,24,32]{2,1,0:T(8,128)(2,1)S(1)} %get-tuple-element.43.selector, f32[1,24,1]{2,1,0:T(8,128)S(1)} %get-tuple-element.44.scales, bf16[32,1024]{1,0:T(8,128)(2,1)S(1)} %collective-permute-done.12.crossed), custom_call_target="tpu_custom_call" | custom-call | bytes 214624 | tf_op jit(solution)/shard_map/pallas_call | solution.py:38
  (14 shorter events, 0.1 us)
Async XLA Ops:
  2.5 1.8 %collective-permute-start = (bf16[24,3200]{1,0:T(8,128)(2,1)S(1)}, bf16[24,3200]{1,0:T(8,128)(2,1)S(1)}, u32[]{:S(2)}, u32[]{:S(2)}) collective-permute-start(bf16[24,3200]{1,0:T(8,128)(2,1)S(1)} %get-tuple-element.25.own.refs_4_), channel_id=1, source_target_pairs={{0,1},{1,0},{2,3},{3,2},{4,5},{5,4},{6,7},{7,6},{8,9},{9,8},{10,11... | collective-permute-start | bytes 460808 | tf_op jit(solution)/shard_map/ppermute | solution.py:58
  5.1 9.0 %collective-permute-start.3 = (bf16[48,1024]{1,0:T(8,128)(2,1)S(1)}, bf16[48,1024]{1,0:T(8,128)(2,1)S(1)}, u32[]{:S(2)}, u32[]{:S(2)}) collective-permute-start(bf16[48,1024]{1,0:T(8,128)(2,1)S(1)} %get-tuple-element.30), channel_id=1, source_target_pairs={{0,2},{2,0},{1,3},{3,1},{4,6},{6,4},{5,7},{7,5},{8,10},{10,8},{9,1... | collective-permute-start | bytes 294920 | tf_op jit(solution)/shard_map/ppermute | solution.py:52
  8.0 6.1 %collective-permute-start.1 = (bf16[24,1024]{1,0:T(8,128)(2,1)S(1)}, bf16[24,1024]{1,0:T(8,128)(2,1)S(1)}, u32[]{:S(2)}, u32[]{:S(2)}) collective-permute-start(bf16[24,1024]{1,0:T(8,128)(2,1)S(1)} %shard_map.121), channel_id=1, source_target_pairs={{0,8},{4,12},{8,0},{12,4},{1,9},{5,13},{9,1},{13,5},{2,10},{6,14},... | collective-permute-start | bytes 147464 | tf_op jit(solution)/shard_map/ppermute | solution.py:428
  14.1 4.1 %collective-permute-start.2 = (bf16[24,1024]{1,0:T(8,128)(2,1)S(1)}, bf16[24,1024]{1,0:T(8,128)(2,1)S(1)}, u32[]{:S(2)}, u32[]{:S(2)}) collective-permute-start(bf16[24,1024]{1,0:T(8,128)(2,1)S(1)} %collective-permute-done.1.refs_0_), channel_id=1, source_target_pairs={{0,2},{2,0},{1,3},{3,1},{4,6},{6,4},{5,7},{7,5},{8,10},{10,8},{9,1... | collective-permute-start | bytes 147464 | tf_op jit(solution)/shard_map/ppermute | solution.py:52
  14.3 6.4 %collective-permute-start.4 = (bf16[24,1024]{1,0:T(8,128)(2,1)S(1)}, bf16[24,1024]{1,0:T(8,128)(2,1)S(1)}, u32[]{:S(2)}, u32[]{:S(2)}) collective-permute-start(bf16[24,1024]{1,0:T(8,128)(2,1)S(1)} %get-tuple-element.31), channel_id=1, source_target_pairs={{0,4},{4,8},{8,12},{12,0},{1,5},{5,9},{9,13},{13,1},{2,6},{6,10},{... | collective-permute-start | bytes 147464 | tf_op jit(solution)/shard_map/ppermute | solution.py:428
  15.4 5.3 %collective-permute-start.5 = (bf16[24,1024]{1,0:T(8,128)(2,1)S(1)}, bf16[24,1024]{1,0:T(8,128)(2,1)S(1)}, u32[]{:S(2)}, u32[]{:S(2)}) collective-permute-start(bf16[24,1024]{1,0:T(8,128)(2,1)S(1)} %get-tuple-element.32), channel_id=1, source_target_pairs={{0,12},{4,0},{8,4},{12,8},{1,13},{5,1},{9,5},{13,9},{2,14},{6,2},{... | collective-permute-start | bytes 147464 | tf_op jit(solution)/shard_map/ppermute | solution.py:428
  20.7 2.7 %collective-permute-start.6 = (bf16[64,1024]{1,0:T(8,128)(2,1)S(1)}, bf16[64,1024]{1,0:T(8,128)(2,1)S(1)}, u32[]{:S(2)}, u32[]{:S(2)}) collective-permute-start(bf16[64,1024]{1,0:T(8,128)(2,1)S(1)} %shard_map.123), channel_id=1, source_target_pairs={{0,1},{1,0},{2,3},{3,2},{4,5},{5,4},{6,7},{7,6},{8,9},{9,8},{10,11... | collective-permute-start | bytes 393224 | tf_op jit(solution)/shard_map/ppermute | solution.py:58
  20.8 1.9 %copy-start.1 = (f32[2048]{0:T(1024)S(1)}, f32[2048]{0:T(1024)}, u32[]{:S(2)}) copy-start(f32[2048]{0:T(1024)} %param.18) | copy-start | bytes 24580
  22.7 3.4 %copy-start = (bf16[1,768,1024]{2,1,0:T(8,128)(2,1)S(1)}, bf16[1,768,1024]{2,1,0:T(8,128)(2,1)}, u32[]{:S(2)}) copy-start(bf16[1,768,1024]{2,1,0:T(8,128)(2,1)} %param.21) | copy-start | bytes 4718596
  23.4 13.0 %copy-start.2 = (f32[24,1]{0,1:T(1,128)S(1)}, f32[24,1]{0,1:T(1,128)}, u32[]{:S(2)}) copy-start(f32[24,1]{0,1:T(1,128)} %param.23) | copy-start | bytes 292
  24.0 4.0 %collective-permute-start.7 = (bf16[48,384]{1,0:T(8,128)(2,1)S(1)}, bf16[48,384]{1,0:T(8,128)(2,1)S(1)}, u32[]{:S(2)}, u32[]{:S(2)}) collective-permute-start(bf16[48,384]{1,0:T(8,128)(2,1)S(1)} %shard_map.126.piece), channel_id=1, source_target_pairs={{0,2},{2,0},{1,3},{3,1},{4,6},{6,4},{5,7},{7,5},{8,10},{10,8},{9,1... | collective-permute-start | bytes 110600 | tf_op jit(solution)/shard_map/ppermute | solution.py:52
  25.9 10.5 %collective-permute-start.11 = (f32[24,1024]{1,0:T(8,128)S(1)}, f32[24,1024]{1,0:T(8,128)S(1)}, u32[]{:S(2)}, u32[]{:S(2)}) collective-permute-start(f32[24,1024]{1,0:T(8,128)S(1)} %get-tuple-element.41), channel_id=1, source_target_pairs={{0,1},{1,0},{2,3},{3,2},{4,5},{5,4},{6,7},{7,6},{8,9},{9,8},{10,11... | collective-permute-start | bytes 294920 | tf_op jit(solution)/shard_map/ppermute | solution.py:58
  28.4 5.7 %collective-permute-start.10 = (bf16[16,1024]{1,0:T(8,128)(2,1)S(1)}, bf16[16,1024]{1,0:T(8,128)(2,1)S(1)}, u32[]{:S(2)}, u32[]{:S(2)}) collective-permute-start(bf16[16,1024]{1,0:T(8,128)(2,1)S(1)} %get-tuple-element.38), channel_id=1, source_target_pairs={{0,8},{4,0},{8,12},{12,4},{1,9},{5,1},{9,13},{13,5},{2,10},{6,2},{... | collective-permute-start | bytes 98312 | tf_op jit(solution)/shard_map/ppermute | solution.py:428
  30.5 4.9 %collective-permute-start.8 = (bf16[16,1024]{1,0:T(8,128)(2,1)S(1)}, bf16[16,1024]{1,0:T(8,128)(2,1)S(1)}, u32[]{:S(2)}, u32[]{:S(2)}) collective-permute-start(bf16[16,1024]{1,0:T(8,128)(2,1)S(1)} %get-tuple-element.36), channel_id=1, source_target_pairs={{0,4},{4,12},{8,0},{12,8},{1,5},{5,13},{9,1},{13,9},{2,6},{6,14},{... | collective-permute-start | bytes 98312 | tf_op jit(solution)/shard_map/ppermute | solution.py:428
  30.5 5.9 %collective-permute-start.9 = (bf16[16,1024]{1,0:T(8,128)(2,1)S(1)}, bf16[16,1024]{1,0:T(8,128)(2,1)S(1)}, u32[]{:S(2)}, u32[]{:S(2)}) collective-permute-start(bf16[16,1024]{1,0:T(8,128)(2,1)S(1)} %get-tuple-element.37), channel_id=1, source_target_pairs={{0,12},{4,8},{8,4},{12,0},{1,13},{5,9},{9,5},{13,1},{2,14},{6,10},... | collective-permute-start | bytes 98312 | tf_op jit(solution)/shard_map/ppermute | solution.py:428
  36.4 1.3 %collective-permute-start.12 = (bf16[32,1024]{1,0:T(8,128)(2,1)S(1)}, bf16[32,1024]{1,0:T(8,128)(2,1)S(1)}, u32[]{:S(2)}, u32[]{:S(2)}) collective-permute-start(bf16[32,1024]{1,0:T(8,128)(2,1)S(1)} %shard_map.130), channel_id=1, source_target_pairs={{0,1},{1,0},{2,3},{3,2},{4,5},{5,4},{6,7},{7,6},{8,9},{9,8},{10,11... | collective-permute-start | bytes 196616 | tf_op jit(solution)/shard_map/ppermute | solution.py:58
